TPU v7x, 128 devices: a whole 4x4x4 slice. The times are simulated.
128 devices in a mesh: tm: 32 (over z, x, core), cam: 4 (over y).
Axes of the slice: x: 4, y: 4, z: 4, core: 2. Of those that a mesh axis runs over, the one named last changes fastest.
Arguments:
- tokens: bfloat16 [4, 32, 512, 1536], P('cam', 'tm'), may hold values from -6 to 6
- w_query: bfloat16 [1536, 768], replicated, may hold values from -18 to 18
- w_key: bfloat16 [1536, 768], replicated, may hold values from -1 to 1
- w_value: bfloat16 [1536, 768], replicated, may hold values from -0.15625 to 0.15625
- w_out: bfloat16 [768, 1536], replicated, may hold values from -1.75 to 1.75
- grad_update: bfloat16 [4, 32, 512, 1536], P('cam', 'tm'), may hold values from -6 to 6
- memory_offsets: int32 [32, 4], replicated, may hold values from 1 to 31, as said below
- strip_count: int32 [4, 4], replicated, may hold values from 0 to 2, as said below
- strip_index: int32 [4, 4, 2], replicated, may hold values from 0 to 3, as said below
Outputs:
- update: bfloat16 [4, 32, 512, 1536], P('cam', 'tm')
- grad_tokens: bfloat16 [4, 32, 512, 1536], P('cam', 'tm')
Inputs may be any that keep to these rules, and one draw needn't show every extreme that they name: `memory_offsets`: every entry of row f is at most max(f, 1). strip_count[c, c] is 0. For every camera c the sum over s of strip_count[s, c] is at most 4; it is exactly 4 for some camera, and some entry is 2. The 2 entries of strip_index[s, c] are different.
All inputs are finite; a program needn't handle non-finite values.
Results may differ from a plain program's by a relative error of at most 0.0085.
The roundings to bfloat16 on the way count: a program that leaves them out, or rounds other values in their place, can miss the bound.
Values may be sent and summed in bfloat16 or wider, within the bound.
No kernel may reach another device: no remote copies, remote signals or barrier semaphores. Data moves between devices by JAX's collectives and lax.ppermute only.
A program may use at most 128 MiB of HBM per device.

v0:
```python
import jax
import jax.numpy as jnp
from jax import lax
from jax.experimental import pallas as pl
from jax.experimental.pallas import tpu as pltpu
from jax.sharding import PartitionSpec as P


LOW = jnp.bfloat16
WIDE = jnp.float32
ROWS = 512
MODEL = 1536
INNER = 768
STRIP = 128
MEM = 32
READS = 4
SLOTS = 6
LIVE_MAX = 4
MEM_AT = ROWS
FAR_AT = ROWS + READS * MEM
KEYS = FAR_AT + LIVE_MAX * STRIP
PAIR = 128
CHUNK = 384
EPS = 1e-05
MASKED = -1e30
NT = (((1,), (1,)), ((), ()))
GROUPS = ((0, 3), (3, 3))


def dot(left, right):
    return jnp.dot(left, right, preferred_element_type=WIDE)


def dot_t(left, right):
    return lax.dot_general(left, right, NT, preferred_element_type=WIDE)


def whole(shape):
    return pl.BlockSpec(shape, lambda *_: (0,) * len(shape))


def call(kernel, grid, scalars, in_specs, out_specs, out_shape, scratch, flops, moved, vmem=24):
    return pl.pallas_call(
        kernel,
        grid_spec=pltpu.PrefetchScalarGridSpec(
            num_scalar_prefetch=scalars,
            grid=(grid,),
            in_specs=in_specs,
            out_specs=out_specs,
            scratch_shapes=scratch,
        ),
        out_shape=out_shape,
        compiler_params=pltpu.CompilerParams(
            dimension_semantics=("arbitrary",), vmem_limit_bytes=vmem << 20
        ),
        cost_estimate=pl.CostEstimate(flops=flops, bytes_accessed=moved, transcendentals=0),
    )


IN_PLACE = pl.BlockSpec(memory_space=pl.ANY)


def array(shape, dtype):
    return jax.ShapeDtypeStruct(shape, dtype)


def normalize(rows):
    widened = rows.astype(WIDE)
    average = jnp.mean(widened, axis=-1, keepdims=True)
    centred = widened - average
    spread = jnp.mean(centred * centred, axis=-1, keepdims=True)
    inverse = lax.rsqrt(spread + EPS)
    return centred * inverse, inverse


def project_keys_kernel(ids, index, tokens, w_key, w_value, low, keys, values, *rest):
    sends, (rows, key_w, value_w, normed_low, made, in_sem, out_sem, send_sem) = rest[:3], rest[3:]
    camera = ids[0]
    loads = []
    for step, start in enumerate(range(0, ROWS, STRIP)):
        at = pl.ds(start, STRIP)
        loads.append(pltpu.make_async_copy(tokens.at[at], rows.at[at], in_sem.at[step]))
    loads.append(pltpu.make_async_copy(w_key, key_w, in_sem.at[4]))
    loads.append(pltpu.make_async_copy(w_value, value_w, in_sem.at[5]))
    for load in loads:
        load.start()
    for step, start in enumerate(range(0, ROWS, STRIP)):
        at = slice(start, start + STRIP)
        loads[step].wait()
        normed_low[at, :] = normalize(rows[at, :])[0].astype(LOW)
    stores = [pltpu.make_async_copy(normed_low, low, out_sem.at[0])]
    stores[0].start()
    for kind, (weight, out) in enumerate(((key_w, keys), (value_w, values))):
        loads[4 + kind].wait()
        for start in range(0, INNER, 256):
            cols = slice(start, start + 256)
            made[kind, :, cols] = dot(normed_low[...], weight[:, cols]).astype(LOW)
        for shift in (1, 2, 3):
            for slot in range(2):
                strip = index[camera, lax.rem(camera + shift, 4), slot]
                at = pl.ds(pl.multiple_of(strip * STRIP, STRIP), STRIP)
                stores.append(
                    pltpu.make_async_copy(
                        made.at[kind, at],
                        sends[shift - 1].at[kind, slot],
                        send_sem.at[kind * SLOTS + 2 * (shift - 1) + slot],
                    )
                )
                stores[-1].start()
        stores.append(pltpu.make_async_copy(made.at[kind], out, out_sem.at[1 + kind]))
        stores[-1].start()
    for store in stores:
        store.wait()


def project_keys(ids, index, tokens, w_key, w_value):
    return call(
        project_keys_kernel,
        1,
        2,
        [IN_PLACE] * 3,
        [IN_PLACE] * 6,
        [array((ROWS, MODEL), LOW), array((ROWS, INNER), LOW), array((ROWS, INNER), LOW)]
        + [array((2, 2, STRIP, INNER), LOW)] * 3,
        [
            pltpu.VMEM((ROWS, MODEL), LOW),
            pltpu.VMEM((MODEL, INNER), LOW),
            pltpu.VMEM((MODEL, INNER), LOW),
            pltpu.VMEM((ROWS, MODEL), LOW),
            pltpu.VMEM((2, ROWS, INNER), LOW),
            pltpu.SemaphoreType.DMA((6,)),
            pltpu.SemaphoreType.DMA((3,)),
            pltpu.SemaphoreType.DMA((2 * SLOTS,)),
        ],
        4 * ROWS * MODEL * INNER,
        12 << 20,
        vmem=16,
    )(ids, index, tokens, w_key, w_value)


def project_queries_kernel(low, grad_update, w_query, w_out, queries, grad_mixed):
    product = dot(low[...], w_query[...]).astype(LOW)
    queries[...] = product * jnp.asarray(0.125, LOW)
    grad_mixed[...] = dot_t(grad_update[...], w_out[...]).astype(LOW)


def project_queries(low, grad_update, w_query, w_out):
    width = 384
    out = pl.BlockSpec((ROWS, width), lambda j: (0, j))
    return call(
        project_queries_kernel,
        INNER // width,
        0,
        [
            whole((ROWS, MODEL)),
            whole((ROWS, MODEL)),
            pl.BlockSpec((MODEL, width), lambda j: (0, j)),
            pl.BlockSpec((width, MODEL), lambda j: (j, 0)),
        ],
        [out, out],
        [array((ROWS, INNER), LOW)] * 2,
        [],
        4 * ROWS * MODEL * INNER,
        10 << 20,
    )(low, grad_update, w_query, w_out)


def parts_of(frame):
    return frame // 8, lax.rem(frame // 2, 4), lax.rem(frame, 2)


def source_of(offsets, frame, read):
    source = frame - offsets[frame, read]
    return jnp.maximum(source, 0), source >= 0


def back_to(frame, source):
    z_here, x_here, core_here = parts_of(frame)
    z_at, x_at, core_at = parts_of(source)
    return lax.rem(z_here - z_at + 4, 4), lax.rem(x_here - x_at + 4, 4), core_at == core_here


def pick_kernel(ids, offsets, held_0, held_1, held_2, held_3, picked, sem):
    frame = ids[1]
    partner = frame + 1 - 2 * lax.rem(frame, 2)
    held = (held_0, held_1, held_2, held_3)
    wanted = []
    for read in range(READS):
        source, live = source_of(offsets, partner, read)
        back_z, back_x, same = back_to(frame, source)
        wanted.append(jnp.logical_and(live, same))
        for shift in range(4):

            @pl.when(jnp.logical_and(wanted[read], back_x == shift))
            def _():
                pltpu.make_async_copy(held[shift].at[back_z], picked.at[read], sem.at[read]).start()

        @pl.when(jnp.logical_not(wanted[read]))
        def _():
            picked[read] = jnp.zeros((MEM, MODEL), LOW)

    for read in range(READS):

        @pl.when(wanted[read])
        def _():
            pltpu.make_async_copy(held_0.at[0], picked.at[read], sem.at[read]).wait()


def pick(ids, offsets, held):
    return call(
        pick_kernel,
        1,
        2,
        [IN_PLACE] * 4,
        whole((READS, MEM, MODEL)),
        array((READS, MEM, MODEL), LOW),
        [pltpu.SemaphoreType.DMA((READS,))],
        0,
        1 << 20,
        vmem=2,
    )(ids, offsets, *held)


def project_memory_kernel(ids, offsets, held_0, held_1, held_2, held_3, given, w_key, w_value, keys, values, *rest):
    rows, low, key_w, value_w, sem, w_sem = rest
    frame = ids[1]
    held = (held_0, held_1, held_2, held_3)
    loads = [
        pltpu.make_async_copy(w_key, key_w, w_sem.at[0]),
        pltpu.make_async_copy(w_value, value_w, w_sem.at[1]),
    ]
    for read in range(READS):
        source, live = source_of(offsets, frame, read)
        back_z, back_x, same = back_to(frame, source)
        mine = jnp.logical_and(live, same)
        for shift in range(4):

            @pl.when(jnp.logical_and(mine, back_x == shift))
            def _():
                pltpu.make_async_copy(held[shift].at[back_z], rows.at[read], sem.at[read]).start()

        @pl.when(jnp.logical_not(mine))
        def _():
            pltpu.make_async_copy(given.at[read], rows.at[read], sem.at[read]).start()

    for load in loads:
        load.start()
    for read in range(READS):
        pltpu.make_async_copy(given.at[read], rows.at[read], sem.at[read]).wait()
        low[read * MEM : (read + 1) * MEM, :] = normalize(rows[read])[0].astype(LOW)
    for load, weight, out in zip(loads, (key_w, value_w), (keys, values)):
        load.wait()
        for start in range(0, INNER, 256):
            cols = slice(start, start + 256)
            out[:, cols] = dot(low[...], weight[:, cols]).astype(LOW)


def project_memory(ids, offsets, held, given, w_key, w_value):
    return call(
        project_memory_kernel,
        1,
        2,
        [IN_PLACE] * 7,
        [whole((READS * MEM, INNER))] * 2,
        [array((READS * MEM, INNER), LOW)] * 2,
        [
            pltpu.VMEM((READS, MEM, MODEL), LOW),
            pltpu.VMEM((READS * MEM, MODEL), LOW),
            pltpu.VMEM((MODEL, INNER), LOW),
            pltpu.VMEM((MODEL, INNER), LOW),
            pltpu.SemaphoreType.DMA((READS,)),
            pltpu.SemaphoreType.DMA((2,)),
        ],
        4 * READS * MEM * MODEL * INNER,
        6 << 20,
        vmem=10,
    )(ids, offsets, *held, given, w_key, w_value)


def shift_z(by):
    return [(f, (f + 8 * by) % 32) for f in range(32)]


def shift_x(by):
    return [(f, f // 8 * 8 + (f % 8 + 2 * by) % 8) for f in range(32)]


SWAP_CORE = [(f, f ^ 1) for f in range(32)]


def shift_cam(by):
    return [(s, (s + by) % 4) for s in range(4)]


def attention_kernel(ids, offsets, count, queries, grads, keys_own, values_own, keys_mem, values_mem, *rest):
    far_in, rest = rest[:3], rest[3:]
    mixed, grad_query, grad_keys, grad_values, grad_mem, grad_mem_low = rest[:6]
    far_out, rest = rest[6:9], rest[9:]
    keys, values, keys_t, values_t, scores, grad_w, weights, grad_s, two_q, two_g, rest_k, rest_v = rest
    camera, frame = ids[0], ids[1]

    slot_live, slot_at, live_total = [], [], 0
    for slot in range(SLOTS):
        sender = lax.rem(camera + 4 - (slot // 2 + 1), 4)
        live = count[sender, camera] > slot % 2
        slot_live.append(jnp.logical_and(live, live_total < LIVE_MAX))
        slot_at.append(jnp.minimum(live_total, LIVE_MAX - 1))
        live_total = live_total + live.astype(jnp.int32)

    keys[0:ROWS, :] = keys_own[...]
    values[0:ROWS, :] = values_own[...]
    keys[MEM_AT:FAR_AT, :] = keys_mem[...]
    values[MEM_AT:FAR_AT, :] = values_mem[...]
    for place in range(LIVE_MAX):

        @pl.when(live_total <= place)
        def _():
            at = slice(FAR_AT + place * STRIP, FAR_AT + (place + 1) * STRIP)
            keys[at, :] = jnp.zeros((STRIP, PAIR), LOW)
            values[at, :] = jnp.zeros((STRIP, PAIR), LOW)

    for slot in range(SLOTS):

        @pl.when(slot_live[slot])
        def _():
            at = pl.ds(pl.multiple_of(FAR_AT + slot_at[slot] * STRIP, STRIP), STRIP)
            keys[at, :] = far_in[slot // 2][0, slot % 2]
            values[at, :] = far_in[slot // 2][1, slot % 2]

    keys_t[...] = keys[...].T
    values_t[...] = values[...].T
    lane = lax.broadcasted_iota(jnp.int32, (ROWS, PAIR), 1)
    for head in range(2):
        keep = (lane >= 64) if head else (lane < 64)
        at = slice(head * ROWS, (head + 1) * ROWS)
        two_q[at, :] = jnp.where(keep, queries[...], jnp.zeros((ROWS, PAIR), LOW))
        two_g[at, :] = jnp.where(keep, grads[...], jnp.zeros((ROWS, PAIR), LOW))

    pieces = [(0, ROWS, None)]
    for read in range(READS):
        start = MEM_AT + read * MEM
        pieces.append((start, start + MEM, offsets[frame, read] <= frame))
    for place in range(LIVE_MAX):
        start = FAR_AT + place * STRIP
        pieces.append((start, start + STRIP, place < live_total))

    def pieces_of(base):
        for start, end, live in pieces:
            low, high = max(start, base), min(end, base + CHUNK)
            if low < high:
                yield low, high, live

    def folded(block):
        return block.reshape(block.shape[0] // 8, 8, ROWS)

    bases = range(0, KEYS, CHUNK)
    highest = [jnp.full((8, ROWS), MASKED, WIDE)] * 2
    total, inner = [jnp.zeros((8, ROWS), WIDE)] * 2, [jnp.zeros((8, ROWS), WIDE)] * 2
    share = [None, None]

    def score(head, base):
        cols = slice(head * ROWS, (head + 1) * ROWS)
        block = dot_t(keys[base : base + CHUNK, :], two_q[cols, :])
        scores[head, base : base + CHUNK, :] = block
        for low, high, live in pieces_of(base):
            top = jnp.max(folded(block[low - base : high - base]), axis=0)
            top = jnp.maximum(highest[head], top)
            highest[head] = top if live is None else jnp.where(live, top, highest[head])
        if base == bases[-1]:
            highest[head] = jnp.max(highest[head], axis=0, keepdims=True)

    def lift(head, base):
        cols = slice(head * ROWS, (head + 1) * ROWS)
        block = dot_t(values[base : base + CHUNK, :], two_g[cols, :])
        grad_w[head, base : base + CHUNK, :] = block
        for low, high, live in pieces_of(base):
            top = highest[head] if live is None else jnp.where(live, highest[head], -MASKED)
            lifted = jnp.exp(scores[head, low:high, :] - top)
            scores[head, low:high, :] = lifted
            total[head] = total[head] + jnp.sum(folded(lifted), axis=0)
            inner[head] = inner[head] + jnp.sum(folded(lifted * block[low - base : high - base]), axis=0)
        if base == bases[-1]:
            share[head] = 1.0 / jnp.sum(total[head], axis=0, keepdims=True)
            inner[head] = jnp.sum(inner[head], axis=0, keepdims=True) * share[head]

    def settle(head, base):
        cols, at = slice(head * ROWS, (head + 1) * ROWS), slice(base, base + CHUNK)
        part = scores[head, at, :] * share[head]
        weights[at, cols] = part.astype(LOW)
        grad_s[at, cols] = (part * (grad_w[head, at, :] - inner[head])).astype(LOW)

    def row_grads(head, base):
        cols, at = slice(head * ROWS, (head + 1) * ROWS), slice(base, base + CHUNK)
        for_value = dot(weights[at, cols], two_g[cols, :])
        for_key = dot(grad_s[at, cols], two_q[cols, :])
        for made, own, far in ((for_key, grad_keys, rest_k), (for_value, grad_values, rest_v)):
            for start, end, ref, shift in ((0, ROWS, own, 0), (ROWS, KEYS, far, ROWS)):
                first, last = max(start, base), min(end, base + CHUNK)
                if first < last:
                    there = slice(first - shift, last - shift)
                    block = made[first - base : last - base]
                    ref[there, :] = block if head == 0 else ref[there, :] + block

    mixed_t, grad_query_t = [None, None], [None, None]

    def query_side(head):
        cols, dims = slice(head * ROWS, (head + 1) * ROWS), slice(head * 64, (head + 1) * 64)
        mixed_t[head] = dot(values_t[dims, :], weights[:, cols])
        grad_query_t[head] = dot(keys_t[dims, :], grad_s[:, cols])

    for base in bases:
        score(0, base)
    for base in bases:
        lift(0, base)
        score(1, base)
    for base in bases:
        settle(0, base)
        lift(1, base)
    for base in bases:
        row_grads(0, base)
        settle(1, base)
    query_side(0)
    for base in bases:
        row_grads(1, base)
    query_side(1)
    mixed[...] = jnp.concatenate(mixed_t, axis=0).T.astype(LOW)
    grad_query[...] = (jnp.concatenate(grad_query_t, axis=0).T * 0.125).astype(LOW)

    grad_mem[0] = rest_k[0 : READS * MEM, :]
    grad_mem[1] = rest_v[0 : READS * MEM, :]
    grad_mem_low[0] = rest_k[0 : READS * MEM, :].astype(LOW)
    grad_mem_low[1] = rest_v[0 : READS * MEM, :].astype(LOW)
    for slot in range(SLOTS):

        @pl.when(slot_live[slot])
        def _():
            start = FAR_AT - ROWS + slot_at[slot] * STRIP
            at = pl.ds(pl.multiple_of(start, STRIP), STRIP)
            far_out[slot // 2][0, slot % 2] = rest_k[at, :].astype(LOW)
            far_out[slot // 2][1, slot % 2] = rest_v[at, :].astype(LOW)


def attention(group, ids, offsets, count, queries, grads, keys_own, values_own, keys_mem, values_mem, far):
    first, pairs = group
    width = pairs * PAIR

    def taken(rows):
        return pl.BlockSpec((rows, PAIR), lambda p, *_: (0, first + p))

    def made(rows):
        return pl.BlockSpec((rows, PAIR), lambda p, *_: (0, p))

    far_in = pl.BlockSpec((2, 2, STRIP, PAIR), lambda p, *_: (0, 0, 0, first + p))
    far_out = pl.BlockSpec((2, 2, STRIP, PAIR), lambda p, *_: (0, 0, 0, p))
    mem_out = pl.BlockSpec((2, READS * MEM, PAIR), lambda p, *_: (0, 0, p))
    return call(
        attention_kernel,
        pairs,
        3,
        [taken(ROWS)] * 4 + [taken(READS * MEM)] * 2 + [far_in] * 3,
        [made(ROWS)] * 4 + [mem_out] * 2 + [far_out] * 3,
        [array((ROWS, width), LOW)] * 2
        + [array((ROWS, width), WIDE)] * 2
        + [array((2, READS * MEM, width), WIDE), array((2, READS * MEM, width), LOW)]
        + [array((2, 2, STRIP, width), LOW)] * 3,
        [pltpu.VMEM((KEYS, PAIR), LOW)] * 2
        + [pltpu.VMEM((PAIR, KEYS), LOW)] * 2
        + [pltpu.VMEM((2, KEYS, ROWS), WIDE)] * 2
        + [pltpu.VMEM((KEYS, 2 * ROWS), LOW)] * 2
        + [pltpu.VMEM((2 * ROWS, PAIR), LOW)] * 2
        + [pltpu.VMEM((KEYS - ROWS, PAIR), WIDE)] * 2,
        pairs * 12 * KEYS * 2 * ROWS * 256,
        pairs * (3 << 20),
    )(ids, offsets, count, queries, grads, keys_own, values_own, keys_mem, values_mem, *far)


def sort_kernel(ids, offsets, *rest):
    count = len(GROUPS)
    own, given = rest[:count], rest[count : 2 * count]
    outs, total = rest[2 * count : 2 * count + 4], rest[2 * count + 4]
    frame = ids[1]
    z_here, x_here, core_here = parts_of(frame)
    partner = frame + 1 - 2 * core_here
    total[...] = jnp.zeros_like(total)
    for reader, arrays in ((frame, own), (partner, given)):
        for read in range(READS):
            source, live = source_of(offsets, reader, read)
            z_at, x_at, core_at = parts_of(source)
            to = lax.rem(x_at - x_here + 4, 4) * 4 + lax.rem(z_at - z_here + 4, 4)

            @pl.when(jnp.logical_and(live, core_at == core_here))
            def _():
                for (first, pairs), part in zip(GROUPS, arrays):
                    cols = slice(first * PAIR, (first + pairs) * PAIR)
                    for kind in range(2):
                        added = part[kind, read * MEM : (read + 1) * MEM, :].astype(WIDE)
                        total[to, kind, :, cols] = total[to, kind, :, cols] + added

    for shift in range(4):
        outs[shift][...] = total[4 * shift : 4 * shift + 4].astype(LOW)


def sort_reads(ids, offsets, own, given):
    shapes = [(2, READS * MEM, pairs * PAIR) for _, pairs in GROUPS]
    return call(
        sort_kernel,
        1,
        2,
        [whole(s) for s in shapes] * 2,
        [whole((4, 2, MEM, INNER))] * 4,
        [array((4, 2, MEM, INNER), LOW)] * 4,
        [pltpu.VMEM((16, 2, MEM, INNER), WIDE)],
        0,
        3 << 20,
    )(ids, offsets, *own, *given)


def add_kernel(part_0, part_1, part_2, part_3, *outs):
    for shift in range(4):
        total = part_0[shift].astype(WIDE) + part_1[shift].astype(WIDE)
        total = total + part_2[shift].astype(WIDE) + part_3[shift].astype(WIDE)
        outs[shift][...] = total.astype(LOW)


def add_reads(parts):
    return call(
        add_kernel,
        1,
        0,
        [whole((4, 2, MEM, INNER))] * 4,
        [whole((2, MEM, INNER))] * 4,
        [array((2, MEM, INNER), LOW)] * 4,
        [],
        0,
        2 << 20,
    )(*parts)


def outward_kernel(*refs):
    count = len(GROUPS)
    mixed, grad_query = refs[:count], refs[count : 2 * count]
    w_out, w_query, update, grad_normed = refs[2 * count :]
    total, part = 0.0, 0.0
    for (first, pairs), mixed_ref, grad_ref in zip(GROUPS, mixed, grad_query):
        cols = slice(first * PAIR, (first + pairs) * PAIR)
        total = total + dot(mixed_ref[...], w_out[cols, :])
        part = part + dot_t(grad_ref[...], w_query[:, cols])
    update[...] = total.astype(LOW)
    grad_normed[...] = part


def outward(mixed, grad_query, w_out, w_query):
    width = 512
    out = pl.BlockSpec((ROWS, width), lambda j: (0, j))
    parts = [whole((ROWS, pairs * PAIR)) for _, pairs in GROUPS]
    return call(
        outward_kernel,
        MODEL // width,
        0,
        parts
        + parts
        + [
            pl.BlockSpec((INNER, width), lambda j: (0, j)),
            pl.BlockSpec((width, INNER), lambda j: (j, 0)),
        ],
        [out, out],
        [array((ROWS, MODEL), LOW), array((ROWS, MODEL), WIDE)],
        [],
        4 * ROWS * MODEL * INNER,
        11 << 20,
    )(*mixed, *grad_query, w_out, w_query)


def token_grads_kernel(ids, count, index, *refs):
    groups = len(GROUPS)
    own = (refs[:groups], refs[groups : 2 * groups])
    back, refs = refs[2 * groups : 5 * groups], refs[5 * groups :]
    kept, (tokens, grad_part, w_key, w_value, grad_tokens), refs = refs[:4], refs[4:9], refs[9:]
    total, far, near, rows, grad_normed, key_w, value_w, low, made = refs[:9]
    own_sem, far_sem, near_sem, in_sem, out_sem = refs[9:]
    camera = ids[0]

    near_loads = [pltpu.make_async_copy(kept[k], near.at[k], near_sem.at[k]) for k in range(4)]
    own_loads, far_loads = [], []
    for group, (first, pairs) in enumerate(GROUPS):
        cols = pl.ds(first * PAIR, pairs * PAIR)
        for kind in range(2):
            own_loads.append(
                pltpu.make_async_copy(
                    own[kind][group], total.at[kind, :, cols], own_sem.at[2 * group + kind]
                )
            )
        for k in range(3):
            far_loads.append(
                pltpu.make_async_copy(
                    back[3 * group + k], far.at[k, :, :, :, cols], far_sem.at[3 * group + k]
                )
            )
    pairs_of_refs = ((w_key, key_w), (w_value, value_w), (grad_part, grad_normed), (tokens, rows))
    loads = [
        pltpu.make_async_copy(source, target, in_sem.at[k])
        for k, (source, target) in enumerate(pairs_of_refs)
    ]
    for load in own_loads + far_loads + near_loads + loads:
        load.start()
    for load in own_loads + far_loads:
        load.wait()
    for shift in (1, 2, 3):
        other = lax.rem(camera + shift, 4)
        for slot in range(2):

            @pl.when(slot < count[camera, other])
            def _():
                start = index[camera, other, slot] * STRIP
                at = pl.ds(pl.multiple_of(start, STRIP), STRIP)
                for kind in range(2):
                    total[kind, at, :] = total[kind, at, :] + far[shift - 1, kind, slot].astype(WIDE)

    for load in near_loads:
        load.wait()
    half = ROWS // 2
    row = lax.broadcasted_iota(jnp.int32, (half, 4 * MEM), 0)
    col = lax.broadcasted_iota(jnp.int32, (half, 4 * MEM), 1)
    stacked = [jnp.concatenate([near[k, kind] for k in range(4)], axis=0) for kind in range(2)]
    for load in loads:
        load.wait()
    stores = []
    for start in range(0, ROWS, half):
        at = slice(start, start + half)
        hit = row + start == (col % MEM) * (ROWS // MEM)
        spread = jnp.where(hit, 1.0, 0.0).astype(LOW)
        for kind in range(2):
            low[kind, at, :] = (total[kind, at, :] + dot(spread, stacked[kind])).astype(LOW)
        for first in range(0, MODEL, 512):
            cols = slice(first, first + 512)
            grad_normed[at, cols] = (
                grad_normed[at, cols]
                + dot_t(low[0, at, :], key_w[cols, :])
                + dot_t(low[1, at, :], value_w[cols, :])
            )
        for begin in range(start, start + half, 64):
            at = slice(begin, begin + 64)
            normed, inverse = normalize(rows[at, :])
            grad = grad_normed[at, :]
            first_mean = jnp.mean(grad, axis=-1, keepdims=True)
            second_mean = jnp.mean(grad * normed, axis=-1, keepdims=True)
            made[at, :] = (inverse * (grad - first_mean - normed * second_mean)).astype(LOW)
        block = pl.ds(start, half)
        stores.append(
            pltpu.make_async_copy(made.at[block], grad_tokens.at[block], out_sem.at[start // half])
        )
        stores[-1].start()
    for store in stores:
        store.wait()


def token_grads(ids, count, index, own_keys, own_values, back, kept, tokens, grad_part, w_key, w_value):
    groups = len(GROUPS)
    return call(
        token_grads_kernel,
        1,
        3,
        [IN_PLACE] * (5 * groups + 8),
        IN_PLACE,
        array((ROWS, MODEL), LOW),
        [
            pltpu.VMEM((2, ROWS, INNER), WIDE),
            pltpu.VMEM((3, 2, 2, STRIP, INNER), LOW),
            pltpu.VMEM((4, 2, MEM, INNER), LOW),
            pltpu.VMEM((ROWS, MODEL), LOW),
            pltpu.VMEM((ROWS, MODEL), WIDE),
            pltpu.VMEM((MODEL, INNER), LOW),
            pltpu.VMEM((MODEL, INNER), LOW),
            pltpu.VMEM((2, ROWS, INNER), LOW),
            pltpu.VMEM((ROWS, MODEL), LOW),
            pltpu.SemaphoreType.DMA((2 * groups,)),
            pltpu.SemaphoreType.DMA((3 * groups,)),
            pltpu.SemaphoreType.DMA((4,)),
            pltpu.SemaphoreType.DMA((4,)),
            pltpu.SemaphoreType.DMA((2,)),
        ],
        4 * ROWS * MODEL * INNER,
        16 << 20,
        vmem=26,
    )(ids, count, index, *own_keys, *own_values, *back, *kept, tokens, grad_part, w_key, w_value)


def send(value, axis, pairs):
    return lax.ppermute(value, axis, pairs)


def local(tokens, w_query, w_key, w_value, w_out, grad_update, offsets, count, index):
    tokens = tokens.reshape(ROWS, MODEL)
    grad_update = grad_update.reshape(ROWS, MODEL)
    ids = jnp.stack([lax.axis_index("cam"), lax.axis_index("tm")]).astype(jnp.int32)
    others = (1, 2, 3)

    kept = tokens.reshape(MEM, ROWS // MEM, MODEL)[:, 0]
    along_z = jnp.stack([kept] + [send(kept, "tm", shift_z(k)) for k in others])
    low, keys, values, *sends = project_keys(ids, index, tokens, w_key, w_value)
    far = [send(sends[k - 1], "cam", shift_cam(k)) for k in others]
    held = [along_z] + [send(along_z, "tm", shift_x(k)) for k in others]
    queries, grads = project_queries(low, grad_update, w_query, w_out)
    given = send(pick(ids, offsets, held), "tm", SWAP_CORE)
    keys_mem, values_mem = project_memory(ids, offsets, held, given, w_key, w_value)

    made, mem_given, back = [], [], []
    for group in GROUPS:
        args = (queries, grads, keys, values, keys_mem, values_mem, far)
        made.append(attention(group, ids, offsets, count, *args))
        mem_given.append(send(made[-1][5], "tm", SWAP_CORE))
        back += [send(made[-1][5 + k], "cam", shift_cam(-k)) for k in others]
    mixed, grad_query, own_keys, own_values, mem = [[m[k] for m in made] for k in range(5)]

    sorted_x = sort_reads(ids, offsets, mem, mem_given)
    parts = [sorted_x[0]] + [send(sorted_x[k], "tm", shift_x(k)) for k in others]
    update, grad_part = outward(mixed, grad_query, w_out, w_query)
    sorted_z = add_reads(parts)
    kept_grads = [sorted_z[0]] + [send(sorted_z[k], "tm", shift_z(k)) for k in others]
    args = (own_keys, own_values, back, kept_grads, tokens, grad_part, w_key, w_value)
    grad_tokens = token_grads(ids, count, index, *args)
    shape = (1, 1, ROWS, MODEL)
    return update.reshape(shape), grad_tokens.reshape(shape)


def solution(mesh):
    frames = P("cam", "tm", None, None)
    return jax.shard_map(
        local,
        mesh=mesh,
        in_specs=(frames, P(), P(), P(), P(), frames, P(), P(), P()),
        out_specs=(frames, frames),
        check_vma=False,
    )
```

profile of v0, /device:TPU:1, one launch (start us, length us, event | category | flops | bytes accessed | tf_op | source)
XLA Modules:
  0.0 158.6 jit_solution(18446489147121181560)
XLA Ops:
  1.9 4.5 %collective-permute-start.1 = (bf16[32,1536]{1,0:T(8,128)(2,1)S(1)}, bf16[32,1536]{1,0:T(8,128)(2,1)S(1)}, u32[]{:S(2)}, u32[]{:S(2)}) collective-permute-start(bf16[32,1536]{1,0:T(8,128)(2,1)S(1)} %bitcast.20), channel_id=1, source_target_pairs={{0,64},{4,68},{8,72},{12,76},{16,80},{20,84},{24,88},{28,92},{32,9... | collective-permute-start | bytes 294920 | tf_op jit(solution)/shard_map/ppermute | solution.py:689
  7.1 1.9 %collective-permute-start.2 = (bf16[32,1536]{1,0:T(8,128)(2,1)S(1)}, bf16[32,1536]{1,0:T(8,128)(2,1)S(1)}, u32[]{:S(2)}, u32[]{:S(2)}) collective-permute-start(bf16[32,1536]{1,0:T(8,128)(2,1)S(1)} %bitcast.22), channel_id=1, source_target_pairs={{0,96},{4,100},{8,104},{12,108},{16,112},{20,116},{24,120},{28,124... | collective-permute-start | bytes 294920 | tf_op jit(solution)/shard_map/ppermute | solution.py:689
  9.1 2.0 %collective-permute-done = bf16[32,1536]{1,0:T(8,128)(2,1)S(1)} collective-permute-done((bf16[32,1536]{1,0:T(8,128)(2,1)S(1)}, bf16[32,1536]{1,0:T(8,128)(2,1)S(1)}, u32[]{:S(2)}, u32[]{:S(2)}) %collective-permute-start) | collective-permute-done | bytes 98336 | tf_op jit(solution)/shard_map/ppermute | solution.py:689
  11.7 2.5 %collective-permute-start.5 = (bf16[4,32,1536]{2,1,0:T(8,128)(2,1)S(1)}, bf16[4,32,1536]{2,1,0:T(8,128)(2,1)S(1)}, u32[]{:S(2)}, u32[]{:S(2)}) collective-permute-start(bf16[4,32,1536]{2,1,0:T(8,128)(2,1)S(1)} %pad_maximum_fusion.held_0), channel_id=1, source_target_pairs={{0,24},{4,28},{8,0},{12,4},{16,8},{20,12},{24,16},{28,20},{32,56},... | collective-permute-start | bytes 1179656 | tf_op jit(solution)/shard_map/ppermute | solution.py:689
  21.0 7.7 %shard_map.104 = (bf16[512,1536]{1,0:T(8,128)(2,1)S(1)}, bf16[512,768]{1,0:T(8,128)(2,1)S(1)}, bf16[512,768]{1,0:T(8,128)(2,1)S(1)}, bf16[2,2,128,768]{3,2,1,0:T...) custom-call(s32[2]{0:T(128)S(1)} %pad_add_fusion.ids, s32[4,4,2]{2,1,0:T(4,128)S(1)} %copy.18.index, ...), custom_call_target="tpu_custom_call" | custom-call | flops 2415919104 | bytes 12582912 | tf_op jit(solution)/shard_map/pallas_call | solution.py:117
  33.0 2.6 %collective-permute-start.8 = (bf16[2,2,128,768]{3,2,1,0:T(8,128)(2,1)}, bf16[2,2,128,768]{3,2,1,0:T(8,128)(2,1)}, u32[]{:S(2)}, u32[]{:S(2)}) collective-permute-start(bf16[2,2,128,768]{3,2,1,0:T(8,128)(2,1)} %get-tuple-element.48), channel_id=1, source_target_pairs={{0,2},{1,3},{2,0},{3,1},{4,6},{5,7},{6,4},{7,5},{8,10},{9,11},{10,... | collective-permute-start | bytes 2359304 | tf_op jit(solution)/shard_map/ppermute | solution.py:689
  37.8 3.7 %collective-permute-start.6 = (bf16[4,32,1536]{2,1,0:T(8,128)(2,1)S(1)}, bf16[4,32,1536]{2,1,0:T(8,128)(2,1)S(1)}, u32[]{:S(2)}, u32[]{:S(2)}) collective-permute-start(bf16[4,32,1536]{2,1,0:T(8,128)(2,1)S(1)} %shard_map.106), channel_id=1, source_target_pairs={{0,4},{4,0},{8,12},{12,8},{16,20},{20,16},{24,28},{28,24},{32,36},... | collective-permute-start | bytes 1179656 | tf_op jit(solution)/shard_map/ppermute | solution.py:689
  46.3 4.0 %shard_map.105 = (bf16[512,768]{1,0:T(8,128)(2,1)S(1)}, bf16[512,768]{1,0:T(8,128)(2,1)S(1)}) custom-call(bf16[512,1536]{1,0:T(8,128)(2,1)S(1)} %copy-done.13, bf16[512,1536]{1,0:T(8,128)(2,1)S(1)} %bitcast.18, bf16[1536,768]{1,0:T(8,128)(2,1)S(1)} %copy-done.7, bf16[768,1536]{1,0:T(8,128)(2,1)S(1)} %copy-done.9), custom_call_target="tpu_custom_call" | custom-call | flops 2415919104 | bytes 10485760 | tf_op jit(solution)/shard_map/pallas_call | solution.py:150
  50.4 4.0 %shard_map.107 = (bf16[128,768]{1,0:T(8,128)(2,1)S(1)}, bf16[128,768]{1,0:T(8,128)(2,1)S(1)}) custom-call(s32[2]{0:T(128)S(1)} %pad_add_fusion.ids, s32[32,4]{1,0:T(8,128)S(1)} %copy.22.offsets, bf16[4,32,1536]{2,1,0:T(8,128)(2,1)S(1)} %pad_maximum_fusion.held_0, bf16[4,32,1536]{2,1,0:T(8,128)(2,1)S(1)} %collective-permute-done.3.held_1, ...), custom_call_target="tpu_custom_call" | custom-call | flops 603979776 | bytes 6291456 | tf_op jit(solution)/shard_map/pallas_call | solution.py:259
  54.4 13.7 %collective-permute-done.8.rest_1_ = bf16[2,2,128,768]{3,2,1,0:T(8,128)(2,1)} collective-permute-done((bf16[2,2,128,768]{3,2,1,0:T(8,128)(2,1)}, bf16[2,2,128,768]{3,2,1,0:T(8,128)(2,1)}, u32[]{:S(2)}, u32[]{:S(2)}) %collective-permute-start.8) | collective-permute-done | bytes 786464 | tf_op jit(solution)/shard_map/ppermute | solution.py:689
  69.2 16.8 %shard_map.109 = (bf16[512,384]{1,0:T(8,128)(2,1)S(1)}, bf16[512,384]{1,0:T(8,128)(2,1)S(1)}, f32[512,384]{1,0:T(8,128)S(1)}, f32[512,384]{1,0:T(8,128)S(1)}, f3...) custom-call(s32[2]{0:T(128)S(1)} %pad_add_fusion.ids, ...), custom_call_target="tpu_custom_call" | custom-call | flops 10871635968 | bytes 9437184 | tf_op jit(solution)/shard_map/pallas_call | solution.py:456
  86.0 2.2 %collective-permute-start.17 = (bf16[2,128,384]{2,1,0:T(8,128)(2,1)S(1)}, bf16[2,128,384]{2,1,0:T(8,128)(2,1)S(1)}, u32[]{:S(2)}, u32[]{:S(2)}) collective-permute-start(bf16[2,128,384]{2,1,0:T(8,128)(2,1)S(1)} %get-tuple-element.68), channel_id=1, source_target_pairs={{0,4},{4,0},{8,12},{12,8},{16,20},{20,16},{24,28},{28,24},{32,36},... | collective-permute-start | bytes 589832 | tf_op jit(solution)/shard_map/ppermute | solution.py:689
  88.3 16.8 %shard_map.108 = (bf16[512,384]{1,0:T(8,128)(2,1)S(1)}, bf16[512,384]{1,0:T(8,128)(2,1)S(1)}, f32[512,384]{1,0:T(8,128)S(1)}, f32[512,384]{1,0:T(8,128)S(1)}, f3...) custom-call(s32[2]{0:T(128)S(1)} %pad_add_fusion.ids, ...), custom_call_target="tpu_custom_call" | custom-call | flops 10871635968 | bytes 9437184 | tf_op jit(solution)/shard_map/pallas_call | solution.py:456
  105.2 1.8 %collective-permute-start.13 = (bf16[2,2,128,384]{3,2,1,0:T(8,128)(2,1)S(1)}, bf16[2,2,128,384]{3,2,1,0:T(8,128)(2,1)S(1)}, u32[]{:S(2)}, u32[]{:S(2)}) collective-permute-start(bf16[2,2,128,384]{3,2,1,0:T(8,128)(2,1)S(1)} %get-tuple-element.62), channel_id=1, source_target_pairs={{0,3},{1,0},{2,1},{3,2},{4,7},{5,4},{6,5},{7,6},{8,11},{9,8},{10,9... | collective-permute-start | bytes 1179656 | tf_op jit(solution)/shard_map/ppermute | solution.py:689
  110.2 1.7 %collective-permute-start.19 = (bf16[4,2,32,768]{3,2,1,0:T(8,128)(2,1)S(1)}, bf16[4,2,32,768]{3,2,1,0:T(8,128)(2,1)S(1)}, u32[]{:S(2)}, u32[]{:S(2)}) collective-permute-start(bf16[4,2,32,768]{3,2,1,0:T(8,128)(2,1)S(1)} %get-tuple-element.71), channel_id=1, source_target_pairs={{0,16},{4,20},{8,24},{12,28},{16,0},{20,4},{24,8},{28,12},{32,48},... | collective-permute-start | bytes 1179656 | tf_op jit(solution)/shard_map/ppermute | solution.py:689
  112.7 1.8 %collective-permute-start.14 = (bf16[2,2,128,384]{3,2,1,0:T(8,128)(2,1)S(1)}, bf16[2,2,128,384]{3,2,1,0:T(8,128)(2,1)S(1)}, u32[]{:S(2)}, u32[]{:S(2)}) collective-permute-start(bf16[2,2,128,384]{3,2,1,0:T(8,128)(2,1)S(1)} %get-tuple-element.63), channel_id=1, source_target_pairs={{0,2},{1,3},{2,0},{3,1},{4,6},{5,7},{6,4},{7,5},{8,10},{9,11},{10,... | collective-permute-start | bytes 1179656 | tf_op jit(solution)/shard_map/ppermute | solution.py:689
  116.3 3.4 %collective-permute-done.18.part_1 = bf16[4,2,32,768]{3,2,1,0:T(8,128)(2,1)S(1)} collective-permute-done((bf16[4,2,32,768]{3,2,1,0:T(8,128)(2,1)S(1)}, bf16[4,2,32,768]{3,2,1,0:T(8,128)(2,1)S(1)}, u32[]{:S(2)}, u32[]{:S(2)}) %collective-permute-start.18) | collective-permute-done | bytes 393248 | tf_op jit(solution)/shard_map/ppermute | solution.py:689
  119.7 1.9 %collective-permute-start.10 = (bf16[2,2,128,384]{3,2,1,0:T(8,128)(2,1)S(1)}, bf16[2,2,128,384]{3,2,1,0:T(8,128)(2,1)S(1)}, u32[]{:S(2)}, u32[]{:S(2)}) collective-permute-start(bf16[2,2,128,384]{3,2,1,0:T(8,128)(2,1)S(1)} %get-tuple-element.59), channel_id=1, source_target_pairs={{0,3},{1,0},{2,1},{3,2},{4,7},{5,4},{6,5},{7,6},{8,11},{9,8},{10,9... | collective-permute-start | bytes 1179656 | tf_op jit(solution)/shard_map/ppermute | solution.py:689
  121.7 7.1 %collective-permute-done.19.part_2 = bf16[4,2,32,768]{3,2,1,0:T(8,128)(2,1)S(1)} collective-permute-done((bf16[4,2,32,768]{3,2,1,0:T(8,128)(2,1)S(1)}, bf16[4,2,32,768]{3,2,1,0:T(8,128)(2,1)S(1)}, u32[]{:S(2)}, u32[]{:S(2)}) %collective-permute-start.19) | collective-permute-done | bytes 393248 | tf_op jit(solution)/shard_map/ppermute | solution.py:689
  128.8 2.4 %collective-permute-start.11 = (bf16[2,2,128,384]{3,2,1,0:T(8,128)(2,1)S(1)}, bf16[2,2,128,384]{3,2,1,0:T(8,128)(2,1)S(1)}, u32[]{:S(2)}, u32[]{:S(2)}) collective-permute-start(bf16[2,2,128,384]{3,2,1,0:T(8,128)(2,1)S(1)} %get-tuple-element.60), channel_id=1, source_target_pairs={{0,2},{1,3},{2,0},{3,1},{4,6},{5,7},{6,4},{7,5},{8,10},{9,11},{10,... | collective-permute-start | bytes 1179656 | tf_op jit(solution)/shard_map/ppermute | solution.py:689
  132.4 2.8 %collective-permute-start.22 = (bf16[2,32,768]{2,1,0:T(8,128)(2,1)S(1)}, bf16[2,32,768]{2,1,0:T(8,128)(2,1)S(1)}, u32[]{:S(2)}, u32[]{:S(2)}) collective-permute-start(bf16[2,32,768]{2,1,0:T(8,128)(2,1)S(1)} %get-tuple-element.75), channel_id=1, source_target_pairs={{0,64},{4,68},{8,72},{12,76},{16,80},{20,84},{24,88},{28,92},{32,9... | collective-permute-start | bytes 294920 | tf_op jit(solution)/shard_map/ppermute | solution.py:689
  135.8 4.3 %shard_map.110 = (bf16[512,1536]{1,0:T(8,128)(2,1)}, f32[512,1536]{1,0:T(8,128)S(1)}) custom-call(bf16[512,384]{1,0:T(8,128)(2,1)S(1)} %get-tuple-element.50.refs_0_, bf16[512,384]{1,0:T(8,128)(2,1)S(1)} %get-tuple-element.51.refs_1_, bf16[512,384]{1,0:T(8,128)(2,1)S(1)} %get-tuple-element.52.refs_2_, bf16[512,384]{1,0:T(8,128)(2,1)S(1)} %get-tuple-element.53.refs_3_, ...), custom_call_target="tpu_custom_call" | custom-call | flops 2415919104 | bytes 11534336 | tf_op jit(solution)/shard_map/pallas_call | solution.py:556
  141.5 9.2 %collective-permute-done.12.refs_6_ = bf16[2,2,128,384]{3,2,1,0:T(8,128)(2,1)S(1)} collective-permute-done((bf16[2,2,128,384]{3,2,1,0:T(8,128)(2,1)S(1)}, bf16[2,2,128,384]{3,2,1,0:T(8,128)(2,1)S(1)}, u32[]{:S(2)}, u32[]{:S(2)}) %collective-permute-start.12) | collective-permute-done | bytes 393248 | tf_op jit(solution)/shard_map/ppermute | solution.py:689
  150.6 7.8 %shard_map.113 = bf16[512,1536]{1,0:T(8,128)(2,1)} custom-call(s32[2]{0:T(128)S(1)} %pad_add_fusion.ids, s32[4,4]{1,0:T(4,128)S(1)} %copy-done.6, s32[4,4,2]{2,1,0:T(4,128)S(1)} %copy.18.index, f32[512,384]{1,0:T(8,128)S(1)} %get-tuple-element.55.refs_0_, f32[512,384]{1,0:T(8,128)S(1)} %get-tuple-element.56.refs_1_, ...), custom_call_target="tpu_custom_call" | custom-call | flops 2415919104 | bytes 16777216 | tf_op jit(solution)/shard_map/pallas_call | solution.py:659
  (78 shorter events, 30.7 us)
Async XLA Ops:
  1.9 7.2 %collective-permute-start.1 = (bf16[32,1536]{1,0:T(8,128)(2,1)S(1)}, bf16[32,1536]{1,0:T(8,128)(2,1)S(1)}, u32[]{:S(2)}, u32[]{:S(2)}) collective-permute-start(bf16[32,1536]{1,0:T(8,128)(2,1)S(1)} %bitcast.20), channel_id=1, source_target_pairs={{0,64},{4,68},{8,72},{12,76},{16,80},{20,84},{24,88},{28,92},{32,9... | collective-permute-start | bytes 294920 | tf_op jit(solution)/shard_map/ppermute | solution.py:689
  6.4 4.7 %collective-permute-start = (bf16[32,1536]{1,0:T(8,128)(2,1)S(1)}, bf16[32,1536]{1,0:T(8,128)(2,1)S(1)}, u32[]{:S(2)}, u32[]{:S(2)}) collective-permute-start(bf16[32,1536]{1,0:T(8,128)(2,1)S(1)} %bitcast.21), channel_id=1, source_target_pairs={{0,32},{4,36},{8,40},{12,44},{16,48},{20,52},{24,56},{28,60},{32,6... | collective-permute-start | bytes 294920 | tf_op jit(solution)/shard_map/ppermute | solution.py:689
  7.1 4.6 %collective-permute-start.2 = (bf16[32,1536]{1,0:T(8,128)(2,1)S(1)}, bf16[32,1536]{1,0:T(8,128)(2,1)S(1)}, u32[]{:S(2)}, u32[]{:S(2)}) collective-permute-start(bf16[32,1536]{1,0:T(8,128)(2,1)S(1)} %bitcast.22), channel_id=1, source_target_pairs={{0,96},{4,100},{8,104},{12,108},{16,112},{20,116},{24,120},{28,124... | collective-permute-start | bytes 294920 | tf_op jit(solution)/shard_map/ppermute | solution.py:689
  11.7 23.9 %collective-permute-start.5 = (bf16[4,32,1536]{2,1,0:T(8,128)(2,1)S(1)}, bf16[4,32,1536]{2,1,0:T(8,128)(2,1)S(1)}, u32[]{:S(2)}, u32[]{:S(2)}) collective-permute-start(bf16[4,32,1536]{2,1,0:T(8,128)(2,1)S(1)} %pad_maximum_fusion.held_0), channel_id=1, source_target_pairs={{0,24},{4,28},{8,0},{12,4},{16,8},{20,12},{24,16},{28,20},{32,56},... | collective-permute-start | bytes 1179656 | tf_op jit(solution)/shard_map/ppermute | solution.py:689
  15.2 21.6 %collective-permute-start.4 = (bf16[4,32,1536]{2,1,0:T(8,128)(2,1)S(1)}, bf16[4,32,1536]{2,1,0:T(8,128)(2,1)S(1)}, u32[]{:S(2)}, u32[]{:S(2)}) collective-permute-start(bf16[4,32,1536]{2,1,0:T(8,128)(2,1)S(1)} %pad_maximum_fusion.held_0), channel_id=1, source_target_pairs={{0,16},{4,20},{8,24},{12,28},{16,0},{20,4},{24,8},{28,12},{32,48},... | collective-permute-start | bytes 1179656 | tf_op jit(solution)/shard_map/ppermute | solution.py:689
  15.7 21.1 %collective-permute-start.3 = (bf16[4,32,1536]{2,1,0:T(8,128)(2,1)S(1)}, bf16[4,32,1536]{2,1,0:T(8,128)(2,1)S(1)}, u32[]{:S(2)}, u32[]{:S(2)}) collective-permute-start(bf16[4,32,1536]{2,1,0:T(8,128)(2,1)S(1)} %pad_maximum_fusion.held_0), channel_id=1, source_target_pairs={{0,8},{4,12},{8,16},{12,20},{16,24},{20,28},{24,0},{28,4},{32,40},... | collective-permute-start | bytes 1179656 | tf_op jit(solution)/shard_map/ppermute | solution.py:689
  31.7 22.7 %collective-permute-start.7 = (bf16[2,2,128,768]{3,2,1,0:T(8,128)(2,1)}, bf16[2,2,128,768]{3,2,1,0:T(8,128)(2,1)}, u32[]{:S(2)}, u32[]{:S(2)}) collective-permute-start(bf16[2,2,128,768]{3,2,1,0:T(8,128)(2,1)} %get-tuple-element.47), channel_id=1, source_target_pairs={{0,1},{1,2},{2,3},{3,0},{4,5},{5,6},{6,7},{7,4},{8,9},{9,10},{10,1... | collective-permute-start | bytes 2359304 | tf_op jit(solution)/shard_map/ppermute | solution.py:689
  33.0 35.1 %collective-permute-start.8 = (bf16[2,2,128,768]{3,2,1,0:T(8,128)(2,1)}, bf16[2,2,128,768]{3,2,1,0:T(8,128)(2,1)}, u32[]{:S(2)}, u32[]{:S(2)}) collective-permute-start(bf16[2,2,128,768]{3,2,1,0:T(8,128)(2,1)} %get-tuple-element.48), channel_id=1, source_target_pairs={{0,2},{1,3},{2,0},{3,1},{4,6},{5,7},{6,4},{7,5},{8,10},{9,11},{10,... | collective-permute-start | bytes 2359304 | tf_op jit(solution)/shard_map/ppermute | solution.py:689
  35.6 33.5 %collective-permute-start.9 = (bf16[2,2,128,768]{3,2,1,0:T(8,128)(2,1)}, bf16[2,2,128,768]{3,2,1,0:T(8,128)(2,1)}, u32[]{:S(2)}, u32[]{:S(2)}) collective-permute-start(bf16[2,2,128,768]{3,2,1,0:T(8,128)(2,1)} %get-tuple-element.49), channel_id=1, source_target_pairs={{0,3},{1,0},{2,1},{3,2},{4,7},{5,4},{6,5},{7,6},{8,11},{9,8},{10,9... | collective-permute-start | bytes 2359304 | tf_op jit(solution)/shard_map/ppermute | solution.py:689
  37.8 12.5 %collective-permute-start.6 = (bf16[4,32,1536]{2,1,0:T(8,128)(2,1)S(1)}, bf16[4,32,1536]{2,1,0:T(8,128)(2,1)S(1)}, u32[]{:S(2)}, u32[]{:S(2)}) collective-permute-start(bf16[4,32,1536]{2,1,0:T(8,128)(2,1)S(1)} %shard_map.106), channel_id=1, source_target_pairs={{0,4},{4,0},{8,12},{12,8},{16,20},{20,16},{24,28},{28,24},{32,36},... | collective-permute-start | bytes 1179656 | tf_op jit(solution)/shard_map/ppermute | solution.py:689
  86.0 21.0 %collective-permute-start.17 = (bf16[2,128,384]{2,1,0:T(8,128)(2,1)S(1)}, bf16[2,128,384]{2,1,0:T(8,128)(2,1)S(1)}, u32[]{:S(2)}, u32[]{:S(2)}) collective-permute-start(bf16[2,128,384]{2,1,0:T(8,128)(2,1)S(1)} %get-tuple-element.68), channel_id=1, source_target_pairs={{0,4},{4,0},{8,12},{12,8},{16,20},{20,16},{24,28},{28,24},{32,36},... | collective-permute-start | bytes 589832 | tf_op jit(solution)/shard_map/ppermute | solution.py:689
  105.1 1.9 %collective-permute-start.16 = (bf16[2,128,384]{2,1,0:T(8,128)(2,1)S(1)}, bf16[2,128,384]{2,1,0:T(8,128)(2,1)S(1)}, u32[]{:S(2)}, u32[]{:S(2)}) collective-permute-start(bf16[2,128,384]{2,1,0:T(8,128)(2,1)S(1)} %get-tuple-element.67), channel_id=1, source_target_pairs={{0,4},{4,0},{8,12},{12,8},{16,20},{20,16},{24,28},{28,24},{32,36},... | collective-permute-start | bytes 589832 | tf_op jit(solution)/shard_map/ppermute | solution.py:689
  105.2 10.3 %collective-permute-start.13 = (bf16[2,2,128,384]{3,2,1,0:T(8,128)(2,1)S(1)}, bf16[2,2,128,384]{3,2,1,0:T(8,128)(2,1)S(1)}, u32[]{:S(2)}, u32[]{:S(2)}) collective-permute-start(bf16[2,2,128,384]{3,2,1,0:T(8,128)(2,1)S(1)} %get-tuple-element.62), channel_id=1, source_target_pairs={{0,3},{1,0},{2,1},{3,2},{4,7},{5,4},{6,5},{7,6},{8,11},{9,8},{10,9... | collective-permute-start | bytes 1179656 | tf_op jit(solution)/shard_map/ppermute | solution.py:689
  108.6 11.2 %collective-permute-start.18 = (bf16[4,2,32,768]{3,2,1,0:T(8,128)(2,1)S(1)}, bf16[4,2,32,768]{3,2,1,0:T(8,128)(2,1)S(1)}, u32[]{:S(2)}, u32[]{:S(2)}) collective-permute-start(bf16[4,2,32,768]{3,2,1,0:T(8,128)(2,1)S(1)} %get-tuple-element.70), channel_id=1, source_target_pairs={{0,8},{4,12},{8,16},{12,20},{16,24},{20,28},{24,0},{28,4},{32,40},... | collective-permute-start | bytes 1179656 | tf_op jit(solution)/shard_map/ppermute | solution.py:689
  110.2 18.5 %collective-permute-start.19 = (bf16[4,2,32,768]{3,2,1,0:T(8,128)(2,1)S(1)}, bf16[4,2,32,768]{3,2,1,0:T(8,128)(2,1)S(1)}, u32[]{:S(2)}, u32[]{:S(2)}) collective-permute-start(bf16[4,2,32,768]{3,2,1,0:T(8,128)(2,1)S(1)} %get-tuple-element.71), channel_id=1, source_target_pairs={{0,16},{4,20},{8,24},{12,28},{16,0},{20,4},{24,8},{28,12},{32,48},... | collective-permute-start | bytes 1179656 | tf_op jit(solution)/shard_map/ppermute | solution.py:689
  111.9 19.2 %collective-permute-start.20 = (bf16[4,2,32,768]{3,2,1,0:T(8,128)(2,1)S(1)}, bf16[4,2,32,768]{3,2,1,0:T(8,128)(2,1)S(1)}, u32[]{:S(2)}, u32[]{:S(2)}) collective-permute-start(bf16[4,2,32,768]{3,2,1,0:T(8,128)(2,1)S(1)} %get-tuple-element.72), channel_id=1, source_target_pairs={{0,24},{4,28},{8,0},{12,4},{16,8},{20,12},{24,16},{28,20},{32,56},... | collective-permute-start | bytes 1179656 | tf_op jit(solution)/shard_map/ppermute | solution.py:689
  112.7 18.8 %collective-permute-start.14 = (bf16[2,2,128,384]{3,2,1,0:T(8,128)(2,1)S(1)}, bf16[2,2,128,384]{3,2,1,0:T(8,128)(2,1)S(1)}, u32[]{:S(2)}, u32[]{:S(2)}) collective-permute-start(bf16[2,2,128,384]{3,2,1,0:T(8,128)(2,1)S(1)} %get-tuple-element.63), channel_id=1, source_target_pairs={{0,2},{1,3},{2,0},{3,1},{4,6},{5,7},{6,4},{7,5},{8,10},{9,11},{10,... | collective-permute-start | bytes 1179656 | tf_op jit(solution)/shard_map/ppermute | solution.py:689
  115.5 16.9 %collective-permute-start.15 = (bf16[2,2,128,384]{3,2,1,0:T(8,128)(2,1)S(1)}, bf16[2,2,128,384]{3,2,1,0:T(8,128)(2,1)S(1)}, u32[]{:S(2)}, u32[]{:S(2)}) collective-permute-start(bf16[2,2,128,384]{3,2,1,0:T(8,128)(2,1)S(1)} %get-tuple-element.64), channel_id=1, source_target_pairs={{0,1},{1,2},{2,3},{3,0},{4,5},{5,6},{6,7},{7,4},{8,9},{9,10},{10,1... | collective-permute-start | bytes 1179656 | tf_op jit(solution)/shard_map/ppermute | solution.py:689
  119.7 15.5 %collective-permute-start.10 = (bf16[2,2,128,384]{3,2,1,0:T(8,128)(2,1)S(1)}, bf16[2,2,128,384]{3,2,1,0:T(8,128)(2,1)S(1)}, u32[]{:S(2)}, u32[]{:S(2)}) collective-permute-start(bf16[2,2,128,384]{3,2,1,0:T(8,128)(2,1)S(1)} %get-tuple-element.59), channel_id=1, source_target_pairs={{0,3},{1,0},{2,1},{3,2},{4,7},{5,4},{6,5},{7,6},{8,11},{9,8},{10,9... | collective-permute-start | bytes 1179656 | tf_op jit(solution)/shard_map/ppermute | solution.py:689
  128.8 12.7 %collective-permute-start.11 = (bf16[2,2,128,384]{3,2,1,0:T(8,128)(2,1)S(1)}, bf16[2,2,128,384]{3,2,1,0:T(8,128)(2,1)S(1)}, u32[]{:S(2)}, u32[]{:S(2)}) collective-permute-start(bf16[2,2,128,384]{3,2,1,0:T(8,128)(2,1)S(1)} %get-tuple-element.60), channel_id=1, source_target_pairs={{0,2},{1,3},{2,0},{3,1},{4,6},{5,7},{6,4},{7,5},{8,10},{9,11},{10,... | collective-permute-start | bytes 1179656 | tf_op jit(solution)/shard_map/ppermute | solution.py:689
  131.1 19.5 %collective-permute-start.12 = (bf16[2,2,128,384]{3,2,1,0:T(8,128)(2,1)S(1)}, bf16[2,2,128,384]{3,2,1,0:T(8,128)(2,1)S(1)}, u32[]{:S(2)}, u32[]{:S(2)}) collective-permute-start(bf16[2,2,128,384]{3,2,1,0:T(8,128)(2,1)S(1)} %get-tuple-element.61), channel_id=1, source_target_pairs={{0,1},{1,2},{2,3},{3,0},{4,5},{5,6},{6,7},{7,4},{8,9},{9,10},{10,1... | collective-permute-start | bytes 1179656 | tf_op jit(solution)/shard_map/ppermute | solution.py:689
  131.5 19.1 %collective-permute-start.21 = (bf16[2,32,768]{2,1,0:T(8,128)(2,1)S(1)}, bf16[2,32,768]{2,1,0:T(8,128)(2,1)S(1)}, u32[]{:S(2)}, u32[]{:S(2)}) collective-permute-start(bf16[2,32,768]{2,1,0:T(8,128)(2,1)S(1)} %get-tuple-element.74), channel_id=1, source_target_pairs={{0,32},{4,36},{8,40},{12,44},{16,48},{20,52},{24,56},{28,60},{32,6... | collective-permute-start | bytes 294920 | tf_op jit(solution)/shard_map/ppermute | solution.py:689
  132.4 18.2 %collective-permute-start.22 = (bf16[2,32,768]{2,1,0:T(8,128)(2,1)S(1)}, bf16[2,32,768]{2,1,0:T(8,128)(2,1)S(1)}, u32[]{:S(2)}, u32[]{:S(2)}) collective-permute-start(bf16[2,32,768]{2,1,0:T(8,128)(2,1)S(1)} %get-tuple-element.75), channel_id=1, source_target_pairs={{0,64},{4,68},{8,72},{12,76},{16,80},{20,84},{24,88},{28,92},{32,9... | collective-permute-start | bytes 294920 | tf_op jit(solution)/shard_map/ppermute | solution.py:689
  135.2 15.4 %collective-permute-start.23 = (bf16[2,32,768]{2,1,0:T(8,128)(2,1)S(1)}, bf16[2,32,768]{2,1,0:T(8,128)(2,1)S(1)}, u32[]{:S(2)}, u32[]{:S(2)}) collective-permute-start(bf16[2,32,768]{2,1,0:T(8,128)(2,1)S(1)} %get-tuple-element.76), channel_id=1, source_target_pairs={{0,96},{4,100},{8,104},{12,108},{16,112},{20,116},{24,120},{28,124... | collective-permute-start | bytes 294920 | tf_op jit(solution)/shard_map/ppermute | solution.py:689
  (19 other events, 206.3 us)
where the time goes:
time: 159 us
  Pallas kernels  64.3 us (40%)
  waiting for transfers between devices  39.5 us (25%)
  starting transfers between devices  39.2 us (25%)
  local copies, waits for them, and re-layouts  14.6 us (9%)
    ppermute x24, waiting for transfers between devices, send(): return lax.ppermute(value, axis, pairs)  39.5 us
    ppermute x24, starting transfers between devices, send(): return lax.ppermute(value, axis, pairs)  39.2 us
    pallas_call x2, Pallas kernels, attention(): call(attention_kernel, pairs, 3, [taken(ROWS)] * 4 + [taken(READS * MEM)]...  33.7 us
    unnamed x41, local copies, waits for them, and re-layouts  13.3 us
    pallas_call x1, Pallas kernels, token_grads(): call(token_grads_kernel, 1, 3, [IN_PLACE] * (5 * groups + 8), IN_PLACE, a...  7.79 us
    pallas_call x1, Pallas kernels, project_keys(): call(project_keys_kernel, 1, 2, [IN_PLACE] * 3, [IN_PLACE] * 6, [array((R...  7.75 us
    pallas_call x1, Pallas kernels, outward(): call(outward_kernel, MODEL // width, 0, parts + parts + [pl.BlockSpec((IN...  4.31 us
    pallas_call x1, Pallas kernels, project_memory(): call(project_memory_kernel, 1, 2, [IN_PLACE] * 7, [whole((READS * MEM, IN...  4.01 us
  transfers between devices with their start and end apart: 24, of which 9 were waited for; matrix products, arithmetic and copies ran while one was open for 1% of the time, Pallas kernels for 25%

commit v1 on v0

--- a/solution.py
+++ b/solution.py
@@ -58,6 +58,7 @@
 
 
 IN_PLACE = pl.BlockSpec(memory_space=pl.ANY)
+IN_HBM = pl.BlockSpec(memory_space=pltpu.HBM)
 
 
 def array(shape, dtype):
@@ -84,33 +85,48 @@
     loads.append(pltpu.make_async_copy(w_value, value_w, in_sem.at[5]))
     for load in loads:
         load.start()
-    for step, start in enumerate(range(0, ROWS, STRIP)):
-        at = slice(start, start + STRIP)
-        loads[step].wait()
-        normed_low[at, :] = normalize(rows[at, :])[0].astype(LOW)
-    stores = [pltpu.make_async_copy(normed_low, low, out_sem.at[0])]
-    stores[0].start()
-    for kind, (weight, out) in enumerate(((key_w, keys), (value_w, values))):
-        loads[4 + kind].wait()
+
+    def norm(first, last):
+        for start in range(first, last, 64):
+            at = slice(start, start + 64)
+            normed_low[at, :] = normalize(rows[at, :])[0].astype(LOW)
+
+    def product(kind, weight, first, last):
         for start in range(0, INNER, 256):
             cols = slice(start, start + 256)
-            made[kind, :, cols] = dot(normed_low[...], weight[:, cols]).astype(LOW)
+            made[kind, first:last, cols] = dot(normed_low[first:last, :], weight[:, cols]).astype(LOW)
+
+    stores = []
+
+    def store(source, target, sem):
+        stores.append(pltpu.make_async_copy(source, target, sem))
+        stores[-1].start()
+
+    def publish(kind, out):
         for shift in (1, 2, 3):
             for slot in range(2):
                 strip = index[camera, lax.rem(camera + shift, 4), slot]
                 at = pl.ds(pl.multiple_of(strip * STRIP, STRIP), STRIP)
-                stores.append(
-                    pltpu.make_async_copy(
-                        made.at[kind, at],
-                        sends[shift - 1].at[kind, slot],
-                        send_sem.at[kind * SLOTS + 2 * (shift - 1) + slot],
-                    )
-                )
-                stores[-1].start()
-        stores.append(pltpu.make_async_copy(made.at[kind], out, out_sem.at[1 + kind]))
-        stores[-1].start()
-    for store in stores:
-        store.wait()
+                sem = send_sem.at[kind * SLOTS + 2 * (shift - 1) + slot]
+                store(made.at[kind, at], sends[shift - 1].at[kind, slot], sem)
+        store(made.at[kind], out, out_sem.at[1 + kind])
+
+    half = ROWS // 2
+    loads[0].wait()
+    loads[1].wait()
+    norm(0, half)
+    for load in loads[2:5]:
+        load.wait()
+    product(0, key_w, 0, half)
+    norm(half, ROWS)
+    store(normed_low, low, out_sem.at[0])
+    product(0, key_w, half, ROWS)
+    publish(0, keys)
+    loads[5].wait()
+    product(1, value_w, 0, ROWS)
+    publish(1, values)
+    for copy in stores:
+        copy.wait()
 
 
 def project_keys(ids, index, tokens, w_key, w_value):
@@ -118,7 +134,7 @@
         project_keys_kernel,
         1,
         2,
-        [IN_PLACE] * 3,
+        [IN_HBM] * 3,
         [IN_PLACE] * 6,
         [array((ROWS, MODEL), LOW), array((ROWS, INNER), LOW), array((ROWS, INNER), LOW)]
         + [array((2, 2, STRIP, INNER), LOW)] * 3,
@@ -134,7 +150,7 @@
         ],
         4 * ROWS * MODEL * INNER,
         12 << 20,
-        vmem=16,
+        vmem=60,
     )(ids, index, tokens, w_key, w_value)
 
 
@@ -260,7 +276,7 @@
         project_memory_kernel,
         1,
         2,
-        [IN_PLACE] * 7,
+        [IN_PLACE] * 5 + [IN_HBM] * 2,
         [whole((READS * MEM, INNER))] * 2,
         [array((READS * MEM, INNER), LOW)] * 2,
         [

time: 159 us -> 152 us (0.956)
  local copies, waits for them, and re-layouts: 14.6 us -> 7.5 us
  waiting for transfers between devices: 39.5 us -> 42.6 us
  starting transfers between devices: 39.2 us -> 36.5 us
    unnamed x41 -> x33, local copies, waits for them, and re-layouts: 13.3 us -> 6.26 us
    ppermute x24, waiting for transfers between devices: 39.5 us -> 42.6 us  [send(): return lax.ppermute(value, axis, pairs)]
    ppermute x24, starting transfers between devices: 39.2 us -> 36.5 us  [send(): return lax.ppermute(value, axis, pairs)]
  transfers between devices with their start and end apart: 24 -> 24, of which waited for: 9 -> 10; matrix products, arithmetic and copies ran while one was open for 1% -> 1% of each run, Pallas kernels for 25% -> 26%
where the time goes in v1:
time: 152 us
  Pallas kernels  64 us (42%)
  waiting for transfers between devices  42.6 us (28%)
  starting transfers between devices  36.5 us (24%)
  local copies, waits for them, and re-layouts  7.5 us (5%)
    ppermute x24, waiting for transfers between devices, send(): return lax.ppermute(value, axis, pairs)  42.6 us
    ppermute x24, starting transfers between devices, send(): return lax.ppermute(value, axis, pairs)  36.5 us
    pallas_call x2, Pallas kernels, attention(): call(attention_kernel, pairs, 3, [taken(ROWS)] * 4 + [taken(READS * MEM)]...  33.7 us
    pallas_call x1, Pallas kernels, token_grads(): call(token_grads_kernel, 1, 3, [IN_PLACE] * (5 * groups + 8), IN_PLACE, a...  7.79 us
    pallas_call x1, Pallas kernels, project_keys(): call(project_keys_kernel, 1, 2, [IN_HBM] * 3, [IN_PLACE] * 6, [array((ROW...  7.44 us
    unnamed x33, local copies, waits for them, and re-layouts  6.26 us
    pallas_call x1, Pallas kernels, outward(): call(outward_kernel, MODEL // width, 0, parts + parts + [pl.BlockSpec((IN...  4.32 us
    pallas_call x1, Pallas kernels, project_memory(): call(project_memory_kernel, 1, 2, [IN_PLACE] * 5 + [IN_HBM] * 2, [whole((...  4.01 us
  transfers between devices with their start and end apart: 24, of which 10 were waited for; matrix products, arithmetic and copies ran while one was open for 1% of the time, Pallas kernels for 26%

profile of v1, /device:TPU:1, one launch (start us, length us, event | category | flops | bytes accessed | tf_op | source)
XLA Modules:
  0.0 152.1 jit_solution(921786241747097137)
XLA Ops:
  1.9 4.5 %collective-permute-start.1 = (bf16[32,1536]{1,0:T(8,128)(2,1)S(1)}, bf16[32,1536]{1,0:T(8,128)(2,1)S(1)}, u32[]{:S(2)}, u32[]{:S(2)}) collective-permute-start(bf16[32,1536]{1,0:T(8,128)(2,1)S(1)} %bitcast.20), channel_id=1, source_target_pairs={{0,64},{4,68},{8,72},{12,76},{16,80},{20,84},{24,88},{28,92},{32,9... | collective-permute-start | bytes 294920 | tf_op jit(solution)/shard_map/ppermute | solution.py:705
  7.1 1.9 %collective-permute-start.2 = (bf16[32,1536]{1,0:T(8,128)(2,1)S(1)}, bf16[32,1536]{1,0:T(8,128)(2,1)S(1)}, u32[]{:S(2)}, u32[]{:S(2)}) collective-permute-start(bf16[32,1536]{1,0:T(8,128)(2,1)S(1)} %bitcast.22), channel_id=1, source_target_pairs={{0,96},{4,100},{8,104},{12,108},{16,112},{20,116},{24,120},{28,124... | collective-permute-start | bytes 294920 | tf_op jit(solution)/shard_map/ppermute | solution.py:705
  9.1 2.0 %collective-permute-done = bf16[32,1536]{1,0:T(8,128)(2,1)S(1)} collective-permute-done((bf16[32,1536]{1,0:T(8,128)(2,1)S(1)}, bf16[32,1536]{1,0:T(8,128)(2,1)S(1)}, u32[]{:S(2)}, u32[]{:S(2)}) %collective-permute-start) | collective-permute-done | bytes 98336 | tf_op jit(solution)/shard_map/ppermute | solution.py:705
  11.7 2.5 %collective-permute-start.5 = (bf16[4,32,1536]{2,1,0:T(8,128)(2,1)S(1)}, bf16[4,32,1536]{2,1,0:T(8,128)(2,1)S(1)}, u32[]{:S(2)}, u32[]{:S(2)}) collective-permute-start(bf16[4,32,1536]{2,1,0:T(8,128)(2,1)S(1)} %pad_maximum_fusion.held_0), channel_id=1, source_target_pairs={{0,24},{4,28},{8,0},{12,4},{16,8},{20,12},{24,16},{28,20},{32,56},... | collective-permute-start | bytes 1179656 | tf_op jit(solution)/shard_map/ppermute | solution.py:705
  17.4 7.4 %shard_map.104 = (bf16[512,1536]{1,0:T(8,128)(2,1)}, bf16[512,768]{1,0:T(8,128)(2,1)}, bf16[512,768]{1,0:T(8,128)(2,1)}, bf16[2,2,128,768]{3,2,1,0:T(8,128)(2,1)...) custom-call(s32[2]{0:T(128)} %pad_add_fusion.ids, s32[4,4,2]{2,1,0:T(4,128)} %copy.18.index, ...), custom_call_target="tpu_custom_call" | custom-call | flops 2415919104 | bytes 12582912 | tf_op jit(solution)/shard_map/pallas_call | solution.py:133
  26.2 2.6 %collective-permute-start.8 = (bf16[2,2,128,768]{3,2,1,0:T(8,128)(2,1)}, bf16[2,2,128,768]{3,2,1,0:T(8,128)(2,1)}, u32[]{:S(2)}, u32[]{:S(2)}) collective-permute-start(bf16[2,2,128,768]{3,2,1,0:T(8,128)(2,1)} %get-tuple-element.48), channel_id=1, source_target_pairs={{0,2},{1,3},{2,0},{3,1},{4,6},{5,7},{6,4},{7,5},{8,10},{9,11},{10,... | collective-permute-start | bytes 2359304 | tf_op jit(solution)/shard_map/ppermute | solution.py:705
  30.0 7.3 %collective-permute-done.3.held_1 = bf16[4,32,1536]{2,1,0:T(8,128)(2,1)S(1)} collective-permute-done((bf16[4,32,1536]{2,1,0:T(8,128)(2,1)S(1)}, bf16[4,32,1536]{2,1,0:T(8,128)(2,1)S(1)}, u32[]{:S(2)}, u32[]{:S(2)}) %collective-permute-start.3) | collective-permute-done | bytes 393248 | tf_op jit(solution)/shard_map/ppermute | solution.py:705
  44.1 4.0 %shard_map.105 = (bf16[512,768]{1,0:T(8,128)(2,1)S(1)}, bf16[512,768]{1,0:T(8,128)(2,1)S(1)}) custom-call(bf16[512,1536]{1,0:T(8,128)(2,1)S(1)} %copy-done.11, bf16[512,1536]{1,0:T(8,128)(2,1)S(1)} %bitcast.18, bf16[1536,768]{1,0:T(8,128)(2,1)S(1)} %copy-done.6, bf16[768,1536]{1,0:T(8,128)(2,1)S(1)} %copy-done.8), custom_call_target="tpu_custom_call" | custom-call | flops 2415919104 | bytes 10485760 | tf_op jit(solution)/shard_map/pallas_call | solution.py:166
  48.1 4.0 %shard_map.107 = (bf16[128,768]{1,0:T(8,128)(2,1)S(1)}, bf16[128,768]{1,0:T(8,128)(2,1)S(1)}) custom-call(s32[2]{0:T(128)S(1)} %copy-done.4, s32[32,4]{1,0:T(8,128)S(1)} %copy.22.offsets, bf16[4,32,1536]{2,1,0:T(8,128)(2,1)S(1)} %pad_maximum_fusion.held_0, bf16[4,32,1536]{2,1,0:T(8,128)(2,1)S(1)} %collective-permute-done.3.held_1, ...), custom_call_target="tpu_custom_call" | custom-call | flops 603979776 | bytes 6291456 | tf_op jit(solution)/shard_map/pallas_call | solution.py:275
  52.2 9.1 %collective-permute-done.8.rest_1_ = bf16[2,2,128,768]{3,2,1,0:T(8,128)(2,1)} collective-permute-done((bf16[2,2,128,768]{3,2,1,0:T(8,128)(2,1)}, bf16[2,2,128,768]{3,2,1,0:T(8,128)(2,1)}, u32[]{:S(2)}, u32[]{:S(2)}) %collective-permute-start.8) | collective-permute-done | bytes 786464 | tf_op jit(solution)/shard_map/ppermute | solution.py:705
  62.5 16.8 %shard_map.109 = (bf16[512,384]{1,0:T(8,128)(2,1)S(1)}, bf16[512,384]{1,0:T(8,128)(2,1)S(1)}, f32[512,384]{1,0:T(8,128)S(1)}, f32[512,384]{1,0:T(8,128)S(1)}, f3...) custom-call(s32[2]{0:T(128)S(1)} %copy-done.4, ...), custom_call_target="tpu_custom_call" | custom-call | flops 10871635968 | bytes 9437184 | tf_op jit(solution)/shard_map/pallas_call | solution.py:472
  79.3 2.1 %collective-permute-start.17 = (bf16[2,128,384]{2,1,0:T(8,128)(2,1)S(1)}, bf16[2,128,384]{2,1,0:T(8,128)(2,1)S(1)}, u32[]{:S(2)}, u32[]{:S(2)}) collective-permute-start(bf16[2,128,384]{2,1,0:T(8,128)(2,1)S(1)} %get-tuple-element.68), channel_id=1, source_target_pairs={{0,4},{4,0},{8,12},{12,8},{16,20},{20,16},{24,28},{28,24},{32,36},... | collective-permute-start | bytes 589832 | tf_op jit(solution)/shard_map/ppermute | solution.py:705
  81.4 16.8 %shard_map.108 = (bf16[512,384]{1,0:T(8,128)(2,1)S(1)}, bf16[512,384]{1,0:T(8,128)(2,1)S(1)}, f32[512,384]{1,0:T(8,128)S(1)}, f32[512,384]{1,0:T(8,128)S(1)}, f3...) custom-call(s32[2]{0:T(128)S(1)} %copy-done.4, ...), custom_call_target="tpu_custom_call" | custom-call | flops 10871635968 | bytes 9437184 | tf_op jit(solution)/shard_map/pallas_call | solution.py:472
  98.4 1.9 %collective-permute-start.13 = (bf16[2,2,128,384]{3,2,1,0:T(8,128)(2,1)S(1)}, bf16[2,2,128,384]{3,2,1,0:T(8,128)(2,1)S(1)}, u32[]{:S(2)}, u32[]{:S(2)}) collective-permute-start(bf16[2,2,128,384]{3,2,1,0:T(8,128)(2,1)S(1)} %get-tuple-element.62), channel_id=1, source_target_pairs={{0,3},{1,0},{2,1},{3,2},{4,7},{5,4},{6,5},{7,6},{8,11},{9,8},{10,9... | collective-permute-start | bytes 1179656 | tf_op jit(solution)/shard_map/ppermute | solution.py:705
  103.5 1.7 %collective-permute-start.19 = (bf16[4,2,32,768]{3,2,1,0:T(8,128)(2,1)S(1)}, bf16[4,2,32,768]{3,2,1,0:T(8,128)(2,1)S(1)}, u32[]{:S(2)}, u32[]{:S(2)}) collective-permute-start(bf16[4,2,32,768]{3,2,1,0:T(8,128)(2,1)S(1)} %get-tuple-element.71), channel_id=1, source_target_pairs={{0,16},{4,20},{8,24},{12,28},{16,0},{20,4},{24,8},{28,12},{32,48},... | collective-permute-start | bytes 1179656 | tf_op jit(solution)/shard_map/ppermute | solution.py:705
  106.0 1.7 %collective-permute-start.14 = (bf16[2,2,128,384]{3,2,1,0:T(8,128)(2,1)S(1)}, bf16[2,2,128,384]{3,2,1,0:T(8,128)(2,1)S(1)}, u32[]{:S(2)}, u32[]{:S(2)}) collective-permute-start(bf16[2,2,128,384]{3,2,1,0:T(8,128)(2,1)S(1)} %get-tuple-element.63), channel_id=1, source_target_pairs={{0,2},{1,3},{2,0},{3,1},{4,6},{5,7},{6,4},{7,5},{8,10},{9,11},{10,... | collective-permute-start | bytes 1179656 | tf_op jit(solution)/shard_map/ppermute | solution.py:705
  109.6 3.5 %collective-permute-done.18.part_1 = bf16[4,2,32,768]{3,2,1,0:T(8,128)(2,1)S(1)} collective-permute-done((bf16[4,2,32,768]{3,2,1,0:T(8,128)(2,1)S(1)}, bf16[4,2,32,768]{3,2,1,0:T(8,128)(2,1)S(1)}, u32[]{:S(2)}, u32[]{:S(2)}) %collective-permute-start.18) | collective-permute-done | bytes 393248 | tf_op jit(solution)/shard_map/ppermute | solution.py:705
  113.0 1.9 %collective-permute-start.10 = (bf16[2,2,128,384]{3,2,1,0:T(8,128)(2,1)S(1)}, bf16[2,2,128,384]{3,2,1,0:T(8,128)(2,1)S(1)}, u32[]{:S(2)}, u32[]{:S(2)}) collective-permute-start(bf16[2,2,128,384]{3,2,1,0:T(8,128)(2,1)S(1)} %get-tuple-element.59), channel_id=1, source_target_pairs={{0,3},{1,0},{2,1},{3,2},{4,7},{5,4},{6,5},{7,6},{8,11},{9,8},{10,9... | collective-permute-start | bytes 1179656 | tf_op jit(solution)/shard_map/ppermute | solution.py:705
  115.0 7.1 %collective-permute-done.19.part_2 = bf16[4,2,32,768]{3,2,1,0:T(8,128)(2,1)S(1)} collective-permute-done((bf16[4,2,32,768]{3,2,1,0:T(8,128)(2,1)S(1)}, bf16[4,2,32,768]{3,2,1,0:T(8,128)(2,1)S(1)}, u32[]{:S(2)}, u32[]{:S(2)}) %collective-permute-start.19) | collective-permute-done | bytes 393248 | tf_op jit(solution)/shard_map/ppermute | solution.py:705
  122.1 2.3 %collective-permute-start.11 = (bf16[2,2,128,384]{3,2,1,0:T(8,128)(2,1)S(1)}, bf16[2,2,128,384]{3,2,1,0:T(8,128)(2,1)S(1)}, u32[]{:S(2)}, u32[]{:S(2)}) collective-permute-start(bf16[2,2,128,384]{3,2,1,0:T(8,128)(2,1)S(1)} %get-tuple-element.60), channel_id=1, source_target_pairs={{0,2},{1,3},{2,0},{3,1},{4,6},{5,7},{6,4},{7,5},{8,10},{9,11},{10,... | collective-permute-start | bytes 1179656 | tf_op jit(solution)/shard_map/ppermute | solution.py:705
  125.7 2.8 %collective-permute-start.22 = (bf16[2,32,768]{2,1,0:T(8,128)(2,1)S(1)}, bf16[2,32,768]{2,1,0:T(8,128)(2,1)S(1)}, u32[]{:S(2)}, u32[]{:S(2)}) collective-permute-start(bf16[2,32,768]{2,1,0:T(8,128)(2,1)S(1)} %get-tuple-element.75), channel_id=1, source_target_pairs={{0,64},{4,68},{8,72},{12,76},{16,80},{20,84},{24,88},{28,92},{32,9... | collective-permute-start | bytes 294920 | tf_op jit(solution)/shard_map/ppermute | solution.py:705
  129.1 4.3 %shard_map.110 = (bf16[512,1536]{1,0:T(8,128)(2,1)}, f32[512,1536]{1,0:T(8,128)S(1)}) custom-call(bf16[512,384]{1,0:T(8,128)(2,1)S(1)} %get-tuple-element.50.refs_0_, bf16[512,384]{1,0:T(8,128)(2,1)S(1)} %get-tuple-element.51.refs_1_, bf16[512,384]{1,0:T(8,128)(2,1)S(1)} %get-tuple-element.52.refs_2_, bf16[512,384]{1,0:T(8,128)(2,1)S(1)} %get-tuple-element.53.refs_3_, ...), custom_call_target="tpu_custom_call" | custom-call | flops 2415919104 | bytes 11534336 | tf_op jit(solution)/shard_map/pallas_call | solution.py:572
  134.8 9.4 %collective-permute-done.12.refs_6_ = bf16[2,2,128,384]{3,2,1,0:T(8,128)(2,1)S(1)} collective-permute-done((bf16[2,2,128,384]{3,2,1,0:T(8,128)(2,1)S(1)}, bf16[2,2,128,384]{3,2,1,0:T(8,128)(2,1)S(1)}, u32[]{:S(2)}, u32[]{:S(2)}) %collective-permute-start.12) | collective-permute-done | bytes 393248 | tf_op jit(solution)/shard_map/ppermute | solution.py:705
  144.2 7.8 %shard_map.113 = bf16[512,1536]{1,0:T(8,128)(2,1)} custom-call(s32[2]{0:T(128)S(1)} %copy-done.4, s32[4,4]{1,0:T(4,128)S(1)} %copy-done.5, s32[4,4,2]{2,1,0:T(4,128)S(1)} %copy-done.3, f32[512,384]{1,0:T(8,128)S(1)} %get-tuple-element.55.refs_0_, f32[512,384]{1,0:T(8,128)S(1)} %get-tuple-element.56.refs_1_, f32[512,384]{1,0:T(8,128)S(1)} %get-tuple-element.57.refs_2_, ...), custom_call_target="tpu_custom_call" | custom-call | flops 2415919104 | bytes 16777216 | tf_op jit(solution)/shard_map/pallas_call | solution.py:675
  (70 shorter events, 25.4 us)
Async XLA Ops:
  1.9 7.2 %collective-permute-start.1 = (bf16[32,1536]{1,0:T(8,128)(2,1)S(1)}, bf16[32,1536]{1,0:T(8,128)(2,1)S(1)}, u32[]{:S(2)}, u32[]{:S(2)}) collective-permute-start(bf16[32,1536]{1,0:T(8,128)(2,1)S(1)} %bitcast.20), channel_id=1, source_target_pairs={{0,64},{4,68},{8,72},{12,76},{16,80},{20,84},{24,88},{28,92},{32,9... | collective-permute-start | bytes 294920 | tf_op jit(solution)/shard_map/ppermute | solution.py:705
  6.4 4.7 %collective-permute-start = (bf16[32,1536]{1,0:T(8,128)(2,1)S(1)}, bf16[32,1536]{1,0:T(8,128)(2,1)S(1)}, u32[]{:S(2)}, u32[]{:S(2)}) collective-permute-start(bf16[32,1536]{1,0:T(8,128)(2,1)S(1)} %bitcast.21), channel_id=1, source_target_pairs={{0,32},{4,36},{8,40},{12,44},{16,48},{20,52},{24,56},{28,60},{32,6... | collective-permute-start | bytes 294920 | tf_op jit(solution)/shard_map/ppermute | solution.py:705
  7.1 4.6 %collective-permute-start.2 = (bf16[32,1536]{1,0:T(8,128)(2,1)S(1)}, bf16[32,1536]{1,0:T(8,128)(2,1)S(1)}, u32[]{:S(2)}, u32[]{:S(2)}) collective-permute-start(bf16[32,1536]{1,0:T(8,128)(2,1)S(1)} %bitcast.22), channel_id=1, source_target_pairs={{0,96},{4,100},{8,104},{12,108},{16,112},{20,116},{24,120},{28,124... | collective-permute-start | bytes 294920 | tf_op jit(solution)/shard_map/ppermute | solution.py:705
  11.7 17.1 %collective-permute-start.5 = (bf16[4,32,1536]{2,1,0:T(8,128)(2,1)S(1)}, bf16[4,32,1536]{2,1,0:T(8,128)(2,1)S(1)}, u32[]{:S(2)}, u32[]{:S(2)}) collective-permute-start(bf16[4,32,1536]{2,1,0:T(8,128)(2,1)S(1)} %pad_maximum_fusion.held_0), channel_id=1, source_target_pairs={{0,24},{4,28},{8,0},{12,4},{16,8},{20,12},{24,16},{28,20},{32,56},... | collective-permute-start | bytes 1179656 | tf_op jit(solution)/shard_map/ppermute | solution.py:705
  16.3 13.7 %collective-permute-start.4 = (bf16[4,32,1536]{2,1,0:T(8,128)(2,1)S(1)}, bf16[4,32,1536]{2,1,0:T(8,128)(2,1)S(1)}, u32[]{:S(2)}, u32[]{:S(2)}) collective-permute-start(bf16[4,32,1536]{2,1,0:T(8,128)(2,1)S(1)} %pad_maximum_fusion.held_0), channel_id=1, source_target_pairs={{0,16},{4,20},{8,24},{12,28},{16,0},{20,4},{24,8},{28,12},{32,48},... | collective-permute-start | bytes 1179656 | tf_op jit(solution)/shard_map/ppermute | solution.py:705
  16.8 20.6 %collective-permute-start.3 = (bf16[4,32,1536]{2,1,0:T(8,128)(2,1)S(1)}, bf16[4,32,1536]{2,1,0:T(8,128)(2,1)S(1)}, u32[]{:S(2)}, u32[]{:S(2)}) collective-permute-start(bf16[4,32,1536]{2,1,0:T(8,128)(2,1)S(1)} %pad_maximum_fusion.held_0), channel_id=1, source_target_pairs={{0,8},{4,12},{8,16},{12,20},{16,24},{20,28},{24,0},{28,4},{32,40},... | collective-permute-start | bytes 1179656 | tf_op jit(solution)/shard_map/ppermute | solution.py:705
  24.8 27.3 %collective-permute-start.7 = (bf16[2,2,128,768]{3,2,1,0:T(8,128)(2,1)}, bf16[2,2,128,768]{3,2,1,0:T(8,128)(2,1)}, u32[]{:S(2)}, u32[]{:S(2)}) collective-permute-start(bf16[2,2,128,768]{3,2,1,0:T(8,128)(2,1)} %get-tuple-element.47), channel_id=1, source_target_pairs={{0,1},{1,2},{2,3},{3,0},{4,5},{5,6},{6,7},{7,4},{8,9},{9,10},{10,1... | collective-permute-start | bytes 2359304 | tf_op jit(solution)/shard_map/ppermute | solution.py:705
  26.2 35.1 %collective-permute-start.8 = (bf16[2,2,128,768]{3,2,1,0:T(8,128)(2,1)}, bf16[2,2,128,768]{3,2,1,0:T(8,128)(2,1)}, u32[]{:S(2)}, u32[]{:S(2)}) collective-permute-start(bf16[2,2,128,768]{3,2,1,0:T(8,128)(2,1)} %get-tuple-element.48), channel_id=1, source_target_pairs={{0,2},{1,3},{2,0},{3,1},{4,6},{5,7},{6,4},{7,5},{8,10},{9,11},{10,... | collective-permute-start | bytes 2359304 | tf_op jit(solution)/shard_map/ppermute | solution.py:705
  28.8 33.6 %collective-permute-start.9 = (bf16[2,2,128,768]{3,2,1,0:T(8,128)(2,1)}, bf16[2,2,128,768]{3,2,1,0:T(8,128)(2,1)}, u32[]{:S(2)}, u32[]{:S(2)}) collective-permute-start(bf16[2,2,128,768]{3,2,1,0:T(8,128)(2,1)} %get-tuple-element.49), channel_id=1, source_target_pairs={{0,3},{1,0},{2,1},{3,2},{4,7},{5,4},{6,5},{7,6},{8,11},{9,8},{10,9... | collective-permute-start | bytes 2359304 | tf_op jit(solution)/shard_map/ppermute | solution.py:705
  38.4 9.7 %collective-permute-start.6 = (bf16[4,32,1536]{2,1,0:T(8,128)(2,1)S(1)}, bf16[4,32,1536]{2,1,0:T(8,128)(2,1)S(1)}, u32[]{:S(2)}, u32[]{:S(2)}) collective-permute-start(bf16[4,32,1536]{2,1,0:T(8,128)(2,1)S(1)} %shard_map.106), channel_id=1, source_target_pairs={{0,4},{4,0},{8,12},{12,8},{16,20},{20,16},{24,28},{28,24},{32,36},... | collective-permute-start | bytes 1179656 | tf_op jit(solution)/shard_map/ppermute | solution.py:705
  79.3 21.0 %collective-permute-start.17 = (bf16[2,128,384]{2,1,0:T(8,128)(2,1)S(1)}, bf16[2,128,384]{2,1,0:T(8,128)(2,1)S(1)}, u32[]{:S(2)}, u32[]{:S(2)}) collective-permute-start(bf16[2,128,384]{2,1,0:T(8,128)(2,1)S(1)} %get-tuple-element.68), channel_id=1, source_target_pairs={{0,4},{4,0},{8,12},{12,8},{16,20},{20,16},{24,28},{28,24},{32,36},... | collective-permute-start | bytes 589832 | tf_op jit(solution)/shard_map/ppermute | solution.py:705
  98.3 2.0 %collective-permute-start.16 = (bf16[2,128,384]{2,1,0:T(8,128)(2,1)S(1)}, bf16[2,128,384]{2,1,0:T(8,128)(2,1)S(1)}, u32[]{:S(2)}, u32[]{:S(2)}) collective-permute-start(bf16[2,128,384]{2,1,0:T(8,128)(2,1)S(1)} %get-tuple-element.67), channel_id=1, source_target_pairs={{0,4},{4,0},{8,12},{12,8},{16,20},{20,16},{24,28},{28,24},{32,36},... | collective-permute-start | bytes 589832 | tf_op jit(solution)/shard_map/ppermute | solution.py:705
  98.4 10.3 %collective-permute-start.13 = (bf16[2,2,128,384]{3,2,1,0:T(8,128)(2,1)S(1)}, bf16[2,2,128,384]{3,2,1,0:T(8,128)(2,1)S(1)}, u32[]{:S(2)}, u32[]{:S(2)}) collective-permute-start(bf16[2,2,128,384]{3,2,1,0:T(8,128)(2,1)S(1)} %get-tuple-element.62), channel_id=1, source_target_pairs={{0,3},{1,0},{2,1},{3,2},{4,7},{5,4},{6,5},{7,6},{8,11},{9,8},{10,9... | collective-permute-start | bytes 1179656 | tf_op jit(solution)/shard_map/ppermute | solution.py:705
  101.9 11.2 %collective-permute-start.18 = (bf16[4,2,32,768]{3,2,1,0:T(8,128)(2,1)S(1)}, bf16[4,2,32,768]{3,2,1,0:T(8,128)(2,1)S(1)}, u32[]{:S(2)}, u32[]{:S(2)}) collective-permute-start(bf16[4,2,32,768]{3,2,1,0:T(8,128)(2,1)S(1)} %get-tuple-element.70), channel_id=1, source_target_pairs={{0,8},{4,12},{8,16},{12,20},{16,24},{20,28},{24,0},{28,4},{32,40},... | collective-permute-start | bytes 1179656 | tf_op jit(solution)/shard_map/ppermute | solution.py:705
  103.5 18.5 %collective-permute-start.19 = (bf16[4,2,32,768]{3,2,1,0:T(8,128)(2,1)S(1)}, bf16[4,2,32,768]{3,2,1,0:T(8,128)(2,1)S(1)}, u32[]{:S(2)}, u32[]{:S(2)}) collective-permute-start(bf16[4,2,32,768]{3,2,1,0:T(8,128)(2,1)S(1)} %get-tuple-element.71), channel_id=1, source_target_pairs={{0,16},{4,20},{8,24},{12,28},{16,0},{20,4},{24,8},{28,12},{32,48},... | collective-permute-start | bytes 1179656 | tf_op jit(solution)/shard_map/ppermute | solution.py:705
  105.2 19.1 %collective-permute-start.20 = (bf16[4,2,32,768]{3,2,1,0:T(8,128)(2,1)S(1)}, bf16[4,2,32,768]{3,2,1,0:T(8,128)(2,1)S(1)}, u32[]{:S(2)}, u32[]{:S(2)}) collective-permute-start(bf16[4,2,32,768]{3,2,1,0:T(8,128)(2,1)S(1)} %get-tuple-element.72), channel_id=1, source_target_pairs={{0,24},{4,28},{8,0},{12,4},{16,8},{20,12},{24,16},{28,20},{32,56},... | collective-permute-start | bytes 1179656 | tf_op jit(solution)/shard_map/ppermute | solution.py:705
  106.0 18.8 %collective-permute-start.14 = (bf16[2,2,128,384]{3,2,1,0:T(8,128)(2,1)S(1)}, bf16[2,2,128,384]{3,2,1,0:T(8,128)(2,1)S(1)}, u32[]{:S(2)}, u32[]{:S(2)}) collective-permute-start(bf16[2,2,128,384]{3,2,1,0:T(8,128)(2,1)S(1)} %get-tuple-element.63), channel_id=1, source_target_pairs={{0,2},{1,3},{2,0},{3,1},{4,6},{5,7},{6,4},{7,5},{8,10},{9,11},{10,... | collective-permute-start | bytes 1179656 | tf_op jit(solution)/shard_map/ppermute | solution.py:705
  108.7 17.0 %collective-permute-start.15 = (bf16[2,2,128,384]{3,2,1,0:T(8,128)(2,1)S(1)}, bf16[2,2,128,384]{3,2,1,0:T(8,128)(2,1)S(1)}, u32[]{:S(2)}, u32[]{:S(2)}) collective-permute-start(bf16[2,2,128,384]{3,2,1,0:T(8,128)(2,1)S(1)} %get-tuple-element.64), channel_id=1, source_target_pairs={{0,1},{1,2},{2,3},{3,0},{4,5},{5,6},{6,7},{7,4},{8,9},{9,10},{10,1... | collective-permute-start | bytes 1179656 | tf_op jit(solution)/shard_map/ppermute | solution.py:705
  113.0 15.5 %collective-permute-start.10 = (bf16[2,2,128,384]{3,2,1,0:T(8,128)(2,1)S(1)}, bf16[2,2,128,384]{3,2,1,0:T(8,128)(2,1)S(1)}, u32[]{:S(2)}, u32[]{:S(2)}) collective-permute-start(bf16[2,2,128,384]{3,2,1,0:T(8,128)(2,1)S(1)} %get-tuple-element.59), channel_id=1, source_target_pairs={{0,3},{1,0},{2,1},{3,2},{4,7},{5,4},{6,5},{7,6},{8,11},{9,8},{10,9... | collective-permute-start | bytes 1179656 | tf_op jit(solution)/shard_map/ppermute | solution.py:705
  122.1 12.7 %collective-permute-start.11 = (bf16[2,2,128,384]{3,2,1,0:T(8,128)(2,1)S(1)}, bf16[2,2,128,384]{3,2,1,0:T(8,128)(2,1)S(1)}, u32[]{:S(2)}, u32[]{:S(2)}) collective-permute-start(bf16[2,2,128,384]{3,2,1,0:T(8,128)(2,1)S(1)} %get-tuple-element.60), channel_id=1, source_target_pairs={{0,2},{1,3},{2,0},{3,1},{4,6},{5,7},{6,4},{7,5},{8,10},{9,11},{10,... | collective-permute-start | bytes 1179656 | tf_op jit(solution)/shard_map/ppermute | solution.py:705
  124.4 19.8 %collective-permute-start.12 = (bf16[2,2,128,384]{3,2,1,0:T(8,128)(2,1)S(1)}, bf16[2,2,128,384]{3,2,1,0:T(8,128)(2,1)S(1)}, u32[]{:S(2)}, u32[]{:S(2)}) collective-permute-start(bf16[2,2,128,384]{3,2,1,0:T(8,128)(2,1)S(1)} %get-tuple-element.61), channel_id=1, source_target_pairs={{0,1},{1,2},{2,3},{3,0},{4,5},{5,6},{6,7},{7,4},{8,9},{9,10},{10,1... | collective-permute-start | bytes 1179656 | tf_op jit(solution)/shard_map/ppermute | solution.py:705
  124.8 19.4 %collective-permute-start.21 = (bf16[2,32,768]{2,1,0:T(8,128)(2,1)S(1)}, bf16[2,32,768]{2,1,0:T(8,128)(2,1)S(1)}, u32[]{:S(2)}, u32[]{:S(2)}) collective-permute-start(bf16[2,32,768]{2,1,0:T(8,128)(2,1)S(1)} %get-tuple-element.74), channel_id=1, source_target_pairs={{0,32},{4,36},{8,40},{12,44},{16,48},{20,52},{24,56},{28,60},{32,6... | collective-permute-start | bytes 294920 | tf_op jit(solution)/shard_map/ppermute | solution.py:705
  125.7 18.4 %collective-permute-start.22 = (bf16[2,32,768]{2,1,0:T(8,128)(2,1)S(1)}, bf16[2,32,768]{2,1,0:T(8,128)(2,1)S(1)}, u32[]{:S(2)}, u32[]{:S(2)}) collective-permute-start(bf16[2,32,768]{2,1,0:T(8,128)(2,1)S(1)} %get-tuple-element.75), channel_id=1, source_target_pairs={{0,64},{4,68},{8,72},{12,76},{16,80},{20,84},{24,88},{28,92},{32,9... | collective-permute-start | bytes 294920 | tf_op jit(solution)/shard_map/ppermute | solution.py:705
  128.5 15.6 %collective-permute-start.23 = (bf16[2,32,768]{2,1,0:T(8,128)(2,1)S(1)}, bf16[2,32,768]{2,1,0:T(8,128)(2,1)S(1)}, u32[]{:S(2)}, u32[]{:S(2)}) collective-permute-start(bf16[2,32,768]{2,1,0:T(8,128)(2,1)S(1)} %get-tuple-element.76), channel_id=1, source_target_pairs={{0,96},{4,100},{8,104},{12,108},{16,112},{20,116},{24,120},{28,124... | collective-permute-start | bytes 294920 | tf_op jit(solution)/shard_map/ppermute | solution.py:705
  (15 other events, 218.9 us)

commit v2 on v1

--- a/solution.py
+++ b/solution.py
@@ -24,7 +24,7 @@
 EPS = 1e-05
 MASKED = -1e30
 NT = (((1,), (1,)), ((), ()))
-GROUPS = ((0, 3), (3, 3))
+GROUPS = ((0, 4), (4, 2))
 
 
 def dot(left, right):
@@ -105,7 +105,7 @@
     def publish(kind, out):
         for shift in (1, 2, 3):
             for slot in range(2):
-                strip = index[camera, lax.rem(camera + shift, 4), slot]
+                strip = index[camera, slot, lax.rem(camera + shift, 4)]
                 at = pl.ds(pl.multiple_of(strip * STRIP, STRIP), STRIP)
                 sem = send_sem.at[kind * SLOTS + 2 * (shift - 1) + slot]
                 store(made.at[kind, at], sends[shift - 1].at[kind, slot], sem)
@@ -186,7 +186,7 @@
 
 
 def source_of(offsets, frame, read):
-    source = frame - offsets[frame, read]
+    source = frame - offsets[read, frame]
     return jnp.maximum(source, 0), source >= 0
 
 
@@ -355,7 +355,7 @@
     pieces = [(0, ROWS, None)]
     for read in range(READS):
         start = MEM_AT + read * MEM
-        pieces.append((start, start + MEM, offsets[frame, read] <= frame))
+        pieces.append((start, start + MEM, offsets[read, frame] <= frame))
     for place in range(LIVE_MAX):
         start = FAR_AT + place * STRIP
         pieces.append((start, start + STRIP, place < live_total))
@@ -490,15 +490,13 @@
     )(ids, offsets, count, queries, grads, keys_own, values_own, keys_mem, values_mem, *far)
 
 
-def sort_kernel(ids, offsets, *rest):
-    count = len(GROUPS)
-    own, given = rest[:count], rest[count : 2 * count]
-    outs, total = rest[2 * count : 2 * count + 4], rest[2 * count + 4]
+def sort_kernel(ids, offsets, own, given, out_0, out_1, out_2, out_3, total):
+    outs = (out_0, out_1, out_2, out_3)
     frame = ids[1]
     z_here, x_here, core_here = parts_of(frame)
     partner = frame + 1 - 2 * core_here
     total[...] = jnp.zeros_like(total)
-    for reader, arrays in ((frame, own), (partner, given)):
+    for reader, part in ((frame, own), (partner, given)):
         for read in range(READS):
             source, live = source_of(offsets, reader, read)
             z_at, x_at, core_at = parts_of(source)
@@ -506,36 +504,38 @@
 
             @pl.when(jnp.logical_and(live, core_at == core_here))
             def _():
-                for (first, pairs), part in zip(GROUPS, arrays):
-                    cols = slice(first * PAIR, (first + pairs) * PAIR)
-                    for kind in range(2):
-                        added = part[kind, read * MEM : (read + 1) * MEM, :].astype(WIDE)
-                        total[to, kind, :, cols] = total[to, kind, :, cols] + added
+                for kind in range(2):
+                    added = part[kind, read * MEM : (read + 1) * MEM, :].astype(WIDE)
+                    total[to, kind] = total[to, kind] + added
 
     for shift in range(4):
         outs[shift][...] = total[4 * shift : 4 * shift + 4].astype(LOW)
 
 
 def sort_reads(ids, offsets, own, given):
-    shapes = [(2, READS * MEM, pairs * PAIR) for _, pairs in GROUPS]
+    width = own.shape[2]
+    shape = (4, 2, MEM, width)
     return call(
         sort_kernel,
         1,
         2,
-        [whole(s) for s in shapes] * 2,
-        [whole((4, 2, MEM, INNER))] * 4,
-        [array((4, 2, MEM, INNER), LOW)] * 4,
-        [pltpu.VMEM((16, 2, MEM, INNER), WIDE)],
+        [whole(own.shape)] * 2,
+        [whole(shape)] * 4,
+        [array(shape, LOW)] * 4,
+        [pltpu.VMEM((16, 2, MEM, width), WIDE)],
         0,
-        3 << 20,
-    )(ids, offsets, *own, *given)
-
-
-def add_kernel(part_0, part_1, part_2, part_3, *outs):
-    for shift in range(4):
-        total = part_0[shift].astype(WIDE) + part_1[shift].astype(WIDE)
-        total = total + part_2[shift].astype(WIDE) + part_3[shift].astype(WIDE)
-        outs[shift][...] = total.astype(LOW)
+        2 << 20,
+        vmem=12,
+    )(ids, offsets, own, given)
+
+
+def add_kernel(*refs):
+    for group, (first, pairs) in enumerate(GROUPS):
+        parts, cols = refs[4 * group : 4 * group + 4], slice(first * PAIR, (first + pairs) * PAIR)
+        for shift in range(4):
+            total = parts[0][shift].astype(WIDE) + parts[1][shift].astype(WIDE)
+            total = total + parts[2][shift].astype(WIDE) + parts[3][shift].astype(WIDE)
+            refs[4 * len(GROUPS) + shift][:, :, cols] = total.astype(LOW)
 
 
 def add_reads(parts):
@@ -543,12 +543,13 @@
         add_kernel,
         1,
         0,
-        [whole((4, 2, MEM, INNER))] * 4,
+        [whole(part.shape) for part in parts],
         [whole((2, MEM, INNER))] * 4,
         [array((2, MEM, INNER), LOW)] * 4,
         [],
         0,
         2 << 20,
+        vmem=8,
     )(*parts)
 
 
@@ -627,7 +628,7 @@
 
             @pl.when(slot < count[camera, other])
             def _():
-                start = index[camera, other, slot] * STRIP
+                start = index[camera, slot, other] * STRIP
                 at = pl.ds(pl.multiple_of(start, STRIP), STRIP)
                 for kind in range(2):
                     total[kind, at, :] = total[kind, at, :] + far[shift - 1, kind, slot].astype(WIDE)
@@ -709,27 +710,28 @@
     tokens = tokens.reshape(ROWS, MODEL)
     grad_update = grad_update.reshape(ROWS, MODEL)
     ids = jnp.stack([lax.axis_index("cam"), lax.axis_index("tm")]).astype(jnp.int32)
+    index, offsets = jnp.transpose(index, (0, 2, 1)), offsets.T
     others = (1, 2, 3)
 
+    low, keys, values, *sends = project_keys(ids, index, tokens, w_key, w_value)
+    far = [send(sends[k - 1], "cam", shift_cam(k)) for k in others]
     kept = tokens.reshape(MEM, ROWS // MEM, MODEL)[:, 0]
     along_z = jnp.stack([kept] + [send(kept, "tm", shift_z(k)) for k in others])
-    low, keys, values, *sends = project_keys(ids, index, tokens, w_key, w_value)
-    far = [send(sends[k - 1], "cam", shift_cam(k)) for k in others]
     held = [along_z] + [send(along_z, "tm", shift_x(k)) for k in others]
     queries, grads = project_queries(low, grad_update, w_query, w_out)
     given = send(pick(ids, offsets, held), "tm", SWAP_CORE)
     keys_mem, values_mem = project_memory(ids, offsets, held, given, w_key, w_value)
 
-    made, mem_given, back = [], [], []
+    made, back, parts = [], [], []
     for group in GROUPS:
         args = (queries, grads, keys, values, keys_mem, values_mem, far)
         made.append(attention(group, ids, offsets, count, *args))
-        mem_given.append(send(made[-1][5], "tm", SWAP_CORE))
         back += [send(made[-1][5 + k], "cam", shift_cam(-k)) for k in others]
-    mixed, grad_query, own_keys, own_values, mem = [[m[k] for m in made] for k in range(5)]
-
-    sorted_x = sort_reads(ids, offsets, mem, mem_given)
-    parts = [sorted_x[0]] + [send(sorted_x[k], "tm", shift_x(k)) for k in others]
+        mem_given = send(made[-1][5], "tm", SWAP_CORE)
+        to_x = sort_reads(ids, offsets, made[-1][4], mem_given)
+        parts += [to_x[0]] + [send(to_x[k], "tm", shift_x(k)) for k in others]
+    mixed, grad_query, own_keys, own_values = [[m[k] for m in made] for k in range(4)]
+
     update, grad_part = outward(mixed, grad_query, w_out, w_query)
     sorted_z = add_reads(parts)
     kept_grads = [sorted_z[0]] + [send(sorted_z[k], "tm", shift_z(k)) for k in others]

time: 152 us -> 164 us (1.079); the launches traced: 152 us -> 161 us
  waiting for transfers between devices: 42.6 us -> 53.1 us
  Pallas kernels: 64 us -> 61.4 us
  starting transfers between devices: 36.5 us -> 38.7 us
  local copies, waits for them, and re-layouts: 7.5 us -> 5.78 us
    ppermute x24 -> x27, waiting for transfers between devices: 42.6 us -> 53.1 us  [send(): return lax.ppermute(value, axis, pairs)]
    ppermute x24 -> x27, starting transfers between devices: 36.5 us -> 38.7 us  [send(): return lax.ppermute(value, axis, pairs)]
    unnamed x33 -> x29, local copies, waits for them, and re-layouts: 6.26 us -> 4.54 us
    pallas_call x2, Pallas kernels: 33.7 us -> 32 us  [attention(): call(attention_kernel, pairs, 3, [taken(ROWS)] * 4 + [taken(READS * MEM)]...]
  transfers between devices with their start and end apart: 24 -> 27, of which waited for: 10 -> 11; matrix products, arithmetic and copies ran while one was open for 1% -> 0% of each run, Pallas kernels for 26% -> 20%
where the time goes in v2:
time: 164 us; the launch traced here: 161 us
  Pallas kernels  61.4 us (37%)
  waiting for transfers between devices  53.1 us (32%)
  starting transfers between devices  38.7 us (24%)
  local copies, waits for them, and re-layouts  5.78 us (4%)
    ppermute x27, waiting for transfers between devices, send(): return lax.ppermute(value, axis, pairs)  53.1 us
    ppermute x27, starting transfers between devices, send(): return lax.ppermute(value, axis, pairs)  38.7 us
    pallas_call x2, Pallas kernels, attention(): call(attention_kernel, pairs, 3, [taken(ROWS)] * 4 + [taken(READS * MEM)]...  32 us
    pallas_call x1, Pallas kernels, token_grads(): call(token_grads_kernel, 1, 3, [IN_PLACE] * (5 * groups + 8), IN_PLACE, a...  7.77 us
    pallas_call x1, Pallas kernels, project_keys(): call(project_keys_kernel, 1, 2, [IN_HBM] * 3, [IN_PLACE] * 6, [array((ROW...  7.36 us
    unnamed x29, local copies, waits for them, and re-layouts  4.54 us
    pallas_call x1, Pallas kernels, project_queries(): call(project_queries_kernel, INNER // width, 0, [whole((ROWS, MODEL)), wh...  4 us
    pallas_call x1, Pallas kernels, project_memory(): call(project_memory_kernel, 1, 2, [IN_PLACE] * 5 + [IN_HBM] * 2, [whole((...  3.78 us
  transfers between devices with their start and end apart: 27, of which 11 were waited for; matrix products, arithmetic and copies ran while one was open for 0% of the time, Pallas kernels for 20%

profile of v2, /device:TPU:1, one launch (start us, length us, event | category | flops | bytes accessed | tf_op | source)
XLA Modules:
  0.0 160.6 jit_solution(15722263261359640638)
XLA Ops:
  1.9 4.5 %collective-permute-start.1 = (bf16[32,1536]{1,0:T(8,128)(2,1)S(1)}, bf16[32,1536]{1,0:T(8,128)(2,1)S(1)}, u32[]{:S(2)}, u32[]{:S(2)}) collective-permute-start(bf16[32,1536]{1,0:T(8,128)(2,1)S(1)} %bitcast.30), channel_id=1, source_target_pairs={{0,64},{4,68},{8,72},{12,76},{16,80},{20,84},{24,88},{28,92},{32,9... | collective-permute-start | bytes 294920 | tf_op jit(solution)/shard_map/ppermute | solution.py:706
  7.1 1.9 %collective-permute-start.2 = (bf16[32,1536]{1,0:T(8,128)(2,1)S(1)}, bf16[32,1536]{1,0:T(8,128)(2,1)S(1)}, u32[]{:S(2)}, u32[]{:S(2)}) collective-permute-start(bf16[32,1536]{1,0:T(8,128)(2,1)S(1)} %bitcast.32), channel_id=1, source_target_pairs={{0,96},{4,100},{8,104},{12,108},{16,112},{20,116},{24,120},{28,124... | collective-permute-start | bytes 294920 | tf_op jit(solution)/shard_map/ppermute | solution.py:706
  9.1 2.0 %collective-permute-done = bf16[32,1536]{1,0:T(8,128)(2,1)S(1)} collective-permute-done((bf16[32,1536]{1,0:T(8,128)(2,1)S(1)}, bf16[32,1536]{1,0:T(8,128)(2,1)S(1)}, u32[]{:S(2)}, u32[]{:S(2)}) %collective-permute-start) | collective-permute-done | bytes 98336 | tf_op jit(solution)/shard_map/ppermute | solution.py:706
  11.7 2.5 %collective-permute-start.5 = (bf16[4,32,1536]{2,1,0:T(8,128)(2,1)S(1)}, bf16[4,32,1536]{2,1,0:T(8,128)(2,1)S(1)}, u32[]{:S(2)}, u32[]{:S(2)}) collective-permute-start(bf16[4,32,1536]{2,1,0:T(8,128)(2,1)S(1)} %pad_maximum_fusion.held_0), channel_id=1, source_target_pairs={{0,24},{4,28},{8,0},{12,4},{16,8},{20,12},{24,16},{28,20},{32,56},... | collective-permute-start | bytes 1179656 | tf_op jit(solution)/shard_map/ppermute | solution.py:706
  16.0 7.4 %shard_map.104 = (bf16[512,1536]{1,0:T(8,128)(2,1)}, bf16[512,768]{1,0:T(8,128)(2,1)}, bf16[512,768]{1,0:T(8,128)(2,1)}, bf16[2,2,128,768]{3,2,1,0:T(8,128)(2,1)...) custom-call(s32[2]{0:T(128)} %pad_add_fusion.ids, s32[4,2,4]{2,1,0:T(2,128)} %bitcast.26, ...), custom_call_target="tpu_custom_call" | custom-call | flops 2415919104 | bytes 12582912 | tf_op jit(solution)/shard_map/pallas_call | solution.py:133
  24.8 2.6 %collective-permute-start.8 = (bf16[2,2,128,768]{3,2,1,0:T(8,128)(2,1)}, bf16[2,2,128,768]{3,2,1,0:T(8,128)(2,1)S(1)}, u32[]{:S(2)}, u32[]{:S(2)}) collective-permute-start(bf16[2,2,128,768]{3,2,1,0:T(8,128)(2,1)} %get-tuple-element.52), channel_id=1, source_target_pairs={{0,2},{1,3},{2,0},{3,1},{4,6},{5,7},{6,4},{7,5},{8,10},{9,11},{10,... | collective-permute-start | bytes 2359304 | tf_op jit(solution)/shard_map/ppermute | solution.py:706
  28.5 7.4 %collective-permute-done.3.held_1 = bf16[4,32,1536]{2,1,0:T(8,128)(2,1)S(1)} collective-permute-done((bf16[4,32,1536]{2,1,0:T(8,128)(2,1)S(1)}, bf16[4,32,1536]{2,1,0:T(8,128)(2,1)S(1)}, u32[]{:S(2)}, u32[]{:S(2)}) %collective-permute-start.3) | collective-permute-done | bytes 393248 | tf_op jit(solution)/shard_map/ppermute | solution.py:706
  42.2 4.0 %shard_map.105 = (bf16[512,768]{1,0:T(8,128)(2,1)S(1)}, bf16[512,768]{1,0:T(8,128)(2,1)S(1)}) custom-call(bf16[512,1536]{1,0:T(8,128)(2,1)S(1)} %copy-done.11, bf16[512,1536]{1,0:T(8,128)(2,1)S(1)} %bitcast.28, bf16[1536,768]{1,0:T(8,128)(2,1)S(1)} %copy-done.7, bf16[768,1536]{1,0:T(8,128)(2,1)S(1)} %copy-done.8), custom_call_target="tpu_custom_call" | custom-call | flops 2415919104 | bytes 10485760 | tf_op jit(solution)/shard_map/pallas_call | solution.py:166
  46.3 3.8 %shard_map.107 = (bf16[128,768]{1,0:T(8,128)(2,1)S(1)}, bf16[128,768]{1,0:T(8,128)(2,1)S(1)}) custom-call(s32[2]{0:T(128)S(1)} %copy-done.4, s32[4,32]{1,0:T(4,128)S(1)} %bitcast.21, bf16[4,32,1536]{2,1,0:T(8,128)(2,1)S(1)} %pad_maximum_fusion.held_0, bf16[4,32,1536]{2,1,0:T(8,128)(2,1)S(1)} %collective-permute-done.3.held_1, ...), custom_call_target="tpu_custom_call" | custom-call | flops 603979776 | bytes 6291456 | tf_op jit(solution)/shard_map/pallas_call | solution.py:275
  50.1 9.6 %collective-permute-done.8.rest_1_ = bf16[2,2,128,768]{3,2,1,0:T(8,128)(2,1)S(1)} collective-permute-done((bf16[2,2,128,768]{3,2,1,0:T(8,128)(2,1)}, bf16[2,2,128,768]{3,2,1,0:T(8,128)(2,1)S(1)}, u32[]{:S(2)}, u32[]{:S(2)}) %collective-permute-start.8) | collective-permute-done | bytes 786464 | tf_op jit(solution)/shard_map/ppermute | solution.py:706
  61.0 21.2 %shard_map.108 = (bf16[512,512]{1,0:T(8,128)(2,1)S(1)}, bf16[512,512]{1,0:T(8,128)(2,1)S(1)}, f32[512,512]{1,0:T(8,128)S(1)}, f32[512,512]{1,0:T(8,128)S(1)}, f3...) custom-call(s32[2]{0:T(128)S(1)} %copy-done.4, ...), custom_call_target="tpu_custom_call" | custom-call | flops 14495514624 | bytes 12582912 | tf_op jit(solution)/shard_map/pallas_call | solution.py:472
  82.2 2.0 %collective-permute-start.16 = (bf16[2,128,512]{2,1,0:T(8,128)(2,1)S(1)}, bf16[2,128,512]{2,1,0:T(8,128)(2,1)S(1)}, u32[]{:S(2)}, u32[]{:S(2)}) collective-permute-start(bf16[2,128,512]{2,1,0:T(8,128)(2,1)S(1)} %get-tuple-element.70), channel_id=1, source_target_pairs={{0,4},{4,0},{8,12},{12,8},{16,20},{20,16},{24,28},{28,24},{32,36},... | collective-permute-start | bytes 786440 | tf_op jit(solution)/shard_map/ppermute | solution.py:706
  84.2 10.9 %shard_map.109 = (bf16[512,256]{1,0:T(8,128)(2,1)S(1)}, bf16[512,256]{1,0:T(8,128)(2,1)S(1)}, f32[512,256]{1,0:T(8,128)S(1)}, f32[512,256]{1,0:T(8,128)S(1)}, f3...) custom-call(s32[2]{0:T(128)S(1)} %copy-done.4, ...), custom_call_target="tpu_custom_call" | custom-call | flops 7247757312 | bytes 6291456 | tf_op jit(solution)/shard_map/pallas_call | solution.py:472
  97.3 1.8 %collective-permute-start.21 = (bf16[4,2,32,256]{3,2,1,0:T(8,128)(2,1)S(1)}, bf16[4,2,32,256]{3,2,1,0:T(8,128)(2,1)S(1)}, u32[]{:S(2)}, u32[]{:S(2)}) collective-permute-start(bf16[4,2,32,256]{3,2,1,0:T(8,128)(2,1)S(1)} %get-tuple-element.78), channel_id=1, source_target_pairs={{0,8},{4,12},{8,16},{12,20},{16,24},{20,28},{24,0},{28,4},{32,40},... | collective-permute-start | bytes 393224 | tf_op jit(solution)/shard_map/ppermute | solution.py:706
  101.7 1.9 %collective-permute-start.13 = (bf16[2,2,128,256]{3,2,1,0:T(8,128)(2,1)S(1)}, bf16[2,2,128,256]{3,2,1,0:T(8,128)(2,1)S(1)}, u32[]{:S(2)}, u32[]{:S(2)}) collective-permute-start(bf16[2,2,128,256]{3,2,1,0:T(8,128)(2,1)S(1)} %get-tuple-element.66), channel_id=1, source_target_pairs={{0,3},{1,0},{2,1},{3,2},{4,7},{5,4},{6,5},{7,6},{8,11},{9,8},{10,9... | collective-permute-start | bytes 786440 | tf_op jit(solution)/shard_map/ppermute | solution.py:706
  109.0 1.9 %collective-permute-start.11 = (bf16[2,2,128,512]{3,2,1,0:T(8,128)(2,1)S(1)}, bf16[2,2,128,512]{3,2,1,0:T(8,128)(2,1)S(1)}, u32[]{:S(2)}, u32[]{:S(2)}) collective-permute-start(bf16[2,2,128,512]{3,2,1,0:T(8,128)(2,1)S(1)} %get-tuple-element.64), channel_id=1, source_target_pairs={{0,2},{1,3},{2,0},{3,1},{4,6},{5,7},{6,4},{7,5},{8,10},{9,11},{10,... | collective-permute-start | bytes 1572872 | tf_op jit(solution)/shard_map/ppermute | solution.py:706
  110.9 2.3 %collective-permute-done.17.refs_1_ = bf16[4,2,32,512]{3,2,1,0:T(8,128)(2,1)S(1)} collective-permute-done((bf16[4,2,32,512]{3,2,1,0:T(8,128)(2,1)S(1)}, bf16[4,2,32,512]{3,2,1,0:T(8,128)(2,1)S(1)}, u32[]{:S(2)}, u32[]{:S(2)}) %collective-permute-start.17) | collective-permute-done | bytes 262176 | tf_op jit(solution)/shard_map/ppermute | solution.py:706
  113.2 4.1 %collective-permute-done.18.refs_2_ = bf16[4,2,32,512]{3,2,1,0:T(8,128)(2,1)S(1)} collective-permute-done((bf16[4,2,32,512]{3,2,1,0:T(8,128)(2,1)S(1)}, bf16[4,2,32,512]{3,2,1,0:T(8,128)(2,1)S(1)}, u32[]{:S(2)}, u32[]{:S(2)}) %collective-permute-start.18) | collective-permute-done | bytes 262176 | tf_op jit(solution)/shard_map/ppermute | solution.py:706
  117.3 3.3 %collective-permute-start.14 = (bf16[2,2,128,256]{3,2,1,0:T(8,128)(2,1)S(1)}, bf16[2,2,128,256]{3,2,1,0:T(8,128)(2,1)S(1)}, u32[]{:S(2)}, u32[]{:S(2)}) collective-permute-start(bf16[2,2,128,256]{3,2,1,0:T(8,128)(2,1)S(1)} %get-tuple-element.67), channel_id=1, source_target_pairs={{0,2},{1,3},{2,0},{3,1},{4,6},{5,7},{6,4},{7,5},{8,10},{9,11},{10,... | collective-permute-start | bytes 786440 | tf_op jit(solution)/shard_map/ppermute | solution.py:706
  121.0 17.8 %collective-permute-done.14.refs_8_ = bf16[2,2,128,256]{3,2,1,0:T(8,128)(2,1)S(1)} collective-permute-done((bf16[2,2,128,256]{3,2,1,0:T(8,128)(2,1)S(1)}, bf16[2,2,128,256]{3,2,1,0:T(8,128)(2,1)S(1)}, u32[]{:S(2)}, u32[]{:S(2)}) %collective-permute-start.14) | collective-permute-done | bytes 262176 | tf_op jit(solution)/shard_map/ppermute | solution.py:706
  139.7 6.0 %collective-permute-done.15.refs_9_ = bf16[2,2,128,256]{3,2,1,0:T(8,128)(2,1)S(1)} collective-permute-done((bf16[2,2,128,256]{3,2,1,0:T(8,128)(2,1)S(1)}, bf16[2,2,128,256]{3,2,1,0:T(8,128)(2,1)S(1)}, u32[]{:S(2)}, u32[]{:S(2)}) %collective-permute-start.15) | collective-permute-done | bytes 262176 | tf_op jit(solution)/shard_map/ppermute | solution.py:706
  145.6 2.1 %collective-permute-start.25 = (bf16[2,32,768]{2,1,0:T(8,128)(2,1)S(1)}, bf16[2,32,768]{2,1,0:T(8,128)(2,1)S(1)}, u32[]{:S(2)}, u32[]{:S(2)}) collective-permute-start(bf16[2,32,768]{2,1,0:T(8,128)(2,1)S(1)} %get-tuple-element.83), channel_id=1, source_target_pairs={{0,64},{4,68},{8,72},{12,76},{16,80},{20,84},{24,88},{28,92},{32,9... | collective-permute-start | bytes 294920 | tf_op jit(solution)/shard_map/ppermute | solution.py:706
  148.9 3.7 %shard_map.110 = (bf16[512,1536]{1,0:T(8,128)(2,1)}, f32[512,1536]{1,0:T(8,128)S(1)}) custom-call(bf16[512,512]{1,0:T(8,128)(2,1)S(1)} %get-tuple-element.54.refs_0_, bf16[512,256]{1,0:T(8,128)(2,1)S(1)} %get-tuple-element.55.refs_1_, bf16[512,512]{1,0:T(8,128)(2,1)S(1)} %get-tuple-element.56.refs_2_, bf16[512,256]{1,0:T(8,128)(2,1)S(1)} %get-tuple-element.57.refs_3_, ...), custom_call_target="tpu_custom_call" | custom-call | flops 2415919104 | bytes 11534336 | tf_op jit(solution)/shard_map/pallas_call | solution.py:573
  152.6 7.8 %shard_map.114 = bf16[512,1536]{1,0:T(8,128)(2,1)} custom-call(s32[2]{0:T(128)S(1)} %copy-done.4, s32[4,4]{1,0:T(4,128)S(1)} %copy-done.6, s32[4,2,4]{2,1,0:T(2,128)S(1)} %bitcast.27, f32[512,512]{1,0:T(8,128)S(1)} %get-tuple-element.59.refs_0_, f32[512,256]{1,0:T(8,128)S(1)} %get-tuple-element.60.refs_1_, f32[512,512]{1,0:T(8,128)S(1)} %get-tuple-element.61.refs_2_, ...), custom_call_target="tpu_custom_call" | custom-call | flops 2415919104 | bytes 16777216 | tf_op jit(solution)/shard_map/pallas_call | solution.py:676
  (73 shorter events, 27.1 us)
Async XLA Ops:
  1.9 7.2 %collective-permute-start.1 = (bf16[32,1536]{1,0:T(8,128)(2,1)S(1)}, bf16[32,1536]{1,0:T(8,128)(2,1)S(1)}, u32[]{:S(2)}, u32[]{:S(2)}) collective-permute-start(bf16[32,1536]{1,0:T(8,128)(2,1)S(1)} %bitcast.30), channel_id=1, source_target_pairs={{0,64},{4,68},{8,72},{12,76},{16,80},{20,84},{24,88},{28,92},{32,9... | collective-permute-start | bytes 294920 | tf_op jit(solution)/shard_map/ppermute | solution.py:706
  11.7 15.6 %collective-permute-start.5 = (bf16[4,32,1536]{2,1,0:T(8,128)(2,1)S(1)}, bf16[4,32,1536]{2,1,0:T(8,128)(2,1)S(1)}, u32[]{:S(2)}, u32[]{:S(2)}) collective-permute-start(bf16[4,32,1536]{2,1,0:T(8,128)(2,1)S(1)} %pad_maximum_fusion.held_0), channel_id=1, source_target_pairs={{0,24},{4,28},{8,0},{12,4},{16,8},{20,12},{24,16},{28,20},{32,56},... | collective-permute-start | bytes 1179656 | tf_op jit(solution)/shard_map/ppermute | solution.py:706
  14.9 13.6 %collective-permute-start.4 = (bf16[4,32,1536]{2,1,0:T(8,128)(2,1)S(1)}, bf16[4,32,1536]{2,1,0:T(8,128)(2,1)S(1)}, u32[]{:S(2)}, u32[]{:S(2)}) collective-permute-start(bf16[4,32,1536]{2,1,0:T(8,128)(2,1)S(1)} %pad_maximum_fusion.held_0), channel_id=1, source_target_pairs={{0,16},{4,20},{8,24},{12,28},{16,0},{20,4},{24,8},{28,12},{32,48},... | collective-permute-start | bytes 1179656 | tf_op jit(solution)/shard_map/ppermute | solution.py:706
  15.4 20.4 %collective-permute-start.3 = (bf16[4,32,1536]{2,1,0:T(8,128)(2,1)S(1)}, bf16[4,32,1536]{2,1,0:T(8,128)(2,1)S(1)}, u32[]{:S(2)}, u32[]{:S(2)}) collective-permute-start(bf16[4,32,1536]{2,1,0:T(8,128)(2,1)S(1)} %pad_maximum_fusion.held_0), channel_id=1, source_target_pairs={{0,8},{4,12},{8,16},{12,20},{16,24},{20,28},{24,0},{28,4},{32,40},... | collective-permute-start | bytes 1179656 | tf_op jit(solution)/shard_map/ppermute | solution.py:706
  23.4 26.7 %collective-permute-start.7 = (bf16[2,2,128,768]{3,2,1,0:T(8,128)(2,1)}, bf16[2,2,128,768]{3,2,1,0:T(8,128)(2,1)S(1)}, u32[]{:S(2)}, u32[]{:S(2)}) collective-permute-start(bf16[2,2,128,768]{3,2,1,0:T(8,128)(2,1)} %get-tuple-element.51), channel_id=1, source_target_pairs={{0,1},{1,2},{2,3},{3,0},{4,5},{5,6},{6,7},{7,4},{8,9},{9,10},{10,1... | collective-permute-start | bytes 2359304 | tf_op jit(solution)/shard_map/ppermute | solution.py:706
  24.8 35.0 %collective-permute-start.8 = (bf16[2,2,128,768]{3,2,1,0:T(8,128)(2,1)}, bf16[2,2,128,768]{3,2,1,0:T(8,128)(2,1)S(1)}, u32[]{:S(2)}, u32[]{:S(2)}) collective-permute-start(bf16[2,2,128,768]{3,2,1,0:T(8,128)(2,1)} %get-tuple-element.52), channel_id=1, source_target_pairs={{0,2},{1,3},{2,0},{3,1},{4,6},{5,7},{6,4},{7,5},{8,10},{9,11},{10,... | collective-permute-start | bytes 2359304 | tf_op jit(solution)/shard_map/ppermute | solution.py:706
  27.4 33.6 %collective-permute-start.9 = (bf16[2,2,128,768]{3,2,1,0:T(8,128)(2,1)}, bf16[2,2,128,768]{3,2,1,0:T(8,128)(2,1)S(1)}, u32[]{:S(2)}, u32[]{:S(2)}) collective-permute-start(bf16[2,2,128,768]{3,2,1,0:T(8,128)(2,1)} %get-tuple-element.53), channel_id=1, source_target_pairs={{0,3},{1,0},{2,1},{3,2},{4,7},{5,4},{6,5},{7,6},{8,11},{9,8},{10,9... | collective-permute-start | bytes 2359304 | tf_op jit(solution)/shard_map/ppermute | solution.py:706
  36.7 9.6 %collective-permute-start.6 = (bf16[4,32,1536]{2,1,0:T(8,128)(2,1)S(1)}, bf16[4,32,1536]{2,1,0:T(8,128)(2,1)S(1)}, u32[]{:S(2)}, u32[]{:S(2)}) collective-permute-start(bf16[4,32,1536]{2,1,0:T(8,128)(2,1)S(1)} %shard_map.106), channel_id=1, source_target_pairs={{0,4},{4,0},{8,12},{12,8},{16,20},{20,16},{24,28},{28,24},{32,36},... | collective-permute-start | bytes 1179656 | tf_op jit(solution)/shard_map/ppermute | solution.py:706
  82.2 21.4 %collective-permute-start.16 = (bf16[2,128,512]{2,1,0:T(8,128)(2,1)S(1)}, bf16[2,128,512]{2,1,0:T(8,128)(2,1)S(1)}, u32[]{:S(2)}, u32[]{:S(2)}) collective-permute-start(bf16[2,128,512]{2,1,0:T(8,128)(2,1)S(1)} %get-tuple-element.70), channel_id=1, source_target_pairs={{0,4},{4,0},{8,12},{12,8},{16,20},{20,16},{24,28},{28,24},{32,36},... | collective-permute-start | bytes 786440 | tf_op jit(solution)/shard_map/ppermute | solution.py:706
  97.3 8.0 %collective-permute-start.21 = (bf16[4,2,32,256]{3,2,1,0:T(8,128)(2,1)S(1)}, bf16[4,2,32,256]{3,2,1,0:T(8,128)(2,1)S(1)}, u32[]{:S(2)}, u32[]{:S(2)}) collective-permute-start(bf16[4,2,32,256]{3,2,1,0:T(8,128)(2,1)S(1)} %get-tuple-element.78), channel_id=1, source_target_pairs={{0,8},{4,12},{8,16},{12,20},{16,24},{20,28},{24,0},{28,4},{32,40},... | collective-permute-start | bytes 393224 | tf_op jit(solution)/shard_map/ppermute | solution.py:706
  99.2 7.9 %collective-permute-start.22 = (bf16[4,2,32,256]{3,2,1,0:T(8,128)(2,1)S(1)}, bf16[4,2,32,256]{3,2,1,0:T(8,128)(2,1)S(1)}, u32[]{:S(2)}, u32[]{:S(2)}) collective-permute-start(bf16[4,2,32,256]{3,2,1,0:T(8,128)(2,1)S(1)} %get-tuple-element.79), channel_id=1, source_target_pairs={{0,16},{4,20},{8,24},{12,28},{16,0},{20,4},{24,8},{28,12},{32,48},... | collective-permute-start | bytes 393224 | tf_op jit(solution)/shard_map/ppermute | solution.py:706
  100.9 6.9 %collective-permute-start.23 = (bf16[4,2,32,256]{3,2,1,0:T(8,128)(2,1)S(1)}, bf16[4,2,32,256]{3,2,1,0:T(8,128)(2,1)S(1)}, u32[]{:S(2)}, u32[]{:S(2)}) collective-permute-start(bf16[4,2,32,256]{3,2,1,0:T(8,128)(2,1)S(1)} %get-tuple-element.80), channel_id=1, source_target_pairs={{0,24},{4,28},{8,0},{12,4},{16,8},{20,12},{24,16},{28,20},{32,56},... | collective-permute-start | bytes 393224 | tf_op jit(solution)/shard_map/ppermute | solution.py:706
  101.7 7.3 %collective-permute-start.13 = (bf16[2,2,128,256]{3,2,1,0:T(8,128)(2,1)S(1)}, bf16[2,2,128,256]{3,2,1,0:T(8,128)(2,1)S(1)}, u32[]{:S(2)}, u32[]{:S(2)}) collective-permute-start(bf16[2,2,128,256]{3,2,1,0:T(8,128)(2,1)S(1)} %get-tuple-element.66), channel_id=1, source_target_pairs={{0,3},{1,0},{2,1},{3,2},{4,7},{5,4},{6,5},{7,6},{8,11},{9,8},{10,9... | collective-permute-start | bytes 786440 | tf_op jit(solution)/shard_map/ppermute | solution.py:706
  104.5 8.7 %collective-permute-start.17 = (bf16[4,2,32,512]{3,2,1,0:T(8,128)(2,1)S(1)}, bf16[4,2,32,512]{3,2,1,0:T(8,128)(2,1)S(1)}, u32[]{:S(2)}, u32[]{:S(2)}) collective-permute-start(bf16[4,2,32,512]{3,2,1,0:T(8,128)(2,1)S(1)} %get-tuple-element.72), channel_id=1, source_target_pairs={{0,8},{4,12},{8,16},{12,20},{16,24},{20,28},{24,0},{28,4},{32,40},... | collective-permute-start | bytes 786440 | tf_op jit(solution)/shard_map/ppermute | solution.py:706
  105.3 12.0 %collective-permute-start.18 = (bf16[4,2,32,512]{3,2,1,0:T(8,128)(2,1)S(1)}, bf16[4,2,32,512]{3,2,1,0:T(8,128)(2,1)S(1)}, u32[]{:S(2)}, u32[]{:S(2)}) collective-permute-start(bf16[4,2,32,512]{3,2,1,0:T(8,128)(2,1)S(1)} %get-tuple-element.73), channel_id=1, source_target_pairs={{0,16},{4,20},{8,24},{12,28},{16,0},{20,4},{24,8},{28,12},{32,48},... | collective-permute-start | bytes 786440 | tf_op jit(solution)/shard_map/ppermute | solution.py:706
  107.1 13.5 %collective-permute-start.19 = (bf16[4,2,32,512]{3,2,1,0:T(8,128)(2,1)S(1)}, bf16[4,2,32,512]{3,2,1,0:T(8,128)(2,1)S(1)}, u32[]{:S(2)}, u32[]{:S(2)}) collective-permute-start(bf16[4,2,32,512]{3,2,1,0:T(8,128)(2,1)S(1)} %get-tuple-element.74), channel_id=1, source_target_pairs={{0,24},{4,28},{8,0},{12,4},{16,8},{20,12},{24,16},{28,20},{32,56},... | collective-permute-start | bytes 786440 | tf_op jit(solution)/shard_map/ppermute | solution.py:706
  107.8 39.9 %collective-permute-start.10 = (bf16[2,2,128,512]{3,2,1,0:T(8,128)(2,1)S(1)}, bf16[2,2,128,512]{3,2,1,0:T(8,128)(2,1)S(1)}, u32[]{:S(2)}, u32[]{:S(2)}) collective-permute-start(bf16[2,2,128,512]{3,2,1,0:T(8,128)(2,1)S(1)} %get-tuple-element.63), channel_id=1, source_target_pairs={{0,3},{1,0},{2,1},{3,2},{4,7},{5,4},{6,5},{7,6},{8,11},{9,8},{10,9... | collective-permute-start | bytes 1572872 | tf_op jit(solution)/shard_map/ppermute | solution.py:706
  109.0 43.5 %collective-permute-start.11 = (bf16[2,2,128,512]{3,2,1,0:T(8,128)(2,1)S(1)}, bf16[2,2,128,512]{3,2,1,0:T(8,128)(2,1)S(1)}, u32[]{:S(2)}, u32[]{:S(2)}) collective-permute-start(bf16[2,2,128,512]{3,2,1,0:T(8,128)(2,1)S(1)} %get-tuple-element.64), channel_id=1, source_target_pairs={{0,2},{1,3},{2,0},{3,1},{4,6},{5,7},{6,4},{7,5},{8,10},{9,11},{10,... | collective-permute-start | bytes 1572872 | tf_op jit(solution)/shard_map/ppermute | solution.py:706
  113.2 39.3 %collective-permute-start.12 = (bf16[2,2,128,512]{3,2,1,0:T(8,128)(2,1)S(1)}, bf16[2,2,128,512]{3,2,1,0:T(8,128)(2,1)S(1)}, u32[]{:S(2)}, u32[]{:S(2)}) collective-permute-start(bf16[2,2,128,512]{3,2,1,0:T(8,128)(2,1)S(1)} %get-tuple-element.65), channel_id=1, source_target_pairs={{0,1},{1,2},{2,3},{3,0},{4,5},{5,6},{6,7},{7,4},{8,9},{9,10},{10,1... | collective-permute-start | bytes 1572872 | tf_op jit(solution)/shard_map/ppermute | solution.py:706
  117.3 21.6 %collective-permute-start.14 = (bf16[2,2,128,256]{3,2,1,0:T(8,128)(2,1)S(1)}, bf16[2,2,128,256]{3,2,1,0:T(8,128)(2,1)S(1)}, u32[]{:S(2)}, u32[]{:S(2)}) collective-permute-start(bf16[2,2,128,256]{3,2,1,0:T(8,128)(2,1)S(1)} %get-tuple-element.67), channel_id=1, source_target_pairs={{0,2},{1,3},{2,0},{3,1},{4,6},{5,7},{6,4},{7,5},{8,10},{9,11},{10,... | collective-permute-start | bytes 786440 | tf_op jit(solution)/shard_map/ppermute | solution.py:706
  120.6 25.0 %collective-permute-start.15 = (bf16[2,2,128,256]{3,2,1,0:T(8,128)(2,1)S(1)}, bf16[2,2,128,256]{3,2,1,0:T(8,128)(2,1)S(1)}, u32[]{:S(2)}, u32[]{:S(2)}) collective-permute-start(bf16[2,2,128,256]{3,2,1,0:T(8,128)(2,1)S(1)} %get-tuple-element.68), channel_id=1, source_target_pairs={{0,1},{1,2},{2,3},{3,0},{4,5},{5,6},{6,7},{7,4},{8,9},{9,10},{10,1... | collective-permute-start | bytes 786440 | tf_op jit(solution)/shard_map/ppermute | solution.py:706
  138.8 13.7 %collective-permute-start.24 = (bf16[2,32,768]{2,1,0:T(8,128)(2,1)S(1)}, bf16[2,32,768]{2,1,0:T(8,128)(2,1)S(1)}, u32[]{:S(2)}, u32[]{:S(2)}) collective-permute-start(bf16[2,32,768]{2,1,0:T(8,128)(2,1)S(1)} %get-tuple-element.82), channel_id=1, source_target_pairs={{0,32},{4,36},{8,40},{12,44},{16,48},{20,52},{24,56},{28,60},{32,6... | collective-permute-start | bytes 294920 | tf_op jit(solution)/shard_map/ppermute | solution.py:706
  145.6 6.9 %collective-permute-start.25 = (bf16[2,32,768]{2,1,0:T(8,128)(2,1)S(1)}, bf16[2,32,768]{2,1,0:T(8,128)(2,1)S(1)}, u32[]{:S(2)}, u32[]{:S(2)}) collective-permute-start(bf16[2,32,768]{2,1,0:T(8,128)(2,1)S(1)} %get-tuple-element.83), channel_id=1, source_target_pairs={{0,64},{4,68},{8,72},{12,76},{16,80},{20,84},{24,88},{28,92},{32,9... | collective-permute-start | bytes 294920 | tf_op jit(solution)/shard_map/ppermute | solution.py:706
  147.7 4.8 %collective-permute-start.26 = (bf16[2,32,768]{2,1,0:T(8,128)(2,1)S(1)}, bf16[2,32,768]{2,1,0:T(8,128)(2,1)S(1)}, u32[]{:S(2)}, u32[]{:S(2)}) collective-permute-start(bf16[2,32,768]{2,1,0:T(8,128)(2,1)S(1)} %get-tuple-element.84), channel_id=1, source_target_pairs={{0,96},{4,100},{8,104},{12,108},{16,112},{20,116},{24,120},{28,124... | collective-permute-start | bytes 294920 | tf_op jit(solution)/shard_map/ppermute | solution.py:706
  (17 other events, 190.2 us)

commit v3 on v2

--- a/solution.py
+++ b/solution.py
@@ -24,7 +24,7 @@
 EPS = 1e-05
 MASKED = -1e30
 NT = (((1,), (1,)), ((), ()))
-GROUPS = ((0, 4), (4, 2))
+GROUPS = ((0, 5), (5, 1))
 
 
 def dot(left, right):
@@ -74,7 +74,7 @@
     return centred * inverse, inverse
 
 
-def project_keys_kernel(ids, index, tokens, w_key, w_value, low, keys, values, *rest):
+def project_keys_kernel(ids, index, tokens, w_key, w_value, low, keys, values, kept, *rest):
     sends, (rows, key_w, value_w, normed_low, made, in_sem, out_sem, send_sem) = rest[:3], rest[3:]
     camera = ids[0]
     loads = []
@@ -110,6 +110,10 @@
                 sem = send_sem.at[kind * SLOTS + 2 * (shift - 1) + slot]
                 store(made.at[kind, at], sends[shift - 1].at[kind, slot], sem)
         store(made.at[kind], out, out_sem.at[1 + kind])
+        row = lax.broadcasted_iota(jnp.int32, (MEM, ROWS), 1)
+        hit = row == lax.broadcasted_iota(jnp.int32, (MEM, ROWS), 0) * (ROWS // MEM)
+        choice = jnp.where(hit, 1.0, 0.0).astype(LOW)
+        kept[:, kind * INNER : (kind + 1) * INNER] = dot(choice, made[kind]).astype(LOW)
 
     half = ROWS // 2
     loads[0].wait()
@@ -135,8 +139,9 @@
         1,
         2,
         [IN_HBM] * 3,
-        [IN_PLACE] * 6,
+        [IN_PLACE] * 3 + [whole((MEM, 2 * INNER))] + [IN_PLACE] * 3,
         [array((ROWS, MODEL), LOW), array((ROWS, INNER), LOW), array((ROWS, INNER), LOW)]
+        + [array((MEM, 2 * INNER), LOW)]
         + [array((2, 2, STRIP, INNER), LOW)] * 3,
         [
             pltpu.VMEM((ROWS, MODEL), LOW),
@@ -213,7 +218,7 @@
 
         @pl.when(jnp.logical_not(wanted[read]))
         def _():
-            picked[read] = jnp.zeros((MEM, MODEL), LOW)
+            picked[read] = jnp.zeros((MEM, 2 * INNER), LOW)
 
     for read in range(READS):
 
@@ -228,8 +233,8 @@
         1,
         2,
         [IN_PLACE] * 4,
-        whole((READS, MEM, MODEL)),
-        array((READS, MEM, MODEL), LOW),
+        whole((READS, MEM, 2 * INNER)),
+        array((READS, MEM, 2 * INNER), LOW),
         [pltpu.SemaphoreType.DMA((READS,))],
         0,
         1 << 20,
@@ -237,62 +242,6 @@
     )(ids, offsets, *held)
 
 
-def project_memory_kernel(ids, offsets, held_0, held_1, held_2, held_3, given, w_key, w_value, keys, values, *rest):
-    rows, low, key_w, value_w, sem, w_sem = rest
-    frame = ids[1]
-    held = (held_0, held_1, held_2, held_3)
-    loads = [
-        pltpu.make_async_copy(w_key, key_w, w_sem.at[0]),
-        pltpu.make_async_copy(w_value, value_w, w_sem.at[1]),
-    ]
-    for read in range(READS):
-        source, live = source_of(offsets, frame, read)
-        back_z, back_x, same = back_to(frame, source)
-        mine = jnp.logical_and(live, same)
-        for shift in range(4):
-
-            @pl.when(jnp.logical_and(mine, back_x == shift))
-            def _():
-                pltpu.make_async_copy(held[shift].at[back_z], rows.at[read], sem.at[read]).start()
-
-        @pl.when(jnp.logical_not(mine))
-        def _():
-            pltpu.make_async_copy(given.at[read], rows.at[read], sem.at[read]).start()
-
-    for load in loads:
-        load.start()
-    for read in range(READS):
-        pltpu.make_async_copy(given.at[read], rows.at[read], sem.at[read]).wait()
-        low[read * MEM : (read + 1) * MEM, :] = normalize(rows[read])[0].astype(LOW)
-    for load, weight, out in zip(loads, (key_w, value_w), (keys, values)):
-        load.wait()
-        for start in range(0, INNER, 256):
-            cols = slice(start, start + 256)
-            out[:, cols] = dot(low[...], weight[:, cols]).astype(LOW)
-
-
-def project_memory(ids, offsets, held, given, w_key, w_value):
-    return call(
-        project_memory_kernel,
-        1,
-        2,
-        [IN_PLACE] * 5 + [IN_HBM] * 2,
-        [whole((READS * MEM, INNER))] * 2,
-        [array((READS * MEM, INNER), LOW)] * 2,
-        [
-            pltpu.VMEM((READS, MEM, MODEL), LOW),
-            pltpu.VMEM((READS * MEM, MODEL), LOW),
-            pltpu.VMEM((MODEL, INNER), LOW),
-            pltpu.VMEM((MODEL, INNER), LOW),
-            pltpu.SemaphoreType.DMA((READS,)),
-            pltpu.SemaphoreType.DMA((2,)),
-        ],
-        4 * READS * MEM * MODEL * INNER,
-        6 << 20,
-        vmem=10,
-    )(ids, offsets, *held, given, w_key, w_value)
-
-
 def shift_z(by):
     return [(f, (f + 8 * by) % 32) for f in range(32)]
 
@@ -308,8 +257,8 @@
     return [(s, (s + by) % 4) for s in range(4)]
 
 
-def attention_kernel(ids, offsets, count, queries, grads, keys_own, values_own, keys_mem, values_mem, *rest):
-    far_in, rest = rest[:3], rest[3:]
+def attention_kernel(ids, offsets, count, queries, grads, keys_own, values_own, *rest):
+    mem_in, far_in, rest = (rest[:5], rest[5:10]), rest[10:13], rest[13:]
     mixed, grad_query, grad_keys, grad_values, grad_mem, grad_mem_low = rest[:6]
     far_out, rest = rest[6:9], rest[9:]
     keys, values, keys_t, values_t, scores, grad_w, weights, grad_s, two_q, two_g, rest_k, rest_v = rest
@@ -325,8 +274,23 @@
 
     keys[0:ROWS, :] = keys_own[...]
     values[0:ROWS, :] = values_own[...]
-    keys[MEM_AT:FAR_AT, :] = keys_mem[...]
-    values[MEM_AT:FAR_AT, :] = values_mem[...]
+    for read in range(READS):
+        source, live = source_of(offsets, frame, read)
+        back_z, back_x, same = back_to(frame, source)
+        mine = jnp.logical_and(live, same)
+        at = slice(MEM_AT + read * MEM, MEM_AT + (read + 1) * MEM)
+        for shift in range(4):
+
+            @pl.when(jnp.logical_and(mine, back_x == shift))
+            def _():
+                keys[at, :] = mem_in[0][shift][back_z]
+                values[at, :] = mem_in[1][shift][back_z]
+
+        @pl.when(jnp.logical_not(mine))
+        def _():
+            keys[at, :] = mem_in[0][4][read]
+            values[at, :] = mem_in[1][4][read]
+
     for place in range(LIVE_MAX):
 
         @pl.when(live_total <= place)
@@ -456,7 +420,7 @@
             far_out[slot // 2][1, slot % 2] = rest_v[at, :].astype(LOW)
 
 
-def attention(group, ids, offsets, count, queries, grads, keys_own, values_own, keys_mem, values_mem, far):
+def attention(group, ids, offsets, count, queries, grads, keys_own, values_own, mem, far):
     first, pairs = group
     width = pairs * PAIR
 
@@ -468,12 +432,14 @@
 
     far_in = pl.BlockSpec((2, 2, STRIP, PAIR), lambda p, *_: (0, 0, 0, first + p))
     far_out = pl.BlockSpec((2, 2, STRIP, PAIR), lambda p, *_: (0, 0, 0, p))
+    mem_k = pl.BlockSpec((4, MEM, PAIR), lambda p, *_: (0, 0, first + p))
+    mem_v = pl.BlockSpec((4, MEM, PAIR), lambda p, *_: (0, 0, INNER // PAIR + first + p))
     mem_out = pl.BlockSpec((2, READS * MEM, PAIR), lambda p, *_: (0, 0, p))
     return call(
         attention_kernel,
         pairs,
         3,
-        [taken(ROWS)] * 4 + [taken(READS * MEM)] * 2 + [far_in] * 3,
+        [taken(ROWS)] * 4 + [mem_k] * 5 + [mem_v] * 5 + [far_in] * 3,
         [made(ROWS)] * 4 + [mem_out] * 2 + [far_out] * 3,
         [array((ROWS, width), LOW)] * 2
         + [array((ROWS, width), WIDE)] * 2
@@ -487,7 +453,7 @@
         + [pltpu.VMEM((KEYS - ROWS, PAIR), WIDE)] * 2,
         pairs * 12 * KEYS * 2 * ROWS * 256,
         pairs * (3 << 20),
-    )(ids, offsets, count, queries, grads, keys_own, values_own, keys_mem, values_mem, *far)
+    )(ids, offsets, count, queries, grads, keys_own, values_own, *mem, *mem, *far)
 
 
 def sort_kernel(ids, offsets, own, given, out_0, out_1, out_2, out_3, total):
@@ -593,35 +559,18 @@
     own = (refs[:groups], refs[groups : 2 * groups])
     back, refs = refs[2 * groups : 5 * groups], refs[5 * groups :]
     kept, (tokens, grad_part, w_key, w_value, grad_tokens), refs = refs[:4], refs[4:9], refs[9:]
-    total, far, near, rows, grad_normed, key_w, value_w, low, made = refs[:9]
-    own_sem, far_sem, near_sem, in_sem, out_sem = refs[9:]
+    total, grad_normed, low, made, out_sem = refs
     camera = ids[0]
 
-    near_loads = [pltpu.make_async_copy(kept[k], near.at[k], near_sem.at[k]) for k in range(4)]
-    own_loads, far_loads = [], []
-    for group, (first, pairs) in enumerate(GROUPS):
-        cols = pl.ds(first * PAIR, pairs * PAIR)
-        for kind in range(2):
-            own_loads.append(
-                pltpu.make_async_copy(
-                    own[kind][group], total.at[kind, :, cols], own_sem.at[2 * group + kind]
-                )
-            )
-        for k in range(3):
-            far_loads.append(
-                pltpu.make_async_copy(
-                    back[3 * group + k], far.at[k, :, :, :, cols], far_sem.at[3 * group + k]
-                )
-            )
-    pairs_of_refs = ((w_key, key_w), (w_value, value_w), (grad_part, grad_normed), (tokens, rows))
-    loads = [
-        pltpu.make_async_copy(source, target, in_sem.at[k])
-        for k, (source, target) in enumerate(pairs_of_refs)
-    ]
-    for load in own_loads + far_loads + near_loads + loads:
-        load.start()
-    for load in own_loads + far_loads:
-        load.wait()
+    row = lax.broadcasted_iota(jnp.int32, (ROWS, 4 * MEM), 0)
+    col = lax.broadcasted_iota(jnp.int32, (ROWS, 4 * MEM), 1)
+    hit = row == (col % MEM) * (ROWS // MEM)
+    spread = jnp.where(hit, 1.0, 0.0).astype(LOW)
+    for kind in range(2):
+        stacked = jnp.concatenate([part[kind] for part in kept], axis=0)
+        for group, (first, pairs) in enumerate(GROUPS):
+            cols = slice(first * PAIR, (first + pairs) * PAIR)
+            total[kind, :, cols] = own[kind][group][...] + dot(spread, stacked[:, cols])
     for shift in (1, 2, 3):
         other = lax.rem(camera + shift, 4)
         for slot in range(2):
@@ -631,33 +580,27 @@
                 start = index[camera, slot, other] * STRIP
                 at = pl.ds(pl.multiple_of(start, STRIP), STRIP)
                 for kind in range(2):
-                    total[kind, at, :] = total[kind, at, :] + far[shift - 1, kind, slot].astype(WIDE)
-
-    for load in near_loads:
-        load.wait()
+                    for group, (first, pairs) in enumerate(GROUPS):
+                        cols = slice(first * PAIR, (first + pairs) * PAIR)
+                        given = back[3 * group + shift - 1][kind, slot]
+                        total[kind, at, cols] = total[kind, at, cols] + given.astype(WIDE)
+
     half = ROWS // 2
-    row = lax.broadcasted_iota(jnp.int32, (half, 4 * MEM), 0)
-    col = lax.broadcasted_iota(jnp.int32, (half, 4 * MEM), 1)
-    stacked = [jnp.concatenate([near[k, kind] for k in range(4)], axis=0) for kind in range(2)]
-    for load in loads:
-        load.wait()
     stores = []
     for start in range(0, ROWS, half):
         at = slice(start, start + half)
-        hit = row + start == (col % MEM) * (ROWS // MEM)
-        spread = jnp.where(hit, 1.0, 0.0).astype(LOW)
         for kind in range(2):
-            low[kind, at, :] = (total[kind, at, :] + dot(spread, stacked[kind])).astype(LOW)
+            low[kind, at, :] = total[kind, at, :].astype(LOW)
         for first in range(0, MODEL, 512):
             cols = slice(first, first + 512)
             grad_normed[at, cols] = (
-                grad_normed[at, cols]
-                + dot_t(low[0, at, :], key_w[cols, :])
-                + dot_t(low[1, at, :], value_w[cols, :])
+                grad_part[at, cols]
+                + dot_t(low[0, at, :], w_key[cols, :])
+                + dot_t(low[1, at, :], w_value[cols, :])
             )
         for begin in range(start, start + half, 64):
             at = slice(begin, begin + 64)
-            normed, inverse = normalize(rows[at, :])
+            normed, inverse = normalize(tokens[at, :])
             grad = grad_normed[at, :]
             first_mean = jnp.mean(grad, axis=-1, keepdims=True)
             second_mean = jnp.mean(grad * normed, axis=-1, keepdims=True)
@@ -672,34 +615,26 @@
 
 
 def token_grads(ids, count, index, own_keys, own_values, back, kept, tokens, grad_part, w_key, w_value):
-    groups = len(GROUPS)
-    return call(
+    operands = (*own_keys, *own_values, *back, *kept, tokens, grad_part, w_key, w_value)
+    return pl.pallas_call(
         token_grads_kernel,
-        1,
-        3,
-        [IN_PLACE] * (5 * groups + 8),
-        IN_PLACE,
-        array((ROWS, MODEL), LOW),
-        [
+        in_specs=[pl.BlockSpec(memory_space=pltpu.SMEM)] * 3
+        + [pl.BlockSpec(memory_space=pltpu.VMEM)] * len(operands),
+        out_specs=IN_PLACE,
+        out_shape=array((ROWS, MODEL), LOW),
+        scratch_shapes=[
             pltpu.VMEM((2, ROWS, INNER), WIDE),
-            pltpu.VMEM((3, 2, 2, STRIP, INNER), LOW),
-            pltpu.VMEM((4, 2, MEM, INNER), LOW),
-            pltpu.VMEM((ROWS, MODEL), LOW),
             pltpu.VMEM((ROWS, MODEL), WIDE),
-            pltpu.VMEM((MODEL, INNER), LOW),
-            pltpu.VMEM((MODEL, INNER), LOW),
             pltpu.VMEM((2, ROWS, INNER), LOW),
             pltpu.VMEM((ROWS, MODEL), LOW),
-            pltpu.SemaphoreType.DMA((2 * groups,)),
-            pltpu.SemaphoreType.DMA((3 * groups,)),
-            pltpu.SemaphoreType.DMA((4,)),
-            pltpu.SemaphoreType.DMA((4,)),
             pltpu.SemaphoreType.DMA((2,)),
         ],
-        4 * ROWS * MODEL * INNER,
-        16 << 20,
-        vmem=26,
-    )(ids, count, index, *own_keys, *own_values, *back, *kept, tokens, grad_part, w_key, w_value)
+        compiler_params=pltpu.CompilerParams(vmem_limit_bytes=36 << 20),
+        cost_estimate=pl.CostEstimate(
+            flops=4 * ROWS * MODEL * INNER, bytes_accessed=16 << 20, transcendentals=0
+        ),
+        name="token_grads",
+    )(ids, count, index, *operands)
 
 
 def send(value, axis, pairs):
@@ -713,18 +648,15 @@
     index, offsets = jnp.transpose(index, (0, 2, 1)), offsets.T
     others = (1, 2, 3)
 
-    low, keys, values, *sends = project_keys(ids, index, tokens, w_key, w_value)
+    low, keys, values, kept, *sends = project_keys(ids, index, tokens, w_key, w_value)
     far = [send(sends[k - 1], "cam", shift_cam(k)) for k in others]
-    kept = tokens.reshape(MEM, ROWS // MEM, MODEL)[:, 0]
     along_z = jnp.stack([kept] + [send(kept, "tm", shift_z(k)) for k in others])
     held = [along_z] + [send(along_z, "tm", shift_x(k)) for k in others]
     queries, grads = project_queries(low, grad_update, w_query, w_out)
     given = send(pick(ids, offsets, held), "tm", SWAP_CORE)
-    keys_mem, values_mem = project_memory(ids, offsets, held, given, w_key, w_value)
-
     made, back, parts = [], [], []
     for group in GROUPS:
-        args = (queries, grads, keys, values, keys_mem, values_mem, far)
+        args = (queries, grads, keys, values, [*held, given], far)
         made.append(attention(group, ids, offsets, count, *args))
         back += [send(made[-1][5 + k], "cam", shift_cam(-k)) for k in others]
         mem_given = send(made[-1][5], "tm", SWAP_CORE)

time: 164 us -> 169 us (1.030)
  the two profiles are of different devices: /device:TPU:1 before, /device:TPU:6 now
where the time goes in v3:
time: 169 us
  waiting for transfers between devices  64.6 us (38%)
  Pallas kernels  60.8 us (36%)
  starting transfers between devices  39.2 us (23%)
    ppermute x27, waiting for transfers between devices, send(): return lax.ppermute(value, axis, pairs)  64.6 us
    ppermute x27, starting transfers between devices, send(): return lax.ppermute(value, axis, pairs)  39.2 us
    pallas_call x2, Pallas kernels, attention(): call(attention_kernel, pairs, 3, [taken(ROWS)] * 4 + [mem_k] * 5 + [mem_v...  33.9 us
    pallas_call x1, Pallas kernels, project_keys(): call(project_keys_kernel, 1, 2, [IN_HBM] * 3, [IN_PLACE] * 3 + [whole((ME...  8.54 us
    pallas_call x1, Pallas kernels, token_grads(): pl.pallas_call(token_grads_kernel, in_specs=[pl.BlockSpec(memory_space=pl...  6.85 us
    pallas_call x1, Pallas kernels, outward(): call(outward_kernel, MODEL // width, 0, parts + parts + [pl.BlockSpec((IN...  4.29 us
    pallas_call x1, Pallas kernels, project_queries(): call(project_queries_kernel, INNER // width, 0, [whole((ROWS, MODEL)), wh...  4 us
  transfers between devices with their start and end apart: 27, of which 13 were waited for; matrix products, arithmetic and copies ran while one was open for 0% of the time, Pallas kernels for 10%

profile of v3, /device:TPU:6, one launch (start us, length us, event | category | flops | bytes accessed | tf_op | source)
XLA Modules:
  0.0 168.7 jit_solution(7127774058281716573)
XLA Ops:
  1.3 8.5 %shard_map.104 = (bf16[512,1536]{1,0:T(8,128)(2,1)}, bf16[512,768]{1,0:T(8,128)(2,1)}, bf16[512,768]{1,0:T(8,128)(2,1)}, bf16[32,1536]{1,0:T(8,128)(2,1)}, bf16[...) custom-call(s32[2]{0:T(128)} %pad_add_fusion.ids, ...), custom_call_target="tpu_custom_call" | custom-call | flops 2415919104 | bytes 12582912 | tf_op jit(solution)/shard_map/pallas_call | solution.py:137
  9.9 4.1 %collective-permute-start.2 = (bf16[32,1536]{1,0:T(8,128)(2,1)}, bf16[32,1536]{1,0:T(8,128)(2,1)S(1)}, u32[]{:S(2)}, u32[]{:S(2)}) collective-permute-start(bf16[32,1536]{1,0:T(8,128)(2,1)} %get-tuple-element.48), channel_id=1, source_target_pairs={{0,96},{4,100},{8,104},{12,108},{16,112},{20,116},{24,120},{28,124... | collective-permute-start | bytes 294920 | tf_op jit(solution)/shard_map/ppermute | solution.py:641
  15.2 3.2 %collective-permute-done.2 = bf16[32,1536]{1,0:T(8,128)(2,1)S(1)} collective-permute-done((bf16[32,1536]{1,0:T(8,128)(2,1)}, bf16[32,1536]{1,0:T(8,128)(2,1)S(1)}, u32[]{:S(2)}, u32[]{:S(2)}) %collective-permute-start.2) | collective-permute-done | bytes 98336 | tf_op jit(solution)/shard_map/ppermute | solution.py:641
  18.4 2.6 %collective-permute-done.1 = bf16[32,1536]{1,0:T(8,128)(2,1)S(1)} collective-permute-done((bf16[32,1536]{1,0:T(8,128)(2,1)}, bf16[32,1536]{1,0:T(8,128)(2,1)S(1)}, u32[]{:S(2)}, u32[]{:S(2)}) %collective-permute-start.1) | collective-permute-done | bytes 98336 | tf_op jit(solution)/shard_map/ppermute | solution.py:641
  26.3 2.1 %collective-permute-start.3 = (bf16[4,32,1536]{2,1,0:T(8,128)(2,1)S(1)}, bf16[4,32,1536]{2,1,0:T(8,128)(2,1)S(1)}, u32[]{:S(2)}, u32[]{:S(2)}) collective-permute-start(bf16[4,32,1536]{2,1,0:T(8,128)(2,1)S(1)} %pad_maximum_fusion.held_0.rest_0_.rest_5_), channel_id=1, source_target_pairs={{0,8},{4,12},{8,16},{12,20},{16,24},{20,28},{24,0},{28,4},{32,40},... | collective-permute-start | bytes 1179656 | tf_op jit(solution)/shard_map/ppermute | solution.py:641
  28.4 2.9 %collective-permute-start.8 = (bf16[2,2,128,768]{3,2,1,0:T(8,128)(2,1)}, bf16[2,2,128,768]{3,2,1,0:T(8,128)(2,1)S(1)}, u32[]{:S(2)}, u32[]{:S(2)}) collective-permute-start(bf16[2,2,128,768]{3,2,1,0:T(8,128)(2,1)} %get-tuple-element.50), channel_id=1, source_target_pairs={{0,2},{1,3},{2,0},{3,1},{4,6},{5,7},{6,4},{7,5},{8,10},{9,11},{10,... | collective-permute-start | bytes 2359304 | tf_op jit(solution)/shard_map/ppermute | solution.py:641
  31.3 11.9 %collective-permute-done.5.held_3.rest_3_.rest_8_ = bf16[4,32,1536]{2,1,0:T(8,128)(2,1)S(1)} collective-permute-done((bf16[4,32,1536]{2,1,0:T(8,128)(2,1)S(1)}, bf16[4,32,1536]{2,1,0:T(8,128)(2,1)S(1)}, u32[]{:S(2)}, u32[]{:S(2)}) %collective-permute-start.5) | collective-permute-done | bytes 393248 | tf_op jit(solution)/shard_map/ppermute | solution.py:641
  43.2 3.0 %collective-permute-start.9 = (bf16[2,2,128,768]{3,2,1,0:T(8,128)(2,1)}, bf16[2,2,128,768]{3,2,1,0:T(8,128)(2,1)S(1)}, u32[]{:S(2)}, u32[]{:S(2)}) collective-permute-start(bf16[2,2,128,768]{3,2,1,0:T(8,128)(2,1)} %get-tuple-element.51), channel_id=1, source_target_pairs={{0,3},{1,0},{2,1},{3,2},{4,7},{5,4},{6,5},{7,6},{8,11},{9,8},{10,9... | collective-permute-start | bytes 2359304 | tf_op jit(solution)/shard_map/ppermute | solution.py:641
  49.1 4.0 %shard_map.105 = (bf16[512,768]{1,0:T(8,128)(2,1)S(1)}, bf16[512,768]{1,0:T(8,128)(2,1)S(1)}) custom-call(bf16[512,1536]{1,0:T(8,128)(2,1)S(1)} %copy-done.10, bf16[512,1536]{1,0:T(8,128)(2,1)S(1)} %bitcast.21, bf16[1536,768]{1,0:T(8,128)(2,1)S(1)} %copy-done.7, bf16[768,1536]{1,0:T(8,128)(2,1)S(1)} %copy-done.8), custom_call_target="tpu_custom_call" | custom-call | flops 2415919104 | bytes 10485760 | tf_op jit(solution)/shard_map/pallas_call | solution.py:171
  53.1 8.9 %collective-permute-done.8.rest_11_ = bf16[2,2,128,768]{3,2,1,0:T(8,128)(2,1)S(1)} collective-permute-done((bf16[2,2,128,768]{3,2,1,0:T(8,128)(2,1)}, bf16[2,2,128,768]{3,2,1,0:T(8,128)(2,1)S(1)}, u32[]{:S(2)}, u32[]{:S(2)}) %collective-permute-start.8) | collective-permute-done | bytes 786464 | tf_op jit(solution)/shard_map/ppermute | solution.py:641
  62.0 2.1 %collective-permute-done.9.rest_12_ = bf16[2,2,128,768]{3,2,1,0:T(8,128)(2,1)S(1)} collective-permute-done((bf16[2,2,128,768]{3,2,1,0:T(8,128)(2,1)}, bf16[2,2,128,768]{3,2,1,0:T(8,128)(2,1)S(1)}, u32[]{:S(2)}, u32[]{:S(2)}) %collective-permute-start.9) | collective-permute-done | bytes 786464 | tf_op jit(solution)/shard_map/ppermute | solution.py:641
  64.1 28.0 %shard_map.107 = (bf16[512,640]{1,0:T(8,128)(2,1)S(1)}, bf16[512,640]{1,0:T(8,128)(2,1)S(1)}, f32[512,640]{1,0:T(8,128)S(1)}, f32[512,640]{1,0:T(8,128)S(1)}, f3...) custom-call(s32[2]{0:T(128)S(1)} %copy-done.4, ...), custom_call_target="tpu_custom_call" | custom-call | flops 18119393280 | bytes 15728640 | tf_op jit(solution)/shard_map/pallas_call | solution.py:438
  92.2 2.7 %collective-permute-start.10 = (bf16[2,2,128,640]{3,2,1,0:T(8,128)(2,1)S(1)}, bf16[2,2,128,640]{3,2,1,0:T(8,128)(2,1)S(1)}, u32[]{:S(2)}, u32[]{:S(2)}) collective-permute-start(bf16[2,2,128,640]{3,2,1,0:T(8,128)(2,1)S(1)} %get-tuple-element.61), channel_id=1, source_target_pairs={{0,3},{1,0},{2,1},{3,2},{4,7},{5,4},{6,5},{7,6},{8,11},{9,8},{10,9... | collective-permute-start | bytes 1966088 | tf_op jit(solution)/shard_map/ppermute | solution.py:641
  96.9 5.9 %shard_map.108 = (bf16[512,128]{1,0:T(8,128)(2,1)S(1)}, bf16[512,128]{1,0:T(8,128)(2,1)S(1)}, f32[512,128]{1,0:T(8,128)S(1)}, f32[512,128]{1,0:T(8,128)S(1)}, f3...) custom-call(s32[2]{0:T(128)S(1)} %copy-done.4, ...), custom_call_target="tpu_custom_call" | custom-call | flops 3623878656 | bytes 3145728 | tf_op jit(solution)/shard_map/pallas_call | solution.py:438
  106.5 1.9 %collective-permute-start.21 = (bf16[4,2,32,128]{3,2,1,0:T(8,128)(2,1)S(1)}, bf16[4,2,32,128]{3,2,1,0:T(8,128)(2,1)S(1)}, u32[]{:S(2)}, u32[]{:S(2)}) collective-permute-start(bf16[4,2,32,128]{3,2,1,0:T(8,128)(2,1)S(1)} %get-tuple-element.76), channel_id=1, source_target_pairs={{0,8},{4,12},{8,16},{12,20},{16,24},{20,28},{24,0},{28,4},{32,40},... | collective-permute-start | bytes 196616 | tf_op jit(solution)/shard_map/ppermute | solution.py:641
  109.8 3.0 %collective-permute-done.13.refs_7_ = bf16[2,2,128,128]{3,2,1,0:T(8,128)(2,1)S(1)} collective-permute-done((bf16[2,2,128,128]{3,2,1,0:T(8,128)(2,1)S(1)}, bf16[2,2,128,128]{3,2,1,0:T(8,128)(2,1)S(1)}, u32[]{:S(2)}, u32[]{:S(2)}) %collective-permute-start.13) | collective-permute-done | bytes 131104 | tf_op jit(solution)/shard_map/ppermute | solution.py:641
  113.1 2.0 %collective-permute-start.18 = (bf16[4,2,32,640]{3,2,1,0:T(8,128)(2,1)S(1)}, bf16[4,2,32,640]{3,2,1,0:T(8,128)(2,1)S(1)}, u32[]{:S(2)}, u32[]{:S(2)}) collective-permute-start(bf16[4,2,32,640]{3,2,1,0:T(8,128)(2,1)S(1)} %get-tuple-element.71), channel_id=1, source_target_pairs={{0,16},{4,20},{8,24},{12,28},{16,0},{20,4},{24,8},{28,12},{32,48},... | collective-permute-start | bytes 983048 | tf_op jit(solution)/shard_map/ppermute | solution.py:641
  115.1 1.8 %collective-permute-start.19 = (bf16[4,2,32,640]{3,2,1,0:T(8,128)(2,1)S(1)}, bf16[4,2,32,640]{3,2,1,0:T(8,128)(2,1)S(1)}, u32[]{:S(2)}, u32[]{:S(2)}) collective-permute-start(bf16[4,2,32,640]{3,2,1,0:T(8,128)(2,1)S(1)} %get-tuple-element.72), channel_id=1, source_target_pairs={{0,24},{4,28},{8,0},{12,4},{16,8},{20,12},{24,16},{28,20},{32,56},... | collective-permute-start | bytes 983048 | tf_op jit(solution)/shard_map/ppermute | solution.py:641
  116.9 8.4 %collective-permute-done.23.refs_7_ = bf16[4,2,32,128]{3,2,1,0:T(8,128)(2,1)S(1)} collective-permute-done((bf16[4,2,32,128]{3,2,1,0:T(8,128)(2,1)S(1)}, bf16[4,2,32,128]{3,2,1,0:T(8,128)(2,1)S(1)}, u32[]{:S(2)}, u32[]{:S(2)}) %collective-permute-start.23) | collective-permute-done | bytes 65568 | tf_op jit(solution)/shard_map/ppermute | solution.py:641
  125.3 2.2 %collective-permute-start.11 = (bf16[2,2,128,640]{3,2,1,0:T(8,128)(2,1)S(1)}, bf16[2,2,128,640]{3,2,1,0:T(8,128)(2,1)S(1)}, u32[]{:S(2)}, u32[]{:S(2)}) collective-permute-start(bf16[2,2,128,640]{3,2,1,0:T(8,128)(2,1)S(1)} %get-tuple-element.62), channel_id=1, source_target_pairs={{0,2},{1,3},{2,0},{3,1},{4,6},{5,7},{6,4},{7,5},{8,10},{9,11},{10,... | collective-permute-start | bytes 1966088 | tf_op jit(solution)/shard_map/ppermute | solution.py:641
  129.1 1.8 %collective-permute-start.14 = (bf16[2,2,128,128]{3,2,1,0:T(8,128)(2,1)S(1)}, bf16[2,2,128,128]{3,2,1,0:T(8,128)(2,1)S(1)}, u32[]{:S(2)}, u32[]{:S(2)}) collective-permute-start(bf16[2,2,128,128]{3,2,1,0:T(8,128)(2,1)S(1)} %get-tuple-element.65), channel_id=1, source_target_pairs={{0,2},{1,3},{2,0},{3,1},{4,6},{5,7},{6,4},{7,5},{8,10},{9,11},{10,... | collective-permute-start | bytes 393224 | tf_op jit(solution)/shard_map/ppermute | solution.py:641
  133.7 20.2 %collective-permute-done.14.refs_8_ = bf16[2,2,128,128]{3,2,1,0:T(8,128)(2,1)S(1)} collective-permute-done((bf16[2,2,128,128]{3,2,1,0:T(8,128)(2,1)S(1)}, bf16[2,2,128,128]{3,2,1,0:T(8,128)(2,1)S(1)}, u32[]{:S(2)}, u32[]{:S(2)}) %collective-permute-start.14) | collective-permute-done | bytes 131104 | tf_op jit(solution)/shard_map/ppermute | solution.py:641
  157.2 4.3 %shard_map.109 = (bf16[512,1536]{1,0:T(8,128)(2,1)}, f32[512,1536]{1,0:T(8,128)S(1)}) custom-call(bf16[512,640]{1,0:T(8,128)(2,1)S(1)} %get-tuple-element.52.refs_0_, bf16[512,128]{1,0:T(8,128)(2,1)S(1)} %get-tuple-element.53.refs_1_, bf16[512,640]{1,0:T(8,128)(2,1)S(1)} %get-tuple-element.54.refs_2_, bf16[512,128]{1,0:T(8,128)(2,1)S(1)} %get-tuple-element.55.refs_3_, ...), custom_call_target="tpu_custom_call" | custom-call | flops 2415919104 | bytes 11534336 | tf_op jit(solution)/shard_map/pallas_call | solution.py:539
  161.7 6.9 %token_grads.1 = bf16[512,1536]{1,0:T(8,128)(2,1)} custom-call(s32[2]{0:T(128)S(1)} %copy-done.4, s32[4,4]{1,0:T(4,128)S(1)} %copy-done.6, s32[4,2,4]{2,1,0:T(2,128)S(1)} %bitcast.20, f32[512,640]{1,0:T(8,128)S(1)} %get-tuple-element.57.refs_0_, f32[512,128]{1,0:T(8,128)S(1)} %get-tuple-element.58.refs_1_, f32[512,640]{1,0:T(8,128)S(1)} %get-tuple-element.59.refs_2_, ...), custom_call_target="tpu_custom_call" | custom-call | flops 2415919104 | bytes 16777216 | tf_op jit(solution)/shard_map/token_grads/pallas_call | solution.py:619
  (68 shorter events, 25.3 us)
Async XLA Ops:
  9.9 8.6 %collective-permute-start.2 = (bf16[32,1536]{1,0:T(8,128)(2,1)}, bf16[32,1536]{1,0:T(8,128)(2,1)S(1)}, u32[]{:S(2)}, u32[]{:S(2)}) collective-permute-start(bf16[32,1536]{1,0:T(8,128)(2,1)} %get-tuple-element.48), channel_id=1, source_target_pairs={{0,96},{4,100},{8,104},{12,108},{16,112},{20,116},{24,120},{28,124... | collective-permute-start | bytes 294920 | tf_op jit(solution)/shard_map/ppermute | solution.py:641
  14.0 7.1 %collective-permute-start.1 = (bf16[32,1536]{1,0:T(8,128)(2,1)}, bf16[32,1536]{1,0:T(8,128)(2,1)S(1)}, u32[]{:S(2)}, u32[]{:S(2)}) collective-permute-start(bf16[32,1536]{1,0:T(8,128)(2,1)} %get-tuple-element.48), channel_id=1, source_target_pairs={{0,64},{4,68},{8,72},{12,76},{16,80},{20,84},{24,88},{28,92},{32,9... | collective-permute-start | bytes 294920 | tf_op jit(solution)/shard_map/ppermute | solution.py:641
  14.0 7.8 %collective-permute-start = (bf16[32,1536]{1,0:T(8,128)(2,1)}, bf16[32,1536]{1,0:T(8,128)(2,1)S(1)}, u32[]{:S(2)}, u32[]{:S(2)}) collective-permute-start(bf16[32,1536]{1,0:T(8,128)(2,1)} %get-tuple-element.48), channel_id=1, source_target_pairs={{0,32},{4,36},{8,40},{12,44},{16,48},{20,52},{24,56},{28,60},{32,6... | collective-permute-start | bytes 294920 | tf_op jit(solution)/shard_map/ppermute | solution.py:641
  22.7 20.5 %collective-permute-start.5 = (bf16[4,32,1536]{2,1,0:T(8,128)(2,1)S(1)}, bf16[4,32,1536]{2,1,0:T(8,128)(2,1)S(1)}, u32[]{:S(2)}, u32[]{:S(2)}) collective-permute-start(bf16[4,32,1536]{2,1,0:T(8,128)(2,1)S(1)} %pad_maximum_fusion.held_0.rest_0_.rest_5_), channel_id=1, source_target_pairs={{0,24},{4,28},{8,0},{12,4},{16,8},{20,12},{24,16},{28,20},{32,56},... | collective-permute-start | bytes 1179656 | tf_op jit(solution)/shard_map/ppermute | solution.py:641
  23.6 29.5 %collective-permute-start.7 = (bf16[2,2,128,768]{3,2,1,0:T(8,128)(2,1)}, bf16[2,2,128,768]{3,2,1,0:T(8,128)(2,1)S(1)}, u32[]{:S(2)}, u32[]{:S(2)}) collective-permute-start(bf16[2,2,128,768]{3,2,1,0:T(8,128)(2,1)} %get-tuple-element.49), channel_id=1, source_target_pairs={{0,1},{1,2},{2,3},{3,0},{4,5},{5,6},{6,7},{7,4},{8,9},{9,10},{10,1... | collective-permute-start | bytes 2359304 | tf_op jit(solution)/shard_map/ppermute | solution.py:641
  25.2 21.0 %collective-permute-start.4 = (bf16[4,32,1536]{2,1,0:T(8,128)(2,1)S(1)}, bf16[4,32,1536]{2,1,0:T(8,128)(2,1)S(1)}, u32[]{:S(2)}, u32[]{:S(2)}) collective-permute-start(bf16[4,32,1536]{2,1,0:T(8,128)(2,1)S(1)} %pad_maximum_fusion.held_0.rest_0_.rest_5_), channel_id=1, source_target_pairs={{0,16},{4,20},{8,24},{12,28},{16,0},{20,4},{24,8},{28,12},{32,48},... | collective-permute-start | bytes 1179656 | tf_op jit(solution)/shard_map/ppermute | solution.py:641
  26.3 19.9 %collective-permute-start.3 = (bf16[4,32,1536]{2,1,0:T(8,128)(2,1)S(1)}, bf16[4,32,1536]{2,1,0:T(8,128)(2,1)S(1)}, u32[]{:S(2)}, u32[]{:S(2)}) collective-permute-start(bf16[4,32,1536]{2,1,0:T(8,128)(2,1)S(1)} %pad_maximum_fusion.held_0.rest_0_.rest_5_), channel_id=1, source_target_pairs={{0,8},{4,12},{8,16},{12,20},{16,24},{20,28},{24,0},{28,4},{32,40},... | collective-permute-start | bytes 1179656 | tf_op jit(solution)/shard_map/ppermute | solution.py:641
  28.4 33.6 %collective-permute-start.8 = (bf16[2,2,128,768]{3,2,1,0:T(8,128)(2,1)}, bf16[2,2,128,768]{3,2,1,0:T(8,128)(2,1)S(1)}, u32[]{:S(2)}, u32[]{:S(2)}) collective-permute-start(bf16[2,2,128,768]{3,2,1,0:T(8,128)(2,1)} %get-tuple-element.50), channel_id=1, source_target_pairs={{0,2},{1,3},{2,0},{3,1},{4,6},{5,7},{6,4},{7,5},{8,10},{9,11},{10,... | collective-permute-start | bytes 2359304 | tf_op jit(solution)/shard_map/ppermute | solution.py:641
  43.2 20.9 %collective-permute-start.9 = (bf16[2,2,128,768]{3,2,1,0:T(8,128)(2,1)}, bf16[2,2,128,768]{3,2,1,0:T(8,128)(2,1)S(1)}, u32[]{:S(2)}, u32[]{:S(2)}) collective-permute-start(bf16[2,2,128,768]{3,2,1,0:T(8,128)(2,1)} %get-tuple-element.51), channel_id=1, source_target_pairs={{0,3},{1,0},{2,1},{3,2},{4,7},{5,4},{6,5},{7,6},{8,11},{9,8},{10,9... | collective-permute-start | bytes 2359304 | tf_op jit(solution)/shard_map/ppermute | solution.py:641
  47.4 16.7 %collective-permute-start.6 = (bf16[4,32,1536]{2,1,0:T(8,128)(2,1)S(1)}, bf16[4,32,1536]{2,1,0:T(8,128)(2,1)S(1)}, u32[]{:S(2)}, u32[]{:S(2)}) collective-permute-start(bf16[4,32,1536]{2,1,0:T(8,128)(2,1)S(1)} %shard_map.106), channel_id=1, source_target_pairs={{0,4},{4,0},{8,12},{12,8},{16,20},{20,16},{24,28},{28,24},{32,36},... | collective-permute-start | bytes 1179656 | tf_op jit(solution)/shard_map/ppermute | solution.py:641
  92.2 63.3 %collective-permute-start.10 = (bf16[2,2,128,640]{3,2,1,0:T(8,128)(2,1)S(1)}, bf16[2,2,128,640]{3,2,1,0:T(8,128)(2,1)S(1)}, u32[]{:S(2)}, u32[]{:S(2)}) collective-permute-start(bf16[2,2,128,640]{3,2,1,0:T(8,128)(2,1)S(1)} %get-tuple-element.61), channel_id=1, source_target_pairs={{0,3},{1,0},{2,1},{3,2},{4,7},{5,4},{6,5},{7,6},{8,11},{9,8},{10,9... | collective-permute-start | bytes 1966088 | tf_op jit(solution)/shard_map/ppermute | solution.py:641
  96.0 31.5 %collective-permute-start.17 = (bf16[4,2,32,640]{3,2,1,0:T(8,128)(2,1)S(1)}, bf16[4,2,32,640]{3,2,1,0:T(8,128)(2,1)S(1)}, u32[]{:S(2)}, u32[]{:S(2)}) collective-permute-start(bf16[4,2,32,640]{3,2,1,0:T(8,128)(2,1)S(1)} %get-tuple-element.70), channel_id=1, source_target_pairs={{0,8},{4,12},{8,16},{12,20},{16,24},{20,28},{24,0},{28,4},{32,40},... | collective-permute-start | bytes 983048 | tf_op jit(solution)/shard_map/ppermute | solution.py:641
  102.8 10.0 %collective-permute-start.13 = (bf16[2,2,128,128]{3,2,1,0:T(8,128)(2,1)S(1)}, bf16[2,2,128,128]{3,2,1,0:T(8,128)(2,1)S(1)}, u32[]{:S(2)}, u32[]{:S(2)}) collective-permute-start(bf16[2,2,128,128]{3,2,1,0:T(8,128)(2,1)S(1)} %get-tuple-element.64), channel_id=1, source_target_pairs={{0,3},{1,0},{2,1},{3,2},{4,7},{5,4},{6,5},{7,6},{8,11},{9,8},{10,9... | collective-permute-start | bytes 393224 | tf_op jit(solution)/shard_map/ppermute | solution.py:641
  106.5 6.6 %collective-permute-start.21 = (bf16[4,2,32,128]{3,2,1,0:T(8,128)(2,1)S(1)}, bf16[4,2,32,128]{3,2,1,0:T(8,128)(2,1)S(1)}, u32[]{:S(2)}, u32[]{:S(2)}) collective-permute-start(bf16[4,2,32,128]{3,2,1,0:T(8,128)(2,1)S(1)} %get-tuple-element.76), channel_id=1, source_target_pairs={{0,8},{4,12},{8,16},{12,20},{16,24},{20,28},{24,0},{28,4},{32,40},... | collective-permute-start | bytes 196616 | tf_op jit(solution)/shard_map/ppermute | solution.py:641
  108.3 6.8 %collective-permute-start.22 = (bf16[4,2,32,128]{3,2,1,0:T(8,128)(2,1)S(1)}, bf16[4,2,32,128]{3,2,1,0:T(8,128)(2,1)S(1)}, u32[]{:S(2)}, u32[]{:S(2)}) collective-permute-start(bf16[4,2,32,128]{3,2,1,0:T(8,128)(2,1)S(1)} %get-tuple-element.77), channel_id=1, source_target_pairs={{0,16},{4,20},{8,24},{12,28},{16,0},{20,4},{24,8},{28,12},{32,48},... | collective-permute-start | bytes 196616 | tf_op jit(solution)/shard_map/ppermute | solution.py:641
  112.8 12.5 %collective-permute-start.23 = (bf16[4,2,32,128]{3,2,1,0:T(8,128)(2,1)S(1)}, bf16[4,2,32,128]{3,2,1,0:T(8,128)(2,1)S(1)}, u32[]{:S(2)}, u32[]{:S(2)}) collective-permute-start(bf16[4,2,32,128]{3,2,1,0:T(8,128)(2,1)S(1)} %get-tuple-element.78), channel_id=1, source_target_pairs={{0,24},{4,28},{8,0},{12,4},{16,8},{20,12},{24,16},{28,20},{32,56},... | collective-permute-start | bytes 196616 | tf_op jit(solution)/shard_map/ppermute | solution.py:641
  113.1 16.0 %collective-permute-start.18 = (bf16[4,2,32,640]{3,2,1,0:T(8,128)(2,1)S(1)}, bf16[4,2,32,640]{3,2,1,0:T(8,128)(2,1)S(1)}, u32[]{:S(2)}, u32[]{:S(2)}) collective-permute-start(bf16[4,2,32,640]{3,2,1,0:T(8,128)(2,1)S(1)} %get-tuple-element.71), channel_id=1, source_target_pairs={{0,16},{4,20},{8,24},{12,28},{16,0},{20,4},{24,8},{28,12},{32,48},... | collective-permute-start | bytes 983048 | tf_op jit(solution)/shard_map/ppermute | solution.py:641
  115.1 16.8 %collective-permute-start.19 = (bf16[4,2,32,640]{3,2,1,0:T(8,128)(2,1)S(1)}, bf16[4,2,32,640]{3,2,1,0:T(8,128)(2,1)S(1)}, u32[]{:S(2)}, u32[]{:S(2)}) collective-permute-start(bf16[4,2,32,640]{3,2,1,0:T(8,128)(2,1)S(1)} %get-tuple-element.72), channel_id=1, source_target_pairs={{0,24},{4,28},{8,0},{12,4},{16,8},{20,12},{24,16},{28,20},{32,56},... | collective-permute-start | bytes 983048 | tf_op jit(solution)/shard_map/ppermute | solution.py:641
  125.3 36.2 %collective-permute-start.11 = (bf16[2,2,128,640]{3,2,1,0:T(8,128)(2,1)S(1)}, bf16[2,2,128,640]{3,2,1,0:T(8,128)(2,1)S(1)}, u32[]{:S(2)}, u32[]{:S(2)}) collective-permute-start(bf16[2,2,128,640]{3,2,1,0:T(8,128)(2,1)S(1)} %get-tuple-element.62), channel_id=1, source_target_pairs={{0,2},{1,3},{2,0},{3,1},{4,6},{5,7},{6,4},{7,5},{8,10},{9,11},{10,... | collective-permute-start | bytes 1966088 | tf_op jit(solution)/shard_map/ppermute | solution.py:641
  127.5 34.0 %collective-permute-start.12 = (bf16[2,2,128,640]{3,2,1,0:T(8,128)(2,1)S(1)}, bf16[2,2,128,640]{3,2,1,0:T(8,128)(2,1)S(1)}, u32[]{:S(2)}, u32[]{:S(2)}) collective-permute-start(bf16[2,2,128,640]{3,2,1,0:T(8,128)(2,1)S(1)} %get-tuple-element.63), channel_id=1, source_target_pairs={{0,1},{1,2},{2,3},{3,0},{4,5},{5,6},{6,7},{7,4},{8,9},{9,10},{10,1... | collective-permute-start | bytes 1966088 | tf_op jit(solution)/shard_map/ppermute | solution.py:641
  129.1 24.7 %collective-permute-start.14 = (bf16[2,2,128,128]{3,2,1,0:T(8,128)(2,1)S(1)}, bf16[2,2,128,128]{3,2,1,0:T(8,128)(2,1)S(1)}, u32[]{:S(2)}, u32[]{:S(2)}) collective-permute-start(bf16[2,2,128,128]{3,2,1,0:T(8,128)(2,1)S(1)} %get-tuple-element.65), channel_id=1, source_target_pairs={{0,2},{1,3},{2,0},{3,1},{4,6},{5,7},{6,4},{7,5},{8,10},{9,11},{10,... | collective-permute-start | bytes 393224 | tf_op jit(solution)/shard_map/ppermute | solution.py:641
  131.9 23.2 %collective-permute-start.15 = (bf16[2,2,128,128]{3,2,1,0:T(8,128)(2,1)S(1)}, bf16[2,2,128,128]{3,2,1,0:T(8,128)(2,1)S(1)}, u32[]{:S(2)}, u32[]{:S(2)}) collective-permute-start(bf16[2,2,128,128]{3,2,1,0:T(8,128)(2,1)S(1)} %get-tuple-element.66), channel_id=1, source_target_pairs={{0,1},{1,2},{2,3},{3,0},{4,5},{5,6},{6,7},{7,4},{8,9},{9,10},{10,1... | collective-permute-start | bytes 393224 | tf_op jit(solution)/shard_map/ppermute | solution.py:641
  153.9 7.6 %collective-permute-start.24 = (bf16[2,32,768]{2,1,0:T(8,128)(2,1)S(1)}, bf16[2,32,768]{2,1,0:T(8,128)(2,1)S(1)}, u32[]{:S(2)}, u32[]{:S(2)}) collective-permute-start(bf16[2,32,768]{2,1,0:T(8,128)(2,1)S(1)} %get-tuple-element.80), channel_id=1, source_target_pairs={{0,32},{4,36},{8,40},{12,44},{16,48},{20,52},{24,56},{28,60},{32,6... | collective-permute-start | bytes 294920 | tf_op jit(solution)/shard_map/ppermute | solution.py:641
  155.1 6.4 %collective-permute-start.25 = (bf16[2,32,768]{2,1,0:T(8,128)(2,1)S(1)}, bf16[2,32,768]{2,1,0:T(8,128)(2,1)S(1)}, u32[]{:S(2)}, u32[]{:S(2)}) collective-permute-start(bf16[2,32,768]{2,1,0:T(8,128)(2,1)S(1)} %get-tuple-element.81), channel_id=1, source_target_pairs={{0,64},{4,68},{8,72},{12,76},{16,80},{20,84},{24,88},{28,92},{32,9... | collective-permute-start | bytes 294920 | tf_op jit(solution)/shard_map/ppermute | solution.py:641
  (16 other events, 294.9 us)

commit v4 on v3

--- a/solution.py
+++ b/solution.py
@@ -13,6 +13,7 @@
 INNER = 768
 STRIP = 128
 MEM = 32
+POOL = ROWS // MEM
 READS = 4
 SLOTS = 6
 LIVE_MAX = 4
@@ -24,7 +25,7 @@
 EPS = 1e-05
 MASKED = -1e30
 NT = (((1,), (1,)), ((), ()))
-GROUPS = ((0, 5), (5, 1))
+GROUPS = ((0, 4), (4, 2))
 
 
 def dot(left, right):
@@ -75,7 +76,8 @@
 
 
 def project_keys_kernel(ids, index, tokens, w_key, w_value, low, keys, values, kept, *rest):
-    sends, (rows, key_w, value_w, normed_low, made, in_sem, out_sem, send_sem) = rest[:3], rest[3:]
+    sends, rest = rest[:3], rest[3:]
+    rows, key_w, value_w, normed_low, made, kept_wide, kept_low, in_sem, out_sem, send_sem = rest
     camera = ids[0]
     loads = []
     for step, start in enumerate(range(0, ROWS, STRIP)):
@@ -88,13 +90,20 @@
 
     def norm(first, last):
         for start in range(first, last, 64):
-            at = slice(start, start + 64)
-            normed_low[at, :] = normalize(rows[at, :])[0].astype(LOW)
+            normed = normalize(rows[start : start + 64, :])[0]
+            normed_low[start : start + 64, :] = normed.astype(LOW)
+            picked = normed.reshape(64 // POOL, POOL, MODEL)[:, 0, :]
+            kept_wide[start // POOL : (start + 64) // POOL, :] = picked
 
     def product(kind, weight, first, last):
         for start in range(0, INNER, 256):
             cols = slice(start, start + 256)
             made[kind, first:last, cols] = dot(normed_low[first:last, :], weight[:, cols]).astype(LOW)
+
+    def product_kept(kind, weight):
+        for start in range(0, INNER, 256):
+            cols = slice(kind * INNER + start, kind * INNER + start + 256)
+            kept[:, cols] = dot(kept_low[...], weight[:, start : start + 256]).astype(LOW)
 
     stores = []
 
@@ -110,10 +119,6 @@
                 sem = send_sem.at[kind * SLOTS + 2 * (shift - 1) + slot]
                 store(made.at[kind, at], sends[shift - 1].at[kind, slot], sem)
         store(made.at[kind], out, out_sem.at[1 + kind])
-        row = lax.broadcasted_iota(jnp.int32, (MEM, ROWS), 1)
-        hit = row == lax.broadcasted_iota(jnp.int32, (MEM, ROWS), 0) * (ROWS // MEM)
-        choice = jnp.where(hit, 1.0, 0.0).astype(LOW)
-        kept[:, kind * INNER : (kind + 1) * INNER] = dot(choice, made[kind]).astype(LOW)
 
     half = ROWS // 2
     loads[0].wait()
@@ -125,8 +130,11 @@
     norm(half, ROWS)
     store(normed_low, low, out_sem.at[0])
     product(0, key_w, half, ROWS)
+    kept_low[...] = kept_wide[...].astype(LOW)
+    product_kept(0, key_w)
     publish(0, keys)
     loads[5].wait()
+    product_kept(1, value_w)
     product(1, value_w, 0, ROWS)
     publish(1, values)
     for copy in stores:
@@ -149,6 +157,8 @@
             pltpu.VMEM((MODEL, INNER), LOW),
             pltpu.VMEM((ROWS, MODEL), LOW),
             pltpu.VMEM((2, ROWS, INNER), LOW),
+            pltpu.VMEM((MEM, MODEL), WIDE),
+            pltpu.VMEM((MEM, MODEL), LOW),
             pltpu.SemaphoreType.DMA((6,)),
             pltpu.SemaphoreType.DMA((3,)),
             pltpu.SemaphoreType.DMA((2 * SLOTS,)),
@@ -201,44 +211,50 @@
     return lax.rem(z_here - z_at + 4, 4), lax.rem(x_here - x_at + 4, 4), core_at == core_here
 
 
-def pick_kernel(ids, offsets, held_0, held_1, held_2, held_3, picked, sem):
+def pick_kernel(ids, offsets, held_0, held_1, held_2, held_3, for_partner, for_me, sem):
     frame = ids[1]
     partner = frame + 1 - 2 * lax.rem(frame, 2)
     held = (held_0, held_1, held_2, held_3)
     wanted = []
-    for read in range(READS):
-        source, live = source_of(offsets, partner, read)
-        back_z, back_x, same = back_to(frame, source)
-        wanted.append(jnp.logical_and(live, same))
-        for shift in range(4):
-
-            @pl.when(jnp.logical_and(wanted[read], back_x == shift))
+    for at, (reader, picked) in enumerate(((partner, for_partner), (frame, for_me))):
+        for read in range(READS):
+            source, live = source_of(offsets, reader, read)
+            back_z, back_x, same = back_to(frame, source)
+            wanted.append(jnp.logical_and(live, same))
+            slot = at * READS + read
+            for shift in range(4):
+
+                @pl.when(jnp.logical_and(wanted[-1], back_x == shift))
+                def _():
+                    pltpu.make_async_copy(
+                        held[shift].at[back_z], picked.at[read], sem.at[slot]
+                    ).start()
+
+            @pl.when(jnp.logical_not(wanted[-1]))
             def _():
-                pltpu.make_async_copy(held[shift].at[back_z], picked.at[read], sem.at[read]).start()
-
-        @pl.when(jnp.logical_not(wanted[read]))
+                picked[read] = jnp.zeros((MEM, 2 * INNER), LOW)
+
+    for slot in range(2 * READS):
+        picked = (for_partner, for_me)[slot // READS]
+
+        @pl.when(wanted[slot])
         def _():
-            picked[read] = jnp.zeros((MEM, 2 * INNER), LOW)
-
-    for read in range(READS):
-
-        @pl.when(wanted[read])
-        def _():
-            pltpu.make_async_copy(held_0.at[0], picked.at[read], sem.at[read]).wait()
+            pltpu.make_async_copy(held_0.at[0], picked.at[slot % READS], sem.at[slot]).wait()
 
 
 def pick(ids, offsets, held):
+    shape = (READS, MEM, 2 * INNER)
     return call(
         pick_kernel,
         1,
         2,
         [IN_PLACE] * 4,
-        whole((READS, MEM, 2 * INNER)),
-        array((READS, MEM, 2 * INNER), LOW),
-        [pltpu.SemaphoreType.DMA((READS,))],
+        [whole(shape)] * 2,
+        [array(shape, LOW)] * 2,
+        [pltpu.SemaphoreType.DMA((2 * READS,))],
         0,
         1 << 20,
-        vmem=2,
+        vmem=4,
     )(ids, offsets, *held)
 
 
@@ -258,7 +274,7 @@
 
 
 def attention_kernel(ids, offsets, count, queries, grads, keys_own, values_own, *rest):
-    mem_in, far_in, rest = (rest[:5], rest[5:10]), rest[10:13], rest[13:]
+    mem_in, far_in, rest = (rest[:2], rest[2:4]), rest[4:7], rest[7:]
     mixed, grad_query, grad_keys, grad_values, grad_mem, grad_mem_low = rest[:6]
     far_out, rest = rest[6:9], rest[9:]
     keys, values, keys_t, values_t, scores, grad_w, weights, grad_s, two_q, two_g, rest_k, rest_v = rest
@@ -276,20 +292,12 @@
     values[0:ROWS, :] = values_own[...]
     for read in range(READS):
         source, live = source_of(offsets, frame, read)
-        back_z, back_x, same = back_to(frame, source)
+        _, _, same = back_to(frame, source)
         mine = jnp.logical_and(live, same)
         at = slice(MEM_AT + read * MEM, MEM_AT + (read + 1) * MEM)
-        for shift in range(4):
-
-            @pl.when(jnp.logical_and(mine, back_x == shift))
-            def _():
-                keys[at, :] = mem_in[0][shift][back_z]
-                values[at, :] = mem_in[1][shift][back_z]
-
-        @pl.when(jnp.logical_not(mine))
-        def _():
-            keys[at, :] = mem_in[0][4][read]
-            values[at, :] = mem_in[1][4][read]
+        for kind, target in enumerate((keys, values)):
+            picked, given = mem_in[kind]
+            target[at, :] = jnp.where(mine, picked[read], given[read])
 
     for place in range(LIVE_MAX):
 
@@ -439,7 +447,7 @@
         attention_kernel,
         pairs,
         3,
-        [taken(ROWS)] * 4 + [mem_k] * 5 + [mem_v] * 5 + [far_in] * 3,
+        [taken(ROWS)] * 4 + [mem_k] * 2 + [mem_v] * 2 + [far_in] * 3,
         [made(ROWS)] * 4 + [mem_out] * 2 + [far_out] * 3,
         [array((ROWS, width), LOW)] * 2
         + [array((ROWS, width), WIDE)] * 2
@@ -653,12 +661,14 @@
     along_z = jnp.stack([kept] + [send(kept, "tm", shift_z(k)) for k in others])
     held = [along_z] + [send(along_z, "tm", shift_x(k)) for k in others]
     queries, grads = project_queries(low, grad_update, w_query, w_out)
-    given = send(pick(ids, offsets, held), "tm", SWAP_CORE)
+    for_partner, for_me = pick(ids, offsets, held)
+    given = send(for_partner, "tm", SWAP_CORE)
     made, back, parts = [], [], []
     for group in GROUPS:
-        args = (queries, grads, keys, values, [*held, given], far)
+        args = (queries, grads, keys, values, (for_me, given), far)
         made.append(attention(group, ids, offsets, count, *args))
-        back += [send(made[-1][5 + k], "cam", shift_cam(-k)) for k in others]
+        for k in others:
+            back.append(send(made[-1][5 + k], "cam", shift_cam(-k)))
         mem_given = send(made[-1][5], "tm", SWAP_CORE)
         to_x = sort_reads(ids, offsets, made[-1][4], mem_given)
         parts += [to_x[0]] + [send(to_x[k], "tm", shift_x(k)) for k in others]

time: 169 us -> 165 us (0.976)
  the two profiles are of different devices: /device:TPU:6 before, /device:TPU:1 now
where the time goes in v4:
time: 165 us; the launch traced here: 162 us
  waiting for transfers between devices  61.3 us (37%)
  Pallas kernels  58.8 us (36%)
  starting transfers between devices  38 us (23%)
    ppermute x27, waiting for transfers between devices, send(): return lax.ppermute(value, axis, pairs)  61.3 us
    ppermute x27, starting transfers between devices, send(): return lax.ppermute(value, axis, pairs)  38 us
    pallas_call x2, Pallas kernels, attention(): call(attention_kernel, pairs, 3, [taken(ROWS)] * 4 + [mem_k] * 2 + [mem_v...  32.4 us
    pallas_call x1, Pallas kernels, project_keys(): call(project_keys_kernel, 1, 2, [IN_HBM] * 3, [IN_PLACE] * 3 + [whole((ME...  9.2 us
    pallas_call x1, Pallas kernels, token_grads(): pl.pallas_call(token_grads_kernel, in_specs=[pl.BlockSpec(memory_space=pl...  6.58 us
    pallas_call x1, Pallas kernels, project_queries(): call(project_queries_kernel, INNER // width, 0, [whole((ROWS, MODEL)), wh...  4 us
    pallas_call x1, Pallas kernels, outward(): call(outward_kernel, MODEL // width, 0, parts + parts + [pl.BlockSpec((IN...  3.69 us
  transfers between devices with their start and end apart: 27, of which 15 were waited for; matrix products, arithmetic and copies ran while one was open for 0% of the time, Pallas kernels for 13%

profile of v4, /device:TPU:1, one launch (start us, length us, event | category | flops | bytes accessed | tf_op | source)
XLA Modules:
  0.0 162.1 jit_solution(4323255150105377262)
XLA Ops:
  1.3 9.2 %shard_map.104 = (bf16[512,1536]{1,0:T(8,128)(2,1)}, bf16[512,768]{1,0:T(8,128)(2,1)}, bf16[512,768]{1,0:T(8,128)(2,1)}, bf16[32,1536]{1,0:T(8,128)(2,1)}, bf16[...) custom-call(s32[2]{0:T(128)} %pad_add_fusion.ids, ...), custom_call_target="tpu_custom_call" | custom-call | flops 2415919104 | bytes 12582912 | tf_op jit(solution)/shard_map/pallas_call | solution.py:145
  10.5 4.6 %collective-permute-start.2 = (bf16[32,1536]{1,0:T(8,128)(2,1)}, bf16[32,1536]{1,0:T(8,128)(2,1)S(1)}, u32[]{:S(2)}, u32[]{:S(2)}) collective-permute-start(bf16[32,1536]{1,0:T(8,128)(2,1)} %get-tuple-element.50), channel_id=1, source_target_pairs={{0,96},{4,100},{8,104},{12,108},{16,112},{20,116},{24,120},{28,124... | collective-permute-start | bytes 294920 | tf_op jit(solution)/shard_map/ppermute | solution.py:649
  15.8 3.7 %collective-permute-done.2 = bf16[32,1536]{1,0:T(8,128)(2,1)S(1)} collective-permute-done((bf16[32,1536]{1,0:T(8,128)(2,1)}, bf16[32,1536]{1,0:T(8,128)(2,1)S(1)}, u32[]{:S(2)}, u32[]{:S(2)}) %collective-permute-start.2) | collective-permute-done | bytes 98336 | tf_op jit(solution)/shard_map/ppermute | solution.py:649
  20.4 2.7 %collective-permute-done = bf16[32,1536]{1,0:T(8,128)(2,1)S(1)} collective-permute-done((bf16[32,1536]{1,0:T(8,128)(2,1)}, bf16[32,1536]{1,0:T(8,128)(2,1)S(1)}, u32[]{:S(2)}, u32[]{:S(2)}) %collective-permute-start) | collective-permute-done | bytes 98336 | tf_op jit(solution)/shard_map/ppermute | solution.py:649
  24.0 2.5 %collective-permute-start.5 = (bf16[4,32,1536]{2,1,0:T(8,128)(2,1)S(1)}, bf16[4,32,1536]{2,1,0:T(8,128)(2,1)S(1)}, u32[]{:S(2)}, u32[]{:S(2)}) collective-permute-start(bf16[4,32,1536]{2,1,0:T(8,128)(2,1)S(1)} %pad_maximum_fusion.held_0), channel_id=1, source_target_pairs={{0,24},{4,28},{8,0},{12,4},{16,8},{20,12},{24,16},{28,20},{32,56},... | collective-permute-start | bytes 1179656 | tf_op jit(solution)/shard_map/ppermute | solution.py:649
  29.0 2.6 %collective-permute-start.8 = (bf16[2,2,128,768]{3,2,1,0:T(8,128)(2,1)}, bf16[2,2,128,768]{3,2,1,0:T(8,128)(2,1)S(1)}, u32[]{:S(2)}, u32[]{:S(2)}) collective-permute-start(bf16[2,2,128,768]{3,2,1,0:T(8,128)(2,1)} %get-tuple-element.54), channel_id=1, source_target_pairs={{0,2},{1,3},{2,0},{3,1},{4,6},{5,7},{6,4},{7,5},{8,10},{9,11},{10,... | collective-permute-start | bytes 2359304 | tf_op jit(solution)/shard_map/ppermute | solution.py:649
  31.6 3.4 %collective-permute-done.5.held_3 = bf16[4,32,1536]{2,1,0:T(8,128)(2,1)S(1)} collective-permute-done((bf16[4,32,1536]{2,1,0:T(8,128)(2,1)S(1)}, bf16[4,32,1536]{2,1,0:T(8,128)(2,1)S(1)}, u32[]{:S(2)}, u32[]{:S(2)}) %collective-permute-start.5) | collective-permute-done | bytes 393248 | tf_op jit(solution)/shard_map/ppermute | solution.py:649
  35.1 2.7 %collective-permute-start.9 = (bf16[2,2,128,768]{3,2,1,0:T(8,128)(2,1)}, bf16[2,2,128,768]{3,2,1,0:T(8,128)(2,1)S(1)}, u32[]{:S(2)}, u32[]{:S(2)}) collective-permute-start(bf16[2,2,128,768]{3,2,1,0:T(8,128)(2,1)} %get-tuple-element.55), channel_id=1, source_target_pairs={{0,3},{1,0},{2,1},{3,2},{4,7},{5,4},{6,5},{7,6},{8,11},{9,8},{10,9... | collective-permute-start | bytes 2359304 | tf_op jit(solution)/shard_map/ppermute | solution.py:649
  38.8 10.1 %collective-permute-done.3.held_1 = bf16[4,32,1536]{2,1,0:T(8,128)(2,1)S(1)} collective-permute-done((bf16[4,32,1536]{2,1,0:T(8,128)(2,1)S(1)}, bf16[4,32,1536]{2,1,0:T(8,128)(2,1)S(1)}, u32[]{:S(2)}, u32[]{:S(2)}) %collective-permute-start.3) | collective-permute-done | bytes 393248 | tf_op jit(solution)/shard_map/ppermute | solution.py:649
  52.6 4.0 %shard_map.105 = (bf16[512,768]{1,0:T(8,128)(2,1)S(1)}, bf16[512,768]{1,0:T(8,128)(2,1)S(1)}) custom-call(bf16[512,1536]{1,0:T(8,128)(2,1)S(1)} %copy-done.10, bf16[512,1536]{1,0:T(8,128)(2,1)S(1)} %bitcast.21, bf16[1536,768]{1,0:T(8,128)(2,1)S(1)} %copy-done.7, bf16[768,1536]{1,0:T(8,128)(2,1)S(1)} %copy-done.8), custom_call_target="tpu_custom_call" | custom-call | flops 2415919104 | bytes 10485760 | tf_op jit(solution)/shard_map/pallas_call | solution.py:181
  56.6 7.6 %collective-permute-done.8.rest_5_ = bf16[2,2,128,768]{3,2,1,0:T(8,128)(2,1)S(1)} collective-permute-done((bf16[2,2,128,768]{3,2,1,0:T(8,128)(2,1)}, bf16[2,2,128,768]{3,2,1,0:T(8,128)(2,1)S(1)}, u32[]{:S(2)}, u32[]{:S(2)}) %collective-permute-start.8) | collective-permute-done | bytes 786464 | tf_op jit(solution)/shard_map/ppermute | solution.py:649
  64.2 21.4 %shard_map.107 = (bf16[512,512]{1,0:T(8,128)(2,1)S(1)}, bf16[512,512]{1,0:T(8,128)(2,1)S(1)}, f32[512,512]{1,0:T(8,128)S(1)}, f32[512,512]{1,0:T(8,128)S(1)}, f3...) custom-call(s32[2]{0:T(128)S(1)} %copy-done.4, ...), custom_call_target="tpu_custom_call" | custom-call | flops 14495514624 | bytes 12582912 | tf_op jit(solution)/shard_map/pallas_call | solution.py:446
  85.6 2.5 %collective-permute-start.16 = (bf16[2,128,512]{2,1,0:T(8,128)(2,1)S(1)}, bf16[2,128,512]{2,1,0:T(8,128)(2,1)S(1)}, u32[]{:S(2)}, u32[]{:S(2)}) collective-permute-start(bf16[2,128,512]{2,1,0:T(8,128)(2,1)S(1)} %get-tuple-element.72), channel_id=1, source_target_pairs={{0,4},{4,0},{8,12},{12,8},{16,20},{20,16},{24,28},{28,24},{32,36},... | collective-permute-start | bytes 786440 | tf_op jit(solution)/shard_map/ppermute | solution.py:649
  88.1 11.0 %shard_map.108 = (bf16[512,256]{1,0:T(8,128)(2,1)S(1)}, bf16[512,256]{1,0:T(8,128)(2,1)S(1)}, f32[512,256]{1,0:T(8,128)S(1)}, f32[512,256]{1,0:T(8,128)S(1)}, f3...) custom-call(s32[2]{0:T(128)S(1)} %copy-done.4, ...), custom_call_target="tpu_custom_call" | custom-call | flops 7247757312 | bytes 6291456 | tf_op jit(solution)/shard_map/pallas_call | solution.py:446
  101.4 1.9 %collective-permute-start.21 = (bf16[4,2,32,256]{3,2,1,0:T(8,128)(2,1)S(1)}, bf16[4,2,32,256]{3,2,1,0:T(8,128)(2,1)S(1)}, u32[]{:S(2)}, u32[]{:S(2)}) collective-permute-start(bf16[4,2,32,256]{3,2,1,0:T(8,128)(2,1)S(1)} %get-tuple-element.80), channel_id=1, source_target_pairs={{0,8},{4,12},{8,16},{12,20},{16,24},{20,28},{24,0},{28,4},{32,40},... | collective-permute-start | bytes 393224 | tf_op jit(solution)/shard_map/ppermute | solution.py:649
  105.7 2.3 %collective-permute-start.13 = (bf16[2,2,128,256]{3,2,1,0:T(8,128)(2,1)S(1)}, bf16[2,2,128,256]{3,2,1,0:T(8,128)(2,1)S(1)}, u32[]{:S(2)}, u32[]{:S(2)}) collective-permute-start(bf16[2,2,128,256]{3,2,1,0:T(8,128)(2,1)S(1)} %get-tuple-element.68), channel_id=1, source_target_pairs={{0,3},{1,0},{2,1},{3,2},{4,7},{5,4},{6,5},{7,6},{8,11},{9,8},{10,9... | collective-permute-start | bytes 786440 | tf_op jit(solution)/shard_map/ppermute | solution.py:649
  113.6 1.9 %collective-permute-start.11 = (bf16[2,2,128,512]{3,2,1,0:T(8,128)(2,1)S(1)}, bf16[2,2,128,512]{3,2,1,0:T(8,128)(2,1)S(1)}, u32[]{:S(2)}, u32[]{:S(2)}) collective-permute-start(bf16[2,2,128,512]{3,2,1,0:T(8,128)(2,1)S(1)} %get-tuple-element.66), channel_id=1, source_target_pairs={{0,2},{1,3},{2,0},{3,1},{4,6},{5,7},{6,4},{7,5},{8,10},{9,11},{10,... | collective-permute-start | bytes 1572872 | tf_op jit(solution)/shard_map/ppermute | solution.py:649
  115.5 2.2 %collective-permute-done.17.refs_1_ = bf16[4,2,32,512]{3,2,1,0:T(8,128)(2,1)S(1)} collective-permute-done((bf16[4,2,32,512]{3,2,1,0:T(8,128)(2,1)S(1)}, bf16[4,2,32,512]{3,2,1,0:T(8,128)(2,1)S(1)}, u32[]{:S(2)}, u32[]{:S(2)}) %collective-permute-start.17) | collective-permute-done | bytes 262176 | tf_op jit(solution)/shard_map/ppermute | solution.py:649
  119.3 2.5 %collective-permute-done.18.refs_2_ = bf16[4,2,32,512]{3,2,1,0:T(8,128)(2,1)S(1)} collective-permute-done((bf16[4,2,32,512]{3,2,1,0:T(8,128)(2,1)S(1)}, bf16[4,2,32,512]{3,2,1,0:T(8,128)(2,1)S(1)}, u32[]{:S(2)}, u32[]{:S(2)}) %collective-permute-start.18) | collective-permute-done | bytes 262176 | tf_op jit(solution)/shard_map/ppermute | solution.py:649
  121.8 3.1 %collective-permute-start.14 = (bf16[2,2,128,256]{3,2,1,0:T(8,128)(2,1)S(1)}, bf16[2,2,128,256]{3,2,1,0:T(8,128)(2,1)S(1)}, u32[]{:S(2)}, u32[]{:S(2)}) collective-permute-start(bf16[2,2,128,256]{3,2,1,0:T(8,128)(2,1)S(1)} %get-tuple-element.69), channel_id=1, source_target_pairs={{0,2},{1,3},{2,0},{3,1},{4,6},{5,7},{6,4},{7,5},{8,10},{9,11},{10,... | collective-permute-start | bytes 786440 | tf_op jit(solution)/shard_map/ppermute | solution.py:649
  125.5 18.0 %collective-permute-done.14.refs_8_ = bf16[2,2,128,256]{3,2,1,0:T(8,128)(2,1)S(1)} collective-permute-done((bf16[2,2,128,256]{3,2,1,0:T(8,128)(2,1)S(1)}, bf16[2,2,128,256]{3,2,1,0:T(8,128)(2,1)S(1)}, u32[]{:S(2)}, u32[]{:S(2)}) %collective-permute-start.14) | collective-permute-done | bytes 262176 | tf_op jit(solution)/shard_map/ppermute | solution.py:649
  143.6 6.8 %collective-permute-done.15.refs_9_ = bf16[2,2,128,256]{3,2,1,0:T(8,128)(2,1)S(1)} collective-permute-done((bf16[2,2,128,256]{3,2,1,0:T(8,128)(2,1)S(1)}, bf16[2,2,128,256]{3,2,1,0:T(8,128)(2,1)S(1)}, u32[]{:S(2)}, u32[]{:S(2)}) %collective-permute-start.15) | collective-permute-done | bytes 262176 | tf_op jit(solution)/shard_map/ppermute | solution.py:649
  150.8 3.7 %shard_map.109 = (bf16[512,1536]{1,0:T(8,128)(2,1)}, f32[512,1536]{1,0:T(8,128)S(1)}) custom-call(bf16[512,512]{1,0:T(8,128)(2,1)S(1)} %get-tuple-element.56.refs_0_, bf16[512,256]{1,0:T(8,128)(2,1)S(1)} %get-tuple-element.57.refs_1_, bf16[512,512]{1,0:T(8,128)(2,1)S(1)} %get-tuple-element.58.refs_2_, bf16[512,256]{1,0:T(8,128)(2,1)S(1)} %get-tuple-element.59.refs_3_, ...), custom_call_target="tpu_custom_call" | custom-call | flops 2415919104 | bytes 11534336 | tf_op jit(solution)/shard_map/pallas_call | solution.py:547
  155.4 6.6 %token_grads.1 = bf16[512,1536]{1,0:T(8,128)(2,1)} custom-call(s32[2]{0:T(128)S(1)} %copy-done.4, s32[4,4]{1,0:T(4,128)S(1)} %copy-done.6, s32[4,2,4]{2,1,0:T(2,128)S(1)} %bitcast.20, f32[512,512]{1,0:T(8,128)S(1)} %get-tuple-element.61.refs_0_, f32[512,256]{1,0:T(8,128)S(1)} %get-tuple-element.62.refs_1_, f32[512,512]{1,0:T(8,128)S(1)} %get-tuple-element.63.refs_2_, ...), custom_call_target="tpu_custom_call" | custom-call | flops 2415919104 | bytes 16777216 | tf_op jit(solution)/shard_map/token_grads/pallas_call | solution.py:627
  (68 shorter events, 24.1 us)
Async XLA Ops:
  10.5 9.0 %collective-permute-start.2 = (bf16[32,1536]{1,0:T(8,128)(2,1)}, bf16[32,1536]{1,0:T(8,128)(2,1)S(1)}, u32[]{:S(2)}, u32[]{:S(2)}) collective-permute-start(bf16[32,1536]{1,0:T(8,128)(2,1)} %get-tuple-element.50), channel_id=1, source_target_pairs={{0,96},{4,100},{8,104},{12,108},{16,112},{20,116},{24,120},{28,124... | collective-permute-start | bytes 294920 | tf_op jit(solution)/shard_map/ppermute | solution.py:649
  15.1 5.3 %collective-permute-start.1 = (bf16[32,1536]{1,0:T(8,128)(2,1)}, bf16[32,1536]{1,0:T(8,128)(2,1)S(1)}, u32[]{:S(2)}, u32[]{:S(2)}) collective-permute-start(bf16[32,1536]{1,0:T(8,128)(2,1)} %get-tuple-element.50), channel_id=1, source_target_pairs={{0,64},{4,68},{8,72},{12,76},{16,80},{20,84},{24,88},{28,92},{32,9... | collective-permute-start | bytes 294920 | tf_op jit(solution)/shard_map/ppermute | solution.py:649
  15.1 8.0 %collective-permute-start = (bf16[32,1536]{1,0:T(8,128)(2,1)}, bf16[32,1536]{1,0:T(8,128)(2,1)S(1)}, u32[]{:S(2)}, u32[]{:S(2)}) collective-permute-start(bf16[32,1536]{1,0:T(8,128)(2,1)} %get-tuple-element.50), channel_id=1, source_target_pairs={{0,32},{4,36},{8,40},{12,44},{16,48},{20,52},{24,56},{28,60},{32,6... | collective-permute-start | bytes 294920 | tf_op jit(solution)/shard_map/ppermute | solution.py:649
  24.0 11.0 %collective-permute-start.5 = (bf16[4,32,1536]{2,1,0:T(8,128)(2,1)S(1)}, bf16[4,32,1536]{2,1,0:T(8,128)(2,1)S(1)}, u32[]{:S(2)}, u32[]{:S(2)}) collective-permute-start(bf16[4,32,1536]{2,1,0:T(8,128)(2,1)S(1)} %pad_maximum_fusion.held_0), channel_id=1, source_target_pairs={{0,24},{4,28},{8,0},{12,4},{16,8},{20,12},{24,16},{28,20},{32,56},... | collective-permute-start | bytes 1179656 | tf_op jit(solution)/shard_map/ppermute | solution.py:649
  26.6 30.0 %collective-permute-start.7 = (bf16[2,2,128,768]{3,2,1,0:T(8,128)(2,1)}, bf16[2,2,128,768]{3,2,1,0:T(8,128)(2,1)S(1)}, u32[]{:S(2)}, u32[]{:S(2)}) collective-permute-start(bf16[2,2,128,768]{3,2,1,0:T(8,128)(2,1)} %get-tuple-element.53), channel_id=1, source_target_pairs={{0,1},{1,2},{2,3},{3,0},{4,5},{5,6},{6,7},{7,4},{8,9},{9,10},{10,1... | collective-permute-start | bytes 2359304 | tf_op jit(solution)/shard_map/ppermute | solution.py:649
  27.9 10.9 %collective-permute-start.4 = (bf16[4,32,1536]{2,1,0:T(8,128)(2,1)S(1)}, bf16[4,32,1536]{2,1,0:T(8,128)(2,1)S(1)}, u32[]{:S(2)}, u32[]{:S(2)}) collective-permute-start(bf16[4,32,1536]{2,1,0:T(8,128)(2,1)S(1)} %pad_maximum_fusion.held_0), channel_id=1, source_target_pairs={{0,16},{4,20},{8,24},{12,28},{16,0},{20,4},{24,8},{28,12},{32,48},... | collective-permute-start | bytes 1179656 | tf_op jit(solution)/shard_map/ppermute | solution.py:649
  28.4 20.4 %collective-permute-start.3 = (bf16[4,32,1536]{2,1,0:T(8,128)(2,1)S(1)}, bf16[4,32,1536]{2,1,0:T(8,128)(2,1)S(1)}, u32[]{:S(2)}, u32[]{:S(2)}) collective-permute-start(bf16[4,32,1536]{2,1,0:T(8,128)(2,1)S(1)} %pad_maximum_fusion.held_0), channel_id=1, source_target_pairs={{0,8},{4,12},{8,16},{12,20},{16,24},{20,28},{24,0},{28,4},{32,40},... | collective-permute-start | bytes 1179656 | tf_op jit(solution)/shard_map/ppermute | solution.py:649
  29.0 35.1 %collective-permute-start.8 = (bf16[2,2,128,768]{3,2,1,0:T(8,128)(2,1)}, bf16[2,2,128,768]{3,2,1,0:T(8,128)(2,1)S(1)}, u32[]{:S(2)}, u32[]{:S(2)}) collective-permute-start(bf16[2,2,128,768]{3,2,1,0:T(8,128)(2,1)} %get-tuple-element.54), channel_id=1, source_target_pairs={{0,2},{1,3},{2,0},{3,1},{4,6},{5,7},{6,4},{7,5},{8,10},{9,11},{10,... | collective-permute-start | bytes 2359304 | tf_op jit(solution)/shard_map/ppermute | solution.py:649
  35.1 29.1 %collective-permute-start.9 = (bf16[2,2,128,768]{3,2,1,0:T(8,128)(2,1)}, bf16[2,2,128,768]{3,2,1,0:T(8,128)(2,1)S(1)}, u32[]{:S(2)}, u32[]{:S(2)}) collective-permute-start(bf16[2,2,128,768]{3,2,1,0:T(8,128)(2,1)} %get-tuple-element.55), channel_id=1, source_target_pairs={{0,3},{1,0},{2,1},{3,2},{4,7},{5,4},{6,5},{7,6},{8,11},{9,8},{10,9... | collective-permute-start | bytes 2359304 | tf_op jit(solution)/shard_map/ppermute | solution.py:649
  49.9 14.2 %collective-permute-start.6 = (bf16[4,32,1536]{2,1,0:T(8,128)(2,1)S(1)}, bf16[4,32,1536]{2,1,0:T(8,128)(2,1)S(1)}, u32[]{:S(2)}, u32[]{:S(2)}) collective-permute-start(bf16[4,32,1536]{2,1,0:T(8,128)(2,1)S(1)} %get-tuple-element.52), channel_id=1, source_target_pairs={{0,4},{4,0},{8,12},{12,8},{16,20},{20,16},{24,28},{28,24},{32,36},... | collective-permute-start | bytes 1179656 | tf_op jit(solution)/shard_map/ppermute | solution.py:649
  85.6 22.4 %collective-permute-start.16 = (bf16[2,128,512]{2,1,0:T(8,128)(2,1)S(1)}, bf16[2,128,512]{2,1,0:T(8,128)(2,1)S(1)}, u32[]{:S(2)}, u32[]{:S(2)}) collective-permute-start(bf16[2,128,512]{2,1,0:T(8,128)(2,1)S(1)} %get-tuple-element.72), channel_id=1, source_target_pairs={{0,4},{4,0},{8,12},{12,8},{16,20},{20,16},{24,28},{28,24},{32,36},... | collective-permute-start | bytes 786440 | tf_op jit(solution)/shard_map/ppermute | solution.py:649
  101.4 8.4 %collective-permute-start.21 = (bf16[4,2,32,256]{3,2,1,0:T(8,128)(2,1)S(1)}, bf16[4,2,32,256]{3,2,1,0:T(8,128)(2,1)S(1)}, u32[]{:S(2)}, u32[]{:S(2)}) collective-permute-start(bf16[4,2,32,256]{3,2,1,0:T(8,128)(2,1)S(1)} %get-tuple-element.80), channel_id=1, source_target_pairs={{0,8},{4,12},{8,16},{12,20},{16,24},{20,28},{24,0},{28,4},{32,40},... | collective-permute-start | bytes 393224 | tf_op jit(solution)/shard_map/ppermute | solution.py:649
  103.2 7.9 %collective-permute-start.22 = (bf16[4,2,32,256]{3,2,1,0:T(8,128)(2,1)S(1)}, bf16[4,2,32,256]{3,2,1,0:T(8,128)(2,1)S(1)}, u32[]{:S(2)}, u32[]{:S(2)}) collective-permute-start(bf16[4,2,32,256]{3,2,1,0:T(8,128)(2,1)S(1)} %get-tuple-element.81), channel_id=1, source_target_pairs={{0,16},{4,20},{8,24},{12,28},{16,0},{20,4},{24,8},{28,12},{32,48},... | collective-permute-start | bytes 393224 | tf_op jit(solution)/shard_map/ppermute | solution.py:649
  104.9 7.4 %collective-permute-start.23 = (bf16[4,2,32,256]{3,2,1,0:T(8,128)(2,1)S(1)}, bf16[4,2,32,256]{3,2,1,0:T(8,128)(2,1)S(1)}, u32[]{:S(2)}, u32[]{:S(2)}) collective-permute-start(bf16[4,2,32,256]{3,2,1,0:T(8,128)(2,1)S(1)} %get-tuple-element.82), channel_id=1, source_target_pairs={{0,24},{4,28},{8,0},{12,4},{16,8},{20,12},{24,16},{28,20},{32,56},... | collective-permute-start | bytes 393224 | tf_op jit(solution)/shard_map/ppermute | solution.py:649
  105.7 7.9 %collective-permute-start.13 = (bf16[2,2,128,256]{3,2,1,0:T(8,128)(2,1)S(1)}, bf16[2,2,128,256]{3,2,1,0:T(8,128)(2,1)S(1)}, u32[]{:S(2)}, u32[]{:S(2)}) collective-permute-start(bf16[2,2,128,256]{3,2,1,0:T(8,128)(2,1)S(1)} %get-tuple-element.68), channel_id=1, source_target_pairs={{0,3},{1,0},{2,1},{3,2},{4,7},{5,4},{6,5},{7,6},{8,11},{9,8},{10,9... | collective-permute-start | bytes 786440 | tf_op jit(solution)/shard_map/ppermute | solution.py:649
  109.0 8.7 %collective-permute-start.17 = (bf16[4,2,32,512]{3,2,1,0:T(8,128)(2,1)S(1)}, bf16[4,2,32,512]{3,2,1,0:T(8,128)(2,1)S(1)}, u32[]{:S(2)}, u32[]{:S(2)}) collective-permute-start(bf16[4,2,32,512]{3,2,1,0:T(8,128)(2,1)S(1)} %get-tuple-element.74), channel_id=1, source_target_pairs={{0,8},{4,12},{8,16},{12,20},{16,24},{20,28},{24,0},{28,4},{32,40},... | collective-permute-start | bytes 786440 | tf_op jit(solution)/shard_map/ppermute | solution.py:649
  109.8 12.0 %collective-permute-start.18 = (bf16[4,2,32,512]{3,2,1,0:T(8,128)(2,1)S(1)}, bf16[4,2,32,512]{3,2,1,0:T(8,128)(2,1)S(1)}, u32[]{:S(2)}, u32[]{:S(2)}) collective-permute-start(bf16[4,2,32,512]{3,2,1,0:T(8,128)(2,1)S(1)} %get-tuple-element.75), channel_id=1, source_target_pairs={{0,16},{4,20},{8,24},{12,28},{16,0},{20,4},{24,8},{28,12},{32,48},... | collective-permute-start | bytes 786440 | tf_op jit(solution)/shard_map/ppermute | solution.py:649
  111.1 13.7 %collective-permute-start.19 = (bf16[4,2,32,512]{3,2,1,0:T(8,128)(2,1)S(1)}, bf16[4,2,32,512]{3,2,1,0:T(8,128)(2,1)S(1)}, u32[]{:S(2)}, u32[]{:S(2)}) collective-permute-start(bf16[4,2,32,512]{3,2,1,0:T(8,128)(2,1)S(1)} %get-tuple-element.76), channel_id=1, source_target_pairs={{0,24},{4,28},{8,0},{12,4},{16,8},{20,12},{24,16},{28,20},{32,56},... | collective-permute-start | bytes 786440 | tf_op jit(solution)/shard_map/ppermute | solution.py:649
  112.3 38.2 %collective-permute-start.10 = (bf16[2,2,128,512]{3,2,1,0:T(8,128)(2,1)S(1)}, bf16[2,2,128,512]{3,2,1,0:T(8,128)(2,1)S(1)}, u32[]{:S(2)}, u32[]{:S(2)}) collective-permute-start(bf16[2,2,128,512]{3,2,1,0:T(8,128)(2,1)S(1)} %get-tuple-element.65), channel_id=1, source_target_pairs={{0,3},{1,0},{2,1},{3,2},{4,7},{5,4},{6,5},{7,6},{8,11},{9,8},{10,9... | collective-permute-start | bytes 1572872 | tf_op jit(solution)/shard_map/ppermute | solution.py:649
  113.6 40.9 %collective-permute-start.11 = (bf16[2,2,128,512]{3,2,1,0:T(8,128)(2,1)S(1)}, bf16[2,2,128,512]{3,2,1,0:T(8,128)(2,1)S(1)}, u32[]{:S(2)}, u32[]{:S(2)}) collective-permute-start(bf16[2,2,128,512]{3,2,1,0:T(8,128)(2,1)S(1)} %get-tuple-element.66), channel_id=1, source_target_pairs={{0,2},{1,3},{2,0},{3,1},{4,6},{5,7},{6,4},{7,5},{8,10},{9,11},{10,... | collective-permute-start | bytes 1572872 | tf_op jit(solution)/shard_map/ppermute | solution.py:649
  117.7 36.8 %collective-permute-start.12 = (bf16[2,2,128,512]{3,2,1,0:T(8,128)(2,1)S(1)}, bf16[2,2,128,512]{3,2,1,0:T(8,128)(2,1)S(1)}, u32[]{:S(2)}, u32[]{:S(2)}) collective-permute-start(bf16[2,2,128,512]{3,2,1,0:T(8,128)(2,1)S(1)} %get-tuple-element.67), channel_id=1, source_target_pairs={{0,1},{1,2},{2,3},{3,0},{4,5},{5,6},{6,7},{7,4},{8,9},{9,10},{10,1... | collective-permute-start | bytes 1572872 | tf_op jit(solution)/shard_map/ppermute | solution.py:649
  121.8 21.8 %collective-permute-start.14 = (bf16[2,2,128,256]{3,2,1,0:T(8,128)(2,1)S(1)}, bf16[2,2,128,256]{3,2,1,0:T(8,128)(2,1)S(1)}, u32[]{:S(2)}, u32[]{:S(2)}) collective-permute-start(bf16[2,2,128,256]{3,2,1,0:T(8,128)(2,1)S(1)} %get-tuple-element.69), channel_id=1, source_target_pairs={{0,2},{1,3},{2,0},{3,1},{4,6},{5,7},{6,4},{7,5},{8,10},{9,11},{10,... | collective-permute-start | bytes 786440 | tf_op jit(solution)/shard_map/ppermute | solution.py:649
  124.8 25.5 %collective-permute-start.15 = (bf16[2,2,128,256]{3,2,1,0:T(8,128)(2,1)S(1)}, bf16[2,2,128,256]{3,2,1,0:T(8,128)(2,1)S(1)}, u32[]{:S(2)}, u32[]{:S(2)}) collective-permute-start(bf16[2,2,128,256]{3,2,1,0:T(8,128)(2,1)S(1)} %get-tuple-element.70), channel_id=1, source_target_pairs={{0,1},{1,2},{2,3},{3,0},{4,5},{5,6},{6,7},{7,4},{8,9},{9,10},{10,1... | collective-permute-start | bytes 786440 | tf_op jit(solution)/shard_map/ppermute | solution.py:649
  143.6 10.9 %collective-permute-start.24 = (bf16[2,32,768]{2,1,0:T(8,128)(2,1)S(1)}, bf16[2,32,768]{2,1,0:T(8,128)(2,1)S(1)}, u32[]{:S(2)}, u32[]{:S(2)}) collective-permute-start(bf16[2,32,768]{2,1,0:T(8,128)(2,1)S(1)} %get-tuple-element.84), channel_id=1, source_target_pairs={{0,32},{4,36},{8,40},{12,44},{16,48},{20,52},{24,56},{28,60},{32,6... | collective-permute-start | bytes 294920 | tf_op jit(solution)/shard_map/ppermute | solution.py:649
  (16 other events, 301.3 us)

commit v5 on v4

--- a/solution.py
+++ b/solution.py
@@ -77,7 +77,7 @@
 
 def project_keys_kernel(ids, index, tokens, w_key, w_value, low, keys, values, kept, *rest):
     sends, rest = rest[:3], rest[3:]
-    rows, key_w, value_w, normed_low, made, kept_wide, kept_low, in_sem, out_sem, send_sem = rest
+    rows, key_w, value_w, normed_low, made, kept_wide, in_sem, out_sem, send_sem = rest
     camera = ids[0]
     loads = []
     for step, start in enumerate(range(0, ROWS, STRIP)):
@@ -100,11 +100,6 @@
             cols = slice(start, start + 256)
             made[kind, first:last, cols] = dot(normed_low[first:last, :], weight[:, cols]).astype(LOW)
 
-    def product_kept(kind, weight):
-        for start in range(0, INNER, 256):
-            cols = slice(kind * INNER + start, kind * INNER + start + 256)
-            kept[:, cols] = dot(kept_low[...], weight[:, start : start + 256]).astype(LOW)
-
     stores = []
 
     def store(source, target, sem):
@@ -118,7 +113,8 @@
                 at = pl.ds(pl.multiple_of(strip * STRIP, STRIP), STRIP)
                 sem = send_sem.at[kind * SLOTS + 2 * (shift - 1) + slot]
                 store(made.at[kind, at], sends[shift - 1].at[kind, slot], sem)
-        store(made.at[kind], out, out_sem.at[1 + kind])
+        store(made.at[kind, pl.ds(0, ROWS)], out, out_sem.at[1 + kind])
+        kept[:, kind * INNER : (kind + 1) * INNER] = made[kind, ROWS:, :]
 
     half = ROWS // 2
     loads[0].wait()
@@ -128,44 +124,41 @@
         load.wait()
     product(0, key_w, 0, half)
     norm(half, ROWS)
-    store(normed_low, low, out_sem.at[0])
-    product(0, key_w, half, ROWS)
-    kept_low[...] = kept_wide[...].astype(LOW)
-    product_kept(0, key_w)
+    store(normed_low.at[pl.ds(0, ROWS)], low, out_sem.at[0])
+    normed_low[ROWS:, :] = kept_wide[...].astype(LOW)
+    product(0, key_w, half, ROWS + MEM)
     publish(0, keys)
     loads[5].wait()
-    product_kept(1, value_w)
-    product(1, value_w, 0, ROWS)
+    product(1, value_w, 0, ROWS + MEM)
     publish(1, values)
     for copy in stores:
         copy.wait()
 
 
 def project_keys(ids, index, tokens, w_key, w_value):
-    return call(
+    return pl.pallas_call(
         project_keys_kernel,
-        1,
-        2,
-        [IN_HBM] * 3,
-        [IN_PLACE] * 3 + [whole((MEM, 2 * INNER))] + [IN_PLACE] * 3,
-        [array((ROWS, MODEL), LOW), array((ROWS, INNER), LOW), array((ROWS, INNER), LOW)]
+        in_specs=[pl.BlockSpec(memory_space=pltpu.SMEM)] * 2 + [IN_HBM] * 3,
+        out_specs=[IN_HBM] * 3 + [pl.BlockSpec(memory_space=pltpu.VMEM)] + [IN_HBM] * 3,
+        out_shape=[array((ROWS, MODEL), LOW), array((ROWS, INNER), LOW), array((ROWS, INNER), LOW)]
         + [array((MEM, 2 * INNER), LOW)]
         + [array((2, 2, STRIP, INNER), LOW)] * 3,
-        [
+        scratch_shapes=[
             pltpu.VMEM((ROWS, MODEL), LOW),
             pltpu.VMEM((MODEL, INNER), LOW),
             pltpu.VMEM((MODEL, INNER), LOW),
-            pltpu.VMEM((ROWS, MODEL), LOW),
-            pltpu.VMEM((2, ROWS, INNER), LOW),
+            pltpu.VMEM((ROWS + MEM, MODEL), LOW),
+            pltpu.VMEM((2, ROWS + MEM, INNER), LOW),
             pltpu.VMEM((MEM, MODEL), WIDE),
-            pltpu.VMEM((MEM, MODEL), LOW),
             pltpu.SemaphoreType.DMA((6,)),
             pltpu.SemaphoreType.DMA((3,)),
             pltpu.SemaphoreType.DMA((2 * SLOTS,)),
         ],
-        4 * ROWS * MODEL * INNER,
-        12 << 20,
-        vmem=60,
+        compiler_params=pltpu.CompilerParams(vmem_limit_bytes=48 << 20),
+        cost_estimate=pl.CostEstimate(
+            flops=4 * ROWS * MODEL * INNER, bytes_accessed=12 << 20, transcendentals=0
+        ),
+        name="project_keys",
     )(ids, index, tokens, w_key, w_value)
 
 

time: 165 us -> 164 us (level)
  no operation moved by 1% of the time
where the time goes in v5:
time: 164 us; the launch traced here: 162 us
  waiting for transfers between devices  62.3 us (38%)
  Pallas kernels  59.8 us (36%)
  starting transfers between devices  38 us (23%)
    ppermute x27, waiting for transfers between devices, send(): return lax.ppermute(value, axis, pairs)  62.3 us
    ppermute x27, starting transfers between devices, send(): return lax.ppermute(value, axis, pairs)  38 us
    pallas_call x2, Pallas kernels, attention(): call(attention_kernel, pairs, 3, [taken(ROWS)] * 4 + [mem_k] * 2 + [mem_v...  32.4 us
    pallas_call x1, Pallas kernels, project_keys(): pl.pallas_call(project_keys_kernel, in_specs=[pl.BlockSpec(memory_space=p...  10.2 us
    pallas_call x1, Pallas kernels, token_grads(): pl.pallas_call(token_grads_kernel, in_specs=[pl.BlockSpec(memory_space=pl...  6.58 us
    pallas_call x1, Pallas kernels, project_queries(): call(project_queries_kernel, INNER // width, 0, [whole((ROWS, MODEL)), wh...  4.01 us
    pallas_call x1, Pallas kernels, outward(): call(outward_kernel, MODEL // width, 0, parts + parts + [pl.BlockSpec((IN...  3.69 us
  transfers between devices with their start and end apart: 27, of which 15 were waited for; matrix products, arithmetic and copies ran while one was open for 0% of the time, Pallas kernels for 13%

profile of v5, /device:TPU:1, one launch (start us, length us, event | category | flops | bytes accessed | tf_op | source)
XLA Modules:
  0.0 161.9 jit_solution(3487744104971669409)
XLA Ops:
  1.4 10.2 %project_keys.1 = (bf16[512,1536]{1,0:T(8,128)(2,1)S(1)}, bf16[512,768]{1,0:T(8,128)(2,1)S(1)}, bf16[512,768]{1,0:T(8,128)(2,1)S(1)}, bf16[32,1536]{1,0:T(8,128)...) custom-call(s32[2]{0:T(128)S(1)} %pad_add_fusion.ids, ...), custom_call_target="tpu_custom_call" | custom-call | flops 2415919104 | bytes 12582912 | tf_op jit(solution)/shard_map/project_keys/pallas_call | solution.py:139
  11.6 4.6 %collective-permute-start.2 = (bf16[32,1536]{1,0:T(8,128)(2,1)S(1)}, bf16[32,1536]{1,0:T(8,128)(2,1)S(1)}, u32[]{:S(2)}, u32[]{:S(2)}) collective-permute-start(bf16[32,1536]{1,0:T(8,128)(2,1)S(1)} %get-tuple-element.50), channel_id=1, source_target_pairs={{0,96},{4,100},{8,104},{12,108},{16,112},{20,116},{24,120},{28,124... | collective-permute-start | bytes 294920 | tf_op jit(solution)/shard_map/ppermute | solution.py:642
  16.9 3.4 %collective-permute-done.2 = bf16[32,1536]{1,0:T(8,128)(2,1)S(1)} collective-permute-done((bf16[32,1536]{1,0:T(8,128)(2,1)S(1)}, bf16[32,1536]{1,0:T(8,128)(2,1)S(1)}, u32[]{:S(2)}, u32[]{:S(2)}) %collective-permute-start.2) | collective-permute-done | bytes 98336 | tf_op jit(solution)/shard_map/ppermute | solution.py:642
  21.3 2.7 %collective-permute-done = bf16[32,1536]{1,0:T(8,128)(2,1)S(1)} collective-permute-done((bf16[32,1536]{1,0:T(8,128)(2,1)S(1)}, bf16[32,1536]{1,0:T(8,128)(2,1)S(1)}, u32[]{:S(2)}, u32[]{:S(2)}) %collective-permute-start) | collective-permute-done | bytes 98336 | tf_op jit(solution)/shard_map/ppermute | solution.py:642
  24.0 2.5 %collective-permute-start.5 = (bf16[4,32,1536]{2,1,0:T(8,128)(2,1)S(1)}, bf16[4,32,1536]{2,1,0:T(8,128)(2,1)S(1)}, u32[]{:S(2)}, u32[]{:S(2)}) collective-permute-start(bf16[4,32,1536]{2,1,0:T(8,128)(2,1)S(1)} %pad_maximum_fusion.held_0), channel_id=1, source_target_pairs={{0,24},{4,28},{8,0},{12,4},{16,8},{20,12},{24,16},{28,20},{32,56},... | collective-permute-start | bytes 1179656 | tf_op jit(solution)/shard_map/ppermute | solution.py:642
  29.0 2.6 %collective-permute-start.8 = (bf16[2,2,128,768]{3,2,1,0:T(8,128)(2,1)S(1)}, bf16[2,2,128,768]{3,2,1,0:T(8,128)(2,1)S(1)}, u32[]{:S(2)}, u32[]{:S(2)}) collective-permute-start(bf16[2,2,128,768]{3,2,1,0:T(8,128)(2,1)S(1)} %get-tuple-element.54), channel_id=1, source_target_pairs={{0,2},{1,3},{2,0},{3,1},{4,6},{5,7},{6,4},{7,5},{8,10},{9,11},{10,... | collective-permute-start | bytes 2359304 | tf_op jit(solution)/shard_map/ppermute | solution.py:642
  31.6 3.4 %collective-permute-done.5.held_3 = bf16[4,32,1536]{2,1,0:T(8,128)(2,1)S(1)} collective-permute-done((bf16[4,32,1536]{2,1,0:T(8,128)(2,1)S(1)}, bf16[4,32,1536]{2,1,0:T(8,128)(2,1)S(1)}, u32[]{:S(2)}, u32[]{:S(2)}) %collective-permute-start.5) | collective-permute-done | bytes 393248 | tf_op jit(solution)/shard_map/ppermute | solution.py:642
  35.1 2.7 %collective-permute-start.9 = (bf16[2,2,128,768]{3,2,1,0:T(8,128)(2,1)S(1)}, bf16[2,2,128,768]{3,2,1,0:T(8,128)(2,1)S(1)}, u32[]{:S(2)}, u32[]{:S(2)}) collective-permute-start(bf16[2,2,128,768]{3,2,1,0:T(8,128)(2,1)S(1)} %get-tuple-element.55), channel_id=1, source_target_pairs={{0,3},{1,0},{2,1},{3,2},{4,7},{5,4},{6,5},{7,6},{8,11},{9,8},{10,9... | collective-permute-start | bytes 2359304 | tf_op jit(solution)/shard_map/ppermute | solution.py:642
  38.8 10.1 %collective-permute-done.3.held_1 = bf16[4,32,1536]{2,1,0:T(8,128)(2,1)S(1)} collective-permute-done((bf16[4,32,1536]{2,1,0:T(8,128)(2,1)S(1)}, bf16[4,32,1536]{2,1,0:T(8,128)(2,1)S(1)}, u32[]{:S(2)}, u32[]{:S(2)}) %collective-permute-start.3) | collective-permute-done | bytes 393248 | tf_op jit(solution)/shard_map/ppermute | solution.py:642
  51.2 4.0 %shard_map.104 = (bf16[512,768]{1,0:T(8,128)(2,1)S(1)}, bf16[512,768]{1,0:T(8,128)(2,1)S(1)}) custom-call(bf16[512,1536]{1,0:T(8,128)(2,1)S(1)} %get-tuple-element.45.low, bf16[512,1536]{1,0:T(8,128)(2,1)S(1)} %bitcast.22, bf16[1536,768]{1,0:T(8,128)(2,1)S(1)} %copy-done.7, bf16[768,1536]{1,0:T(8,128)(2,1)S(1)} %copy-done.8), custom_call_target="tpu_custom_call" | custom-call | flops 2415919104 | bytes 10485760 | tf_op jit(solution)/shard_map/pallas_call | solution.py:174
  55.2 8.7 %collective-permute-done.8.rest_5_ = bf16[2,2,128,768]{3,2,1,0:T(8,128)(2,1)S(1)} collective-permute-done((bf16[2,2,128,768]{3,2,1,0:T(8,128)(2,1)S(1)}, bf16[2,2,128,768]{3,2,1,0:T(8,128)(2,1)S(1)}, u32[]{:S(2)}, u32[]{:S(2)}) %collective-permute-start.8) | collective-permute-done | bytes 786464 | tf_op jit(solution)/shard_map/ppermute | solution.py:642
  64.0 21.4 %shard_map.106 = (bf16[512,512]{1,0:T(8,128)(2,1)S(1)}, bf16[512,512]{1,0:T(8,128)(2,1)S(1)}, f32[512,512]{1,0:T(8,128)S(1)}, f32[512,512]{1,0:T(8,128)S(1)}, f3...) custom-call(s32[2]{0:T(128)S(1)} %pad_add_fusion.ids, ...), custom_call_target="tpu_custom_call" | custom-call | flops 14495514624 | bytes 12582912 | tf_op jit(solution)/shard_map/pallas_call | solution.py:439
  85.4 2.5 %collective-permute-start.16 = (bf16[2,128,512]{2,1,0:T(8,128)(2,1)S(1)}, bf16[2,128,512]{2,1,0:T(8,128)(2,1)S(1)}, u32[]{:S(2)}, u32[]{:S(2)}) collective-permute-start(bf16[2,128,512]{2,1,0:T(8,128)(2,1)S(1)} %get-tuple-element.72), channel_id=1, source_target_pairs={{0,4},{4,0},{8,12},{12,8},{16,20},{20,16},{24,28},{28,24},{32,36},... | collective-permute-start | bytes 786440 | tf_op jit(solution)/shard_map/ppermute | solution.py:642
  87.9 11.0 %shard_map.107 = (bf16[512,256]{1,0:T(8,128)(2,1)S(1)}, bf16[512,256]{1,0:T(8,128)(2,1)S(1)}, f32[512,256]{1,0:T(8,128)S(1)}, f32[512,256]{1,0:T(8,128)S(1)}, f3...) custom-call(s32[2]{0:T(128)S(1)} %pad_add_fusion.ids, ...), custom_call_target="tpu_custom_call" | custom-call | flops 7247757312 | bytes 6291456 | tf_op jit(solution)/shard_map/pallas_call | solution.py:439
  101.1 1.8 %collective-permute-start.21 = (bf16[4,2,32,256]{3,2,1,0:T(8,128)(2,1)S(1)}, bf16[4,2,32,256]{3,2,1,0:T(8,128)(2,1)S(1)}, u32[]{:S(2)}, u32[]{:S(2)}) collective-permute-start(bf16[4,2,32,256]{3,2,1,0:T(8,128)(2,1)S(1)} %get-tuple-element.80), channel_id=1, source_target_pairs={{0,8},{4,12},{8,16},{12,20},{16,24},{20,28},{24,0},{28,4},{32,40},... | collective-permute-start | bytes 393224 | tf_op jit(solution)/shard_map/ppermute | solution.py:642
  105.4 2.3 %collective-permute-start.13 = (bf16[2,2,128,256]{3,2,1,0:T(8,128)(2,1)S(1)}, bf16[2,2,128,256]{3,2,1,0:T(8,128)(2,1)S(1)}, u32[]{:S(2)}, u32[]{:S(2)}) collective-permute-start(bf16[2,2,128,256]{3,2,1,0:T(8,128)(2,1)S(1)} %get-tuple-element.68), channel_id=1, source_target_pairs={{0,3},{1,0},{2,1},{3,2},{4,7},{5,4},{6,5},{7,6},{8,11},{9,8},{10,9... | collective-permute-start | bytes 786440 | tf_op jit(solution)/shard_map/ppermute | solution.py:642
  113.4 1.9 %collective-permute-start.11 = (bf16[2,2,128,512]{3,2,1,0:T(8,128)(2,1)S(1)}, bf16[2,2,128,512]{3,2,1,0:T(8,128)(2,1)S(1)}, u32[]{:S(2)}, u32[]{:S(2)}) collective-permute-start(bf16[2,2,128,512]{3,2,1,0:T(8,128)(2,1)S(1)} %get-tuple-element.66), channel_id=1, source_target_pairs={{0,2},{1,3},{2,0},{3,1},{4,6},{5,7},{6,4},{7,5},{8,10},{9,11},{10,... | collective-permute-start | bytes 1572872 | tf_op jit(solution)/shard_map/ppermute | solution.py:642
  115.2 2.2 %collective-permute-done.17.refs_1_ = bf16[4,2,32,512]{3,2,1,0:T(8,128)(2,1)S(1)} collective-permute-done((bf16[4,2,32,512]{3,2,1,0:T(8,128)(2,1)S(1)}, bf16[4,2,32,512]{3,2,1,0:T(8,128)(2,1)S(1)}, u32[]{:S(2)}, u32[]{:S(2)}) %collective-permute-start.17) | collective-permute-done | bytes 262176 | tf_op jit(solution)/shard_map/ppermute | solution.py:642
  119.0 2.5 %collective-permute-done.18.refs_2_ = bf16[4,2,32,512]{3,2,1,0:T(8,128)(2,1)S(1)} collective-permute-done((bf16[4,2,32,512]{3,2,1,0:T(8,128)(2,1)S(1)}, bf16[4,2,32,512]{3,2,1,0:T(8,128)(2,1)S(1)}, u32[]{:S(2)}, u32[]{:S(2)}) %collective-permute-start.18) | collective-permute-done | bytes 262176 | tf_op jit(solution)/shard_map/ppermute | solution.py:642
  121.5 3.1 %collective-permute-start.14 = (bf16[2,2,128,256]{3,2,1,0:T(8,128)(2,1)S(1)}, bf16[2,2,128,256]{3,2,1,0:T(8,128)(2,1)S(1)}, u32[]{:S(2)}, u32[]{:S(2)}) collective-permute-start(bf16[2,2,128,256]{3,2,1,0:T(8,128)(2,1)S(1)} %get-tuple-element.69), channel_id=1, source_target_pairs={{0,2},{1,3},{2,0},{3,1},{4,6},{5,7},{6,4},{7,5},{8,10},{9,11},{10,... | collective-permute-start | bytes 786440 | tf_op jit(solution)/shard_map/ppermute | solution.py:642
  125.3 18.0 %collective-permute-done.14.refs_8_ = bf16[2,2,128,256]{3,2,1,0:T(8,128)(2,1)S(1)} collective-permute-done((bf16[2,2,128,256]{3,2,1,0:T(8,128)(2,1)S(1)}, bf16[2,2,128,256]{3,2,1,0:T(8,128)(2,1)S(1)}, u32[]{:S(2)}, u32[]{:S(2)}) %collective-permute-start.14) | collective-permute-done | bytes 262176 | tf_op jit(solution)/shard_map/ppermute | solution.py:642
  143.3 6.8 %collective-permute-done.15.refs_9_ = bf16[2,2,128,256]{3,2,1,0:T(8,128)(2,1)S(1)} collective-permute-done((bf16[2,2,128,256]{3,2,1,0:T(8,128)(2,1)S(1)}, bf16[2,2,128,256]{3,2,1,0:T(8,128)(2,1)S(1)}, u32[]{:S(2)}, u32[]{:S(2)}) %collective-permute-start.15) | collective-permute-done | bytes 262176 | tf_op jit(solution)/shard_map/ppermute | solution.py:642
  150.5 3.7 %shard_map.108 = (bf16[512,1536]{1,0:T(8,128)(2,1)}, f32[512,1536]{1,0:T(8,128)S(1)}) custom-call(bf16[512,512]{1,0:T(8,128)(2,1)S(1)} %get-tuple-element.56.refs_0_, bf16[512,256]{1,0:T(8,128)(2,1)S(1)} %get-tuple-element.57.refs_1_, bf16[512,512]{1,0:T(8,128)(2,1)S(1)} %get-tuple-element.58.refs_2_, bf16[512,256]{1,0:T(8,128)(2,1)S(1)} %get-tuple-element.59.refs_3_, ...), custom_call_target="tpu_custom_call" | custom-call | flops 2415919104 | bytes 11534336 | tf_op jit(solution)/shard_map/pallas_call | solution.py:540
  155.1 6.6 %token_grads.1 = bf16[512,1536]{1,0:T(8,128)(2,1)} custom-call(s32[2]{0:T(128)S(1)} %pad_add_fusion.ids, s32[4,4]{1,0:T(4,128)S(1)} %copy-done.6, s32[4,2,4]{2,1,0:T(2,128)S(1)} %bitcast.21, f32[512,512]{1,0:T(8,128)S(1)} %get-tuple-element.61.refs_0_, f32[512,256]{1,0:T(8,128)S(1)} %get-tuple-element.62.refs_1_, f32[512,512]{1,0:T(8,128)S(1)} %get-tuple-element.63.refs_2_, ...), custom_call_target="tpu_custom_call" | custom-call | flops 2415919104 | bytes 16777216 | tf_op jit(solution)/shard_map/token_grads/pallas_call | solution.py:620
  (62 shorter events, 22.0 us)
Async XLA Ops:
  11.6 8.7 %collective-permute-start.2 = (bf16[32,1536]{1,0:T(8,128)(2,1)S(1)}, bf16[32,1536]{1,0:T(8,128)(2,1)S(1)}, u32[]{:S(2)}, u32[]{:S(2)}) collective-permute-start(bf16[32,1536]{1,0:T(8,128)(2,1)S(1)} %get-tuple-element.50), channel_id=1, source_target_pairs={{0,96},{4,100},{8,104},{12,108},{16,112},{20,116},{24,120},{28,124... | collective-permute-start | bytes 294920 | tf_op jit(solution)/shard_map/ppermute | solution.py:642
  16.2 5.1 %collective-permute-start.1 = (bf16[32,1536]{1,0:T(8,128)(2,1)S(1)}, bf16[32,1536]{1,0:T(8,128)(2,1)S(1)}, u32[]{:S(2)}, u32[]{:S(2)}) collective-permute-start(bf16[32,1536]{1,0:T(8,128)(2,1)S(1)} %get-tuple-element.50), channel_id=1, source_target_pairs={{0,64},{4,68},{8,72},{12,76},{16,80},{20,84},{24,88},{28,92},{32,9... | collective-permute-start | bytes 294920 | tf_op jit(solution)/shard_map/ppermute | solution.py:642
  16.2 7.7 %collective-permute-start = (bf16[32,1536]{1,0:T(8,128)(2,1)S(1)}, bf16[32,1536]{1,0:T(8,128)(2,1)S(1)}, u32[]{:S(2)}, u32[]{:S(2)}) collective-permute-start(bf16[32,1536]{1,0:T(8,128)(2,1)S(1)} %get-tuple-element.50), channel_id=1, source_target_pairs={{0,32},{4,36},{8,40},{12,44},{16,48},{20,52},{24,56},{28,60},{32,6... | collective-permute-start | bytes 294920 | tf_op jit(solution)/shard_map/ppermute | solution.py:642
  24.0 11.0 %collective-permute-start.5 = (bf16[4,32,1536]{2,1,0:T(8,128)(2,1)S(1)}, bf16[4,32,1536]{2,1,0:T(8,128)(2,1)S(1)}, u32[]{:S(2)}, u32[]{:S(2)}) collective-permute-start(bf16[4,32,1536]{2,1,0:T(8,128)(2,1)S(1)} %pad_maximum_fusion.held_0), channel_id=1, source_target_pairs={{0,24},{4,28},{8,0},{12,4},{16,8},{20,12},{24,16},{28,20},{32,56},... | collective-permute-start | bytes 1179656 | tf_op jit(solution)/shard_map/ppermute | solution.py:642
  26.6 28.6 %collective-permute-start.7 = (bf16[2,2,128,768]{3,2,1,0:T(8,128)(2,1)S(1)}, bf16[2,2,128,768]{3,2,1,0:T(8,128)(2,1)S(1)}, u32[]{:S(2)}, u32[]{:S(2)}) collective-permute-start(bf16[2,2,128,768]{3,2,1,0:T(8,128)(2,1)S(1)} %get-tuple-element.53), channel_id=1, source_target_pairs={{0,1},{1,2},{2,3},{3,0},{4,5},{5,6},{6,7},{7,4},{8,9},{9,10},{10,1... | collective-permute-start | bytes 2359304 | tf_op jit(solution)/shard_map/ppermute | solution.py:642
  27.9 10.9 %collective-permute-start.4 = (bf16[4,32,1536]{2,1,0:T(8,128)(2,1)S(1)}, bf16[4,32,1536]{2,1,0:T(8,128)(2,1)S(1)}, u32[]{:S(2)}, u32[]{:S(2)}) collective-permute-start(bf16[4,32,1536]{2,1,0:T(8,128)(2,1)S(1)} %pad_maximum_fusion.held_0), channel_id=1, source_target_pairs={{0,16},{4,20},{8,24},{12,28},{16,0},{20,4},{24,8},{28,12},{32,48},... | collective-permute-start | bytes 1179656 | tf_op jit(solution)/shard_map/ppermute | solution.py:642
  28.4 20.4 %collective-permute-start.3 = (bf16[4,32,1536]{2,1,0:T(8,128)(2,1)S(1)}, bf16[4,32,1536]{2,1,0:T(8,128)(2,1)S(1)}, u32[]{:S(2)}, u32[]{:S(2)}) collective-permute-start(bf16[4,32,1536]{2,1,0:T(8,128)(2,1)S(1)} %pad_maximum_fusion.held_0), channel_id=1, source_target_pairs={{0,8},{4,12},{8,16},{12,20},{16,24},{20,28},{24,0},{28,4},{32,40},... | collective-permute-start | bytes 1179656 | tf_op jit(solution)/shard_map/ppermute | solution.py:642
  29.0 34.9 %collective-permute-start.8 = (bf16[2,2,128,768]{3,2,1,0:T(8,128)(2,1)S(1)}, bf16[2,2,128,768]{3,2,1,0:T(8,128)(2,1)S(1)}, u32[]{:S(2)}, u32[]{:S(2)}) collective-permute-start(bf16[2,2,128,768]{3,2,1,0:T(8,128)(2,1)S(1)} %get-tuple-element.54), channel_id=1, source_target_pairs={{0,2},{1,3},{2,0},{3,1},{4,6},{5,7},{6,4},{7,5},{8,10},{9,11},{10,... | collective-permute-start | bytes 2359304 | tf_op jit(solution)/shard_map/ppermute | solution.py:642
  35.1 28.9 %collective-permute-start.9 = (bf16[2,2,128,768]{3,2,1,0:T(8,128)(2,1)S(1)}, bf16[2,2,128,768]{3,2,1,0:T(8,128)(2,1)S(1)}, u32[]{:S(2)}, u32[]{:S(2)}) collective-permute-start(bf16[2,2,128,768]{3,2,1,0:T(8,128)(2,1)S(1)} %get-tuple-element.55), channel_id=1, source_target_pairs={{0,3},{1,0},{2,1},{3,2},{4,7},{5,4},{6,5},{7,6},{8,11},{9,8},{10,9... | collective-permute-start | bytes 2359304 | tf_op jit(solution)/shard_map/ppermute | solution.py:642
  49.9 14.0 %collective-permute-start.6 = (bf16[4,32,1536]{2,1,0:T(8,128)(2,1)S(1)}, bf16[4,32,1536]{2,1,0:T(8,128)(2,1)S(1)}, u32[]{:S(2)}, u32[]{:S(2)}) collective-permute-start(bf16[4,32,1536]{2,1,0:T(8,128)(2,1)S(1)} %get-tuple-element.52), channel_id=1, source_target_pairs={{0,4},{4,0},{8,12},{12,8},{16,20},{20,16},{24,28},{28,24},{32,36},... | collective-permute-start | bytes 1179656 | tf_op jit(solution)/shard_map/ppermute | solution.py:642
  85.4 22.4 %collective-permute-start.16 = (bf16[2,128,512]{2,1,0:T(8,128)(2,1)S(1)}, bf16[2,128,512]{2,1,0:T(8,128)(2,1)S(1)}, u32[]{:S(2)}, u32[]{:S(2)}) collective-permute-start(bf16[2,128,512]{2,1,0:T(8,128)(2,1)S(1)} %get-tuple-element.72), channel_id=1, source_target_pairs={{0,4},{4,0},{8,12},{12,8},{16,20},{20,16},{24,28},{28,24},{32,36},... | collective-permute-start | bytes 786440 | tf_op jit(solution)/shard_map/ppermute | solution.py:642
  101.1 8.4 %collective-permute-start.21 = (bf16[4,2,32,256]{3,2,1,0:T(8,128)(2,1)S(1)}, bf16[4,2,32,256]{3,2,1,0:T(8,128)(2,1)S(1)}, u32[]{:S(2)}, u32[]{:S(2)}) collective-permute-start(bf16[4,2,32,256]{3,2,1,0:T(8,128)(2,1)S(1)} %get-tuple-element.80), channel_id=1, source_target_pairs={{0,8},{4,12},{8,16},{12,20},{16,24},{20,28},{24,0},{28,4},{32,40},... | collective-permute-start | bytes 393224 | tf_op jit(solution)/shard_map/ppermute | solution.py:642
  103.0 7.9 %collective-permute-start.22 = (bf16[4,2,32,256]{3,2,1,0:T(8,128)(2,1)S(1)}, bf16[4,2,32,256]{3,2,1,0:T(8,128)(2,1)S(1)}, u32[]{:S(2)}, u32[]{:S(2)}) collective-permute-start(bf16[4,2,32,256]{3,2,1,0:T(8,128)(2,1)S(1)} %get-tuple-element.81), channel_id=1, source_target_pairs={{0,16},{4,20},{8,24},{12,28},{16,0},{20,4},{24,8},{28,12},{32,48},... | collective-permute-start | bytes 393224 | tf_op jit(solution)/shard_map/ppermute | solution.py:642
  104.7 7.4 %collective-permute-start.23 = (bf16[4,2,32,256]{3,2,1,0:T(8,128)(2,1)S(1)}, bf16[4,2,32,256]{3,2,1,0:T(8,128)(2,1)S(1)}, u32[]{:S(2)}, u32[]{:S(2)}) collective-permute-start(bf16[4,2,32,256]{3,2,1,0:T(8,128)(2,1)S(1)} %get-tuple-element.82), channel_id=1, source_target_pairs={{0,24},{4,28},{8,0},{12,4},{16,8},{20,12},{24,16},{28,20},{32,56},... | collective-permute-start | bytes 393224 | tf_op jit(solution)/shard_map/ppermute | solution.py:642
  105.4 7.9 %collective-permute-start.13 = (bf16[2,2,128,256]{3,2,1,0:T(8,128)(2,1)S(1)}, bf16[2,2,128,256]{3,2,1,0:T(8,128)(2,1)S(1)}, u32[]{:S(2)}, u32[]{:S(2)}) collective-permute-start(bf16[2,2,128,256]{3,2,1,0:T(8,128)(2,1)S(1)} %get-tuple-element.68), channel_id=1, source_target_pairs={{0,3},{1,0},{2,1},{3,2},{4,7},{5,4},{6,5},{7,6},{8,11},{9,8},{10,9... | collective-permute-start | bytes 786440 | tf_op jit(solution)/shard_map/ppermute | solution.py:642
  108.7 8.7 %collective-permute-start.17 = (bf16[4,2,32,512]{3,2,1,0:T(8,128)(2,1)S(1)}, bf16[4,2,32,512]{3,2,1,0:T(8,128)(2,1)S(1)}, u32[]{:S(2)}, u32[]{:S(2)}) collective-permute-start(bf16[4,2,32,512]{3,2,1,0:T(8,128)(2,1)S(1)} %get-tuple-element.74), channel_id=1, source_target_pairs={{0,8},{4,12},{8,16},{12,20},{16,24},{20,28},{24,0},{28,4},{32,40},... | collective-permute-start | bytes 786440 | tf_op jit(solution)/shard_map/ppermute | solution.py:642
  109.6 12.0 %collective-permute-start.18 = (bf16[4,2,32,512]{3,2,1,0:T(8,128)(2,1)S(1)}, bf16[4,2,32,512]{3,2,1,0:T(8,128)(2,1)S(1)}, u32[]{:S(2)}, u32[]{:S(2)}) collective-permute-start(bf16[4,2,32,512]{3,2,1,0:T(8,128)(2,1)S(1)} %get-tuple-element.75), channel_id=1, source_target_pairs={{0,16},{4,20},{8,24},{12,28},{16,0},{20,4},{24,8},{28,12},{32,48},... | collective-permute-start | bytes 786440 | tf_op jit(solution)/shard_map/ppermute | solution.py:642
  110.9 13.7 %collective-permute-start.19 = (bf16[4,2,32,512]{3,2,1,0:T(8,128)(2,1)S(1)}, bf16[4,2,32,512]{3,2,1,0:T(8,128)(2,1)S(1)}, u32[]{:S(2)}, u32[]{:S(2)}) collective-permute-start(bf16[4,2,32,512]{3,2,1,0:T(8,128)(2,1)S(1)} %get-tuple-element.76), channel_id=1, source_target_pairs={{0,24},{4,28},{8,0},{12,4},{16,8},{20,12},{24,16},{28,20},{32,56},... | collective-permute-start | bytes 786440 | tf_op jit(solution)/shard_map/ppermute | solution.py:642
  112.1 38.2 %collective-permute-start.10 = (bf16[2,2,128,512]{3,2,1,0:T(8,128)(2,1)S(1)}, bf16[2,2,128,512]{3,2,1,0:T(8,128)(2,1)S(1)}, u32[]{:S(2)}, u32[]{:S(2)}) collective-permute-start(bf16[2,2,128,512]{3,2,1,0:T(8,128)(2,1)S(1)} %get-tuple-element.65), channel_id=1, source_target_pairs={{0,3},{1,0},{2,1},{3,2},{4,7},{5,4},{6,5},{7,6},{8,11},{9,8},{10,9... | collective-permute-start | bytes 1572872 | tf_op jit(solution)/shard_map/ppermute | solution.py:642
  113.4 40.8 %collective-permute-start.11 = (bf16[2,2,128,512]{3,2,1,0:T(8,128)(2,1)S(1)}, bf16[2,2,128,512]{3,2,1,0:T(8,128)(2,1)S(1)}, u32[]{:S(2)}, u32[]{:S(2)}) collective-permute-start(bf16[2,2,128,512]{3,2,1,0:T(8,128)(2,1)S(1)} %get-tuple-element.66), channel_id=1, source_target_pairs={{0,2},{1,3},{2,0},{3,1},{4,6},{5,7},{6,4},{7,5},{8,10},{9,11},{10,... | collective-permute-start | bytes 1572872 | tf_op jit(solution)/shard_map/ppermute | solution.py:642
  117.5 36.7 %collective-permute-start.12 = (bf16[2,2,128,512]{3,2,1,0:T(8,128)(2,1)S(1)}, bf16[2,2,128,512]{3,2,1,0:T(8,128)(2,1)S(1)}, u32[]{:S(2)}, u32[]{:S(2)}) collective-permute-start(bf16[2,2,128,512]{3,2,1,0:T(8,128)(2,1)S(1)} %get-tuple-element.67), channel_id=1, source_target_pairs={{0,1},{1,2},{2,3},{3,0},{4,5},{5,6},{6,7},{7,4},{8,9},{9,10},{10,1... | collective-permute-start | bytes 1572872 | tf_op jit(solution)/shard_map/ppermute | solution.py:642
  121.5 21.8 %collective-permute-start.14 = (bf16[2,2,128,256]{3,2,1,0:T(8,128)(2,1)S(1)}, bf16[2,2,128,256]{3,2,1,0:T(8,128)(2,1)S(1)}, u32[]{:S(2)}, u32[]{:S(2)}) collective-permute-start(bf16[2,2,128,256]{3,2,1,0:T(8,128)(2,1)S(1)} %get-tuple-element.69), channel_id=1, source_target_pairs={{0,2},{1,3},{2,0},{3,1},{4,6},{5,7},{6,4},{7,5},{8,10},{9,11},{10,... | collective-permute-start | bytes 786440 | tf_op jit(solution)/shard_map/ppermute | solution.py:642
  124.6 25.5 %collective-permute-start.15 = (bf16[2,2,128,256]{3,2,1,0:T(8,128)(2,1)S(1)}, bf16[2,2,128,256]{3,2,1,0:T(8,128)(2,1)S(1)}, u32[]{:S(2)}, u32[]{:S(2)}) collective-permute-start(bf16[2,2,128,256]{3,2,1,0:T(8,128)(2,1)S(1)} %get-tuple-element.70), channel_id=1, source_target_pairs={{0,1},{1,2},{2,3},{3,0},{4,5},{5,6},{6,7},{7,4},{8,9},{9,10},{10,1... | collective-permute-start | bytes 786440 | tf_op jit(solution)/shard_map/ppermute | solution.py:642
  143.3 10.9 %collective-permute-start.24 = (bf16[2,32,768]{2,1,0:T(8,128)(2,1)S(1)}, bf16[2,32,768]{2,1,0:T(8,128)(2,1)S(1)}, u32[]{:S(2)}, u32[]{:S(2)}) collective-permute-start(bf16[2,32,768]{2,1,0:T(8,128)(2,1)S(1)} %get-tuple-element.84), channel_id=1, source_target_pairs={{0,32},{4,36},{8,40},{12,44},{16,48},{20,52},{24,56},{28,60},{32,6... | collective-permute-start | bytes 294920 | tf_op jit(solution)/shard_map/ppermute | solution.py:642
  (13 other events, 229.8 us)
